TPU v7x, 128 devices: a whole 4x4x4 slice. The times are simulated.
128 devices in a mesh: clu: 8 (over z, y_lo), ang: 16 (over y_hi, x, core).
Axes of the slice: x: 4, y: 4 (y_hi: 2, y_lo: 2; y = y_hi * 2 + y_lo), z: 4, core: 2. Of those that a mesh axis runs over, the one named last changes fastest.
Arguments:
- patterns7: bfloat16 [32768, 2, 64, 128], P(('clu', 'ang')), may hold values from -6 to 6
- polar_up7: bfloat16 [128, 64], replicated, may hold values from -0.25 to 0.25
- azimuth_up7: bfloat16 [128, 256], replicated, may hold values from -0.5 to 0.5
- polar_up6: bfloat16 [256, 128], replicated, may hold values from -0.1875 to 0.1875
- azimuth_up6: bfloat16 [256, 512], replicated, may hold values from -0.375 to 0.375
- polar_first: int32 [512], replicated, may hold values from 0 to 252, as said below
- polar_weights: bfloat16 [512, 4], replicated, may hold values from -1 to 1
- azimuth_first: int32 [1024], replicated, may hold values from 0 to 511, as said below
- azimuth_weights: bfloat16 [1024, 4], replicated, may hold values from -3 to 3
- transfer5: bfloat16 [316, 2, 256, 512], P(None, None, 'ang', 'clu'), may hold values from -1.5 to 1.5
- sources5: int32 [512, 16], replicated, may hold values from -1 to 511, as said below
- offsets5: int32 [512, 16], replicated, may hold values from -1 to 315, as said below
- transfer4: bfloat16 [316, 2, 512, 1024], P(None, None, 'ang', 'clu'), may hold values from -1.5 to 1.5
- sources4: int32 [64, 16], replicated, may hold values from -1 to 63, as said below
- offsets4: int32 [64, 16], replicated, may hold values from -1 to 315, as said below
Outputs:
- translated5: bfloat16 [512, 2, 256, 512], P(None, None, 'ang', 'clu')
- translated4: bfloat16 [64, 2, 512, 1024], P(None, None, 'ang', 'clu')
Inputs may be any that keep to these rules, and one draw needn't show every extreme that they name: The theta stencil of target row r reads source rows polar_first[r] to polar_first[r] + 3, all within floor(r / 2) - 3 to floor(r / 2) + 3. The phi stencil of target column c reads source columns (azimuth_first[c] + k) mod 512, k = 0 to 3, all within floor(c / 2) - 3 to floor(c / 2) + 3 modulo 512. `sources5`: row t lists source clusters of target t: live entries first, then -1; never t itself; at least one live entry. `offsets5`: displacement id of each slot; -1 exactly where sources5 is -1. `sources4`: row t lists source clusters of target t: live entries first, then -1; never t itself; at least one live entry. `offsets4`: displacement id of each slot; -1 exactly where sources4 is -1.
All inputs are finite; a program needn't handle non-finite values.
Results may differ from a plain program's by a relative error of at most 0.015.
Values may be sent and summed in bfloat16 or wider, within the bound.
No kernel may reach another device: no remote copies, remote signals or barrier semaphores. Data moves between devices by JAX's collectives and lax.ppermute only.
A program may use at most 192 MiB of HBM per device.

v0:
```python
import math

import jax
import jax.numpy as jnp
from jax import lax
from jax.sharding import PartitionSpec as P


def extended_2(block, sides, width, periodic):
    for axis, dim in sides:
        count = lax.axis_size(axis)
        forward = [(i, i + 1) for i in range(count - 1)]
        if periodic:
            forward.append((count - 1, 0))
        backward = [(target, source) for source, target in forward]
        low = lax.ppermute(
            lax.slice_in_dim(block, block.shape[dim] - width, None, axis=dim), axis, forward
        )
        high = lax.ppermute(lax.slice_in_dim(block, 0, width, axis=dim), axis, backward)
        block = jnp.concatenate([low, block, high], axis=dim)
    return block


def octant_signs():
    octant = jnp.arange(8, dtype=jnp.int32)
    sign_first = (2 * (octant % 2) - 1).astype(jnp.float32)
    sign_second = (2 * (octant // 2 % 2) - 1).astype(jnp.float32)
    sign_third = (2 * (octant // 4) - 1).astype(jnp.float32)
    return (sign_first, sign_second, sign_third)


def phase_tables(polar_index, azimuth_index, polar_count, azimuth_count):
    polar_angle = (polar_index + 0.5) * (math.pi / polar_count)
    azimuth_angle = azimuth_index * (2.0 * math.pi / azimuth_count)
    direction_x = jnp.sin(polar_angle)[:, None] * jnp.cos(azimuth_angle)[None, :]
    direction_y = jnp.sin(polar_angle)[:, None] * jnp.sin(azimuth_angle)[None, :]
    direction_z = jnp.cos(polar_angle)[:, None] * jnp.ones_like(azimuth_angle)[None, :]
    sign_first, sign_second, sign_third = octant_signs()
    phase_angle = (
        polar_count
        / 8.0
        * (
            sign_first[:, None, None] * direction_x
            + sign_second[:, None, None] * direction_y
            + sign_third[:, None, None] * direction_z
        )
    )
    return (jnp.cos(phase_angle), jnp.sin(phase_angle))


def shift_sum(child_terms, cosine, sine):
    real_part = jnp.sum(child_terms[:, :, 0] * cosine - child_terms[:, :, 1] * sine, axis=1)
    imag_part = jnp.sum(child_terms[:, :, 0] * sine + child_terms[:, :, 1] * cosine, axis=1)
    return jnp.stack([real_part, imag_part], axis=1).astype(jnp.bfloat16)


def stencil_matrix(tap_index, weights, column_count):
    matches = (
        tap_index[:, :, None] == jnp.arange(column_count, dtype=jnp.int32)[None, None, :]
    ).astype(jnp.float32)
    return jnp.sum(weights.astype(jnp.float32)[:, :, None] * matches, axis=1)


def parent_block(children, polar_matrix, azimuth_matrix, cosine, sine):
    parents = children.shape[0] // 8
    grouped = children.reshape(parents, 8, 2, children.shape[2], children.shape[3])
    halfway = jnp.einsum(
        "ut,pkcts->pkcus", polar_matrix, grouped, preferred_element_type=jnp.float32
    ).astype(jnp.bfloat16)
    child_terms = jnp.einsum(
        "pkcus,sv->pkcuv", halfway, azimuth_matrix, preferred_element_type=jnp.float32
    )
    return shift_sum(child_terms, cosine, sine)


def aggregate(children, polar_matrix, azimuth_matrix, cosine, sine, block_parents):
    parent_total = children.shape[0] // 8
    group_size = math.gcd(parent_total, block_parents)
    blocks = children.reshape(
        parent_total // group_size, group_size * 8, 2, children.shape[2], children.shape[3]
    )

    def one_block(block_piece):
        return parent_block(block_piece, polar_matrix, azimuth_matrix, cosine, sine)

    merged = lax.map(one_block, blocks)
    return merged.reshape(parent_total, 2, polar_matrix.shape[0], azimuth_matrix.shape[1])


def translate(patterns, transfer_table, sources, displacements):
    targets = patterns.shape[0]
    flat_patterns = patterns.reshape(targets, 2, -1)
    flat_table = transfer_table.reshape(transfer_table.shape[0], 2, -1)
    samples = flat_patterns.shape[2]
    slots = sources.shape[1]

    def add_slot(slot, totals):
        real_total, imag_total = totals
        source_col = lax.dynamic_index_in_dim(sources, slot, 1, keepdims=False)
        offset_col = lax.dynamic_index_in_dim(displacements, slot, 1, keepdims=False)
        live_slot = (source_col >= 0)[:, None]
        picked = jnp.take(flat_patterns, jnp.maximum(source_col, 0), axis=0)
        factor = jnp.take(flat_table, jnp.maximum(offset_col, 0), axis=0)
        factor_real = jnp.where(live_slot, factor[:, 0].astype(jnp.float32), 0.0)
        factor_imag = jnp.where(live_slot, factor[:, 1].astype(jnp.float32), 0.0)
        picked_real = picked[:, 0].astype(jnp.float32)
        picked_imag = picked[:, 1].astype(jnp.float32)
        real_total = real_total + factor_real * picked_real - factor_imag * picked_imag
        imag_total = imag_total + factor_real * picked_imag + factor_imag * picked_real
        return (real_total, imag_total)

    empty = jnp.zeros((targets, samples), jnp.float32)
    real_total, imag_total = lax.fori_loop(0, slots, add_slot, (empty, empty))
    return jnp.stack([real_total, imag_total], axis=1).astype(jnp.bfloat16).reshape(patterns.shape)


def band_windows(level5, band_count, block_count):
    local_count = level5.shape[0]
    rows_five = level5.shape[2]
    cols_five = level5.shape[3]
    source_rows = rows_five // band_count
    source_cols = cols_five // block_count
    spread = level5.reshape(local_count, 2, band_count, source_rows, block_count, source_cols)
    return spread.transpose(0, 4, 2, 1, 3, 5)


def shards(
    patterns7,
    polar_up7,
    azimuth_up7,
    polar_up6,
    azimuth_up6,
    polar_first,
    polar_weights,
    azimuth_first,
    azimuth_weights,
    transfer5,
    sources5,
    offsets5,
    transfer4,
    sources4,
    offsets4,
):
    rows_six = polar_up7.shape[0]
    cols_six = azimuth_up7.shape[1]
    cosine6, sine6 = phase_tables(
        jnp.arange(rows_six, dtype=jnp.float32),
        jnp.arange(cols_six, dtype=jnp.float32),
        rows_six,
        cols_six,
    )
    level6 = aggregate(patterns7, polar_up7, azimuth_up7, cosine6, sine6, 8)
    rows_five = polar_up6.shape[0]
    cols_five = azimuth_up6.shape[1]
    cosine5, sine5 = phase_tables(
        jnp.arange(rows_five, dtype=jnp.float32),
        jnp.arange(cols_five, dtype=jnp.float32),
        rows_five,
        cols_five,
    )
    level5 = aggregate(level6, polar_up6, azimuth_up6, cosine5, sine5, 8)
    band_count = lax.axis_size("ang")
    block_count = lax.axis_size("clu")
    source_rows = rows_five // band_count
    source_cols = cols_five // block_count
    local_count = level5.shape[0]
    margin = 0
    window_rows = source_rows + 2 * margin
    window_cols = source_cols + 2 * margin
    spread = band_windows(level5, band_count, block_count)
    flat_spread = spread.reshape(local_count, block_count * band_count, 2, window_rows, window_cols)
    arrived = lax.all_to_all(flat_spread, ("clu", "ang"), split_axis=1, concat_axis=0, tiled=True)
    arrived = arrived.reshape(local_count * block_count * band_count, 2, window_rows, window_cols)
    translated5 = translate(arrived, transfer5, sources5, offsets5)
    rows_four = polar_first.shape[0]
    cols_four = azimuth_first.shape[0]
    band_rows = rows_four // band_count
    block_cols = cols_four // block_count
    band_index = lax.axis_index("ang")
    column_block = lax.axis_index("clu")
    four_taps = jnp.arange(4, dtype=jnp.int32)[None, :]
    polar_local = (
        lax.dynamic_slice_in_dim(polar_first, band_index * band_rows, band_rows, 0)
        - band_index * source_rows
        + 3
    )
    polar_local_weights = lax.dynamic_slice_in_dim(
        polar_weights, band_index * band_rows, band_rows, 0
    )
    polar_matrix = stencil_matrix(
        polar_local[:, None] + four_taps, polar_local_weights, source_rows + 6
    ).astype(jnp.bfloat16)
    azimuth_local = (
        lax.dynamic_slice_in_dim(azimuth_first, column_block * block_cols, block_cols, 0)
        - column_block * source_cols
        + 3
    ) % cols_five
    azimuth_local_weights = lax.dynamic_slice_in_dim(
        azimuth_weights, column_block * block_cols, block_cols, 0
    )
    azimuth_matrix = stencil_matrix(
        azimuth_local[:, None] + four_taps, azimuth_local_weights, source_cols + 6
    ).T.astype(jnp.bfloat16)
    extended = extended_2(arrived, (("ang", 2),), 3, False)
    halfway = jnp.einsum(
        "uq,ncqf->ncuf", polar_matrix, extended, preferred_element_type=jnp.float32
    ).astype(jnp.bfloat16)
    widened = extended_2(halfway, (("clu", 3),), 3, True)
    child_terms = jnp.einsum(
        "ncuq,qv->ncuv", widened, azimuth_matrix, preferred_element_type=jnp.float32
    )
    polar_index = (jnp.arange(band_rows, dtype=jnp.int32) + band_index * band_rows).astype(
        jnp.float32
    )
    azimuth_index = (jnp.arange(block_cols, dtype=jnp.int32) + column_block * block_cols).astype(
        jnp.float32
    )
    cosine4, sine4 = phase_tables(polar_index, azimuth_index, rows_four, cols_four)
    parent_count = child_terms.shape[0] // 8
    level4 = shift_sum(
        child_terms.reshape(parent_count, 8, 2, band_rows, block_cols), cosine4, sine4
    )
    translated4 = translate(level4, transfer4, sources4, offsets4)
    return (translated5, translated4)


def solution(mesh):
    in_specs = (
        P(("clu", "ang"), None, None, None),
        P(),
        P(),
        P(),
        P(),
        P(),
        P(),
        P(),
        P(),
        P(None, None, "ang", "clu"),
        P(),
        P(),
        P(None, None, "ang", "clu"),
        P(),
        P(),
    )
    out_specs = (P(None, None, "ang", "clu"), P(None, None, "ang", "clu"))
    return jax.shard_map(shards, mesh=mesh, in_specs=in_specs, out_specs=out_specs, check_vma=False)
```

profile of v0, /device:TPU:7, one launch (start us, length us, event | category | flops | bytes accessed | tf_op | source)
XLA Modules:
  0.0 1710.3 jit_solution(6318439605231223074)
XLA Ops:
  2.8 97.1 %while.51 = (s32[]{:T(128)}, bf16[4,8,2,128,256]{4,3,2,1,0:T(8,128)(2,1)}, bf16[4,64,2,64,128]{4,3,2,1,0:T(8,128)(2,1)}, bf16[128,64]{0,1:T(8,128)(2,1)}, bf16[1...) while((s32[]{:T(128)}, ...), condition=%wide.region_3.4_spmd.clone.clone.clone, body=%wide.region_0.3_spmd.clone.clone.clone.sunk | while | flops 1364197376 | bytes 48650508 | solution.py:86
  249.3 1096.5 %while.49 = (s32[]{:T(128)}, f32[512,1024]{1,0:T(8,128)}, f32[512,1024]{1,0:T(8,128)}, s32[512,16]{0,1:T(8,128)}, s32[512,16]{0,1:T(8,128)}, /*index=5*/bf16[316...) while((s32[]{:T(128)}, f32[512,1024]{1,0:T(8,128)}, ...), condition=%wide.region_7.8_spmd.clone, body=%wide.region_6.7_spmd.clone.sunk | while | flops 10490371 | bytes 35679336 | solution.py:113
  283.9 26.4 %gather_fusion.1 = bf16[512,2,1024]{2,1,0:T(2,128)(2,1)S(1)} fusion(bf16[512,2,1024]{2,1,0:T(2,128)(2,1)} %get-tuple-element.891, s32[1024]{0:T(1024)S(1)} %pad_clamp_fusion.9), kind=kCustom, calls=%fused_computation.1.clone.clone.1 | custom fusion | bytes 4196352 | tf_op jit(solution)/shard_map/while/body/eval_jaxpr/jit(_take)/gather | solution.py:102
  318.1 26.1 %gather_fusion = bf16[512,2,1024]{2,1,0:T(2,128)(2,1)S(1)} fusion(bf16[316,2,1024]{2,1,0:T(2,128)(2,1)} %get-tuple-element.890, s32[1024]{0:T(1024)S(1)} %pad_clamp_fusion.8), kind=kCustom, calls=%fused_computation.clone.clone.1 | custom fusion | bytes 4196352 | tf_op jit(solution)/shard_map/while/body/eval_jaxpr/jit(_take)/gather | solution.py:103
  351.4 26.4 %gather_fusion.1 = bf16[512,2,1024]{2,1,0:T(2,128)(2,1)S(1)} fusion(bf16[512,2,1024]{2,1,0:T(2,128)(2,1)} %get-tuple-element.891, s32[1024]{0:T(1024)S(1)} %pad_clamp_fusion.9), kind=kCustom, calls=%fused_computation.1.clone.clone.1 | custom fusion | bytes 4196352 | tf_op jit(solution)/shard_map/while/body/eval_jaxpr/jit(_take)/gather | solution.py:102
  420.1 26.4 %gather_fusion.1 = bf16[512,2,1024]{2,1,0:T(2,128)(2,1)S(1)} fusion(bf16[512,2,1024]{2,1,0:T(2,128)(2,1)} %get-tuple-element.891, s32[1024]{0:T(1024)S(1)} %pad_clamp_fusion.9), kind=kCustom, calls=%fused_computation.1.clone.clone.1 | custom fusion | bytes 4196352 | tf_op jit(solution)/shard_map/while/body/eval_jaxpr/jit(_take)/gather | solution.py:102
  455.3 26.1 %gather_fusion = bf16[512,2,1024]{2,1,0:T(2,128)(2,1)S(1)} fusion(bf16[316,2,1024]{2,1,0:T(2,128)(2,1)} %get-tuple-element.890, s32[1024]{0:T(1024)S(1)} %pad_clamp_fusion.8), kind=kCustom, calls=%fused_computation.clone.clone.1 | custom fusion | bytes 4196352 | tf_op jit(solution)/shard_map/while/body/eval_jaxpr/jit(_take)/gather | solution.py:103
  488.7 26.4 %gather_fusion.1 = bf16[512,2,1024]{2,1,0:T(2,128)(2,1)S(1)} fusion(bf16[512,2,1024]{2,1,0:T(2,128)(2,1)} %get-tuple-element.891, s32[1024]{0:T(1024)S(1)} %pad_clamp_fusion.9), kind=kCustom, calls=%fused_computation.1.clone.clone.1 | custom fusion | bytes 4196352 | tf_op jit(solution)/shard_map/while/body/eval_jaxpr/jit(_take)/gather | solution.py:102
  524.0 26.1 %gather_fusion = bf16[512,2,1024]{2,1,0:T(2,128)(2,1)S(1)} fusion(bf16[316,2,1024]{2,1,0:T(2,128)(2,1)} %get-tuple-element.890, s32[1024]{0:T(1024)S(1)} %pad_clamp_fusion.8), kind=kCustom, calls=%fused_computation.clone.clone.1 | custom fusion | bytes 4196352 | tf_op jit(solution)/shard_map/while/body/eval_jaxpr/jit(_take)/gather | solution.py:103
  557.3 26.4 %gather_fusion.1 = bf16[512,2,1024]{2,1,0:T(2,128)(2,1)S(1)} fusion(bf16[512,2,1024]{2,1,0:T(2,128)(2,1)} %get-tuple-element.891, s32[1024]{0:T(1024)S(1)} %pad_clamp_fusion.9), kind=kCustom, calls=%fused_computation.1.clone.clone.1 | custom fusion | bytes 4196352 | tf_op jit(solution)/shard_map/while/body/eval_jaxpr/jit(_take)/gather | solution.py:102
  626.0 26.4 %gather_fusion.1 = bf16[512,2,1024]{2,1,0:T(2,128)(2,1)S(1)} fusion(bf16[512,2,1024]{2,1,0:T(2,128)(2,1)} %get-tuple-element.891, s32[1024]{0:T(1024)S(1)} %pad_clamp_fusion.9), kind=kCustom, calls=%fused_computation.1.clone.clone.1 | custom fusion | bytes 4196352 | tf_op jit(solution)/shard_map/while/body/eval_jaxpr/jit(_take)/gather | solution.py:102
  661.2 26.1 %gather_fusion = bf16[512,2,1024]{2,1,0:T(2,128)(2,1)S(1)} fusion(bf16[316,2,1024]{2,1,0:T(2,128)(2,1)} %get-tuple-element.890, s32[1024]{0:T(1024)S(1)} %pad_clamp_fusion.8), kind=kCustom, calls=%fused_computation.clone.clone.1 | custom fusion | bytes 4196352 | tf_op jit(solution)/shard_map/while/body/eval_jaxpr/jit(_take)/gather | solution.py:103
  694.6 26.4 %gather_fusion.1 = bf16[512,2,1024]{2,1,0:T(2,128)(2,1)S(1)} fusion(bf16[512,2,1024]{2,1,0:T(2,128)(2,1)} %get-tuple-element.891, s32[1024]{0:T(1024)S(1)} %pad_clamp_fusion.9), kind=kCustom, calls=%fused_computation.1.clone.clone.1 | custom fusion | bytes 4196352 | tf_op jit(solution)/shard_map/while/body/eval_jaxpr/jit(_take)/gather | solution.py:102
  763.2 26.4 %gather_fusion.1 = bf16[512,2,1024]{2,1,0:T(2,128)(2,1)S(1)} fusion(bf16[512,2,1024]{2,1,0:T(2,128)(2,1)} %get-tuple-element.891, s32[1024]{0:T(1024)S(1)} %pad_clamp_fusion.9), kind=kCustom, calls=%fused_computation.1.clone.clone.1 | custom fusion | bytes 4196352 | tf_op jit(solution)/shard_map/while/body/eval_jaxpr/jit(_take)/gather | solution.py:102
  798.5 26.1 %gather_fusion = bf16[512,2,1024]{2,1,0:T(2,128)(2,1)S(1)} fusion(bf16[316,2,1024]{2,1,0:T(2,128)(2,1)} %get-tuple-element.890, s32[1024]{0:T(1024)S(1)} %pad_clamp_fusion.8), kind=kCustom, calls=%fused_computation.clone.clone.1 | custom fusion | bytes 4196352 | tf_op jit(solution)/shard_map/while/body/eval_jaxpr/jit(_take)/gather | solution.py:103
  831.9 26.4 %gather_fusion.1 = bf16[512,2,1024]{2,1,0:T(2,128)(2,1)S(1)} fusion(bf16[512,2,1024]{2,1,0:T(2,128)(2,1)} %get-tuple-element.891, s32[1024]{0:T(1024)S(1)} %pad_clamp_fusion.9), kind=kCustom, calls=%fused_computation.1.clone.clone.1 | custom fusion | bytes 4196352 | tf_op jit(solution)/shard_map/while/body/eval_jaxpr/jit(_take)/gather | solution.py:102
  900.5 26.4 %gather_fusion.1 = bf16[512,2,1024]{2,1,0:T(2,128)(2,1)S(1)} fusion(bf16[512,2,1024]{2,1,0:T(2,128)(2,1)} %get-tuple-element.891, s32[1024]{0:T(1024)S(1)} %pad_clamp_fusion.9), kind=kCustom, calls=%fused_computation.1.clone.clone.1 | custom fusion | bytes 4196352 | tf_op jit(solution)/shard_map/while/body/eval_jaxpr/jit(_take)/gather | solution.py:102
  969.1 26.3 %gather_fusion.1 = bf16[512,2,1024]{2,1,0:T(2,128)(2,1)S(1)} fusion(bf16[512,2,1024]{2,1,0:T(2,128)(2,1)} %get-tuple-element.891, s32[1024]{0:T(1024)S(1)} %pad_clamp_fusion.9), kind=kCustom, calls=%fused_computation.1.clone.clone.1 | custom fusion | bytes 4196352 | tf_op jit(solution)/shard_map/while/body/eval_jaxpr/jit(_take)/gather | solution.py:102
  1037.6 26.3 %gather_fusion.1 = bf16[512,2,1024]{2,1,0:T(2,128)(2,1)S(1)} fusion(bf16[512,2,1024]{2,1,0:T(2,128)(2,1)} %get-tuple-element.891, s32[1024]{0:T(1024)S(1)} %pad_clamp_fusion.9), kind=kCustom, calls=%fused_computation.1.clone.clone.1 | custom fusion | bytes 4196352 | tf_op jit(solution)/shard_map/while/body/eval_jaxpr/jit(_take)/gather | solution.py:102
  1106.2 26.3 %gather_fusion.1 = bf16[512,2,1024]{2,1,0:T(2,128)(2,1)S(1)} fusion(bf16[512,2,1024]{2,1,0:T(2,128)(2,1)} %get-tuple-element.891, s32[1024]{0:T(1024)S(1)} %pad_clamp_fusion.9), kind=kCustom, calls=%fused_computation.1.clone.clone.1 | custom fusion | bytes 4196352 | tf_op jit(solution)/shard_map/while/body/eval_jaxpr/jit(_take)/gather | solution.py:102
  1174.6 26.3 %gather_fusion.1 = bf16[512,2,1024]{2,1,0:T(2,128)(2,1)S(1)} fusion(bf16[512,2,1024]{2,1,0:T(2,128)(2,1)} %get-tuple-element.891, s32[1024]{0:T(1024)S(1)} %pad_clamp_fusion.9), kind=kCustom, calls=%fused_computation.1.clone.clone.1 | custom fusion | bytes 4196352 | tf_op jit(solution)/shard_map/while/body/eval_jaxpr/jit(_take)/gather | solution.py:102
  1243.0 26.2 %gather_fusion.1 = bf16[512,2,1024]{2,1,0:T(2,128)(2,1)S(1)} fusion(bf16[512,2,1024]{2,1,0:T(2,128)(2,1)} %get-tuple-element.891, s32[1024]{0:T(1024)S(1)} %pad_clamp_fusion.9), kind=kCustom, calls=%fused_computation.1.clone.clone.1 | custom fusion | bytes 4196352 | tf_op jit(solution)/shard_map/while/body/eval_jaxpr/jit(_take)/gather | solution.py:102
  1311.3 26.2 %gather_fusion.1 = bf16[512,2,1024]{2,1,0:T(2,128)(2,1)S(1)} fusion(bf16[512,2,1024]{2,1,0:T(2,128)(2,1)} %get-tuple-element.891, s32[1024]{0:T(1024)S(1)} %pad_clamp_fusion.9), kind=kCustom, calls=%fused_computation.1.clone.clone.1 | custom fusion | bytes 4196352 | tf_op jit(solution)/shard_map/while/body/eval_jaxpr/jit(_take)/gather | solution.py:102
  1368.4 337.8 %while.50 = (s32[]{:T(128)}, f32[64,4096]{1,0:T(8,128)}, f32[64,4096]{1,0:T(8,128)}, s32[64,16]{0,1:T(8,128)}, s32[64,16]{0,1:T(8,128)}, /*index=5*/bf16[316,2,4...) while((s32[]{:T(128)}, f32[64,4096]{1,0:T(8,128)}, ...), condition=%wide.region_13.14_spmd.clone, body=%wide.region_12.13_spmd.clone.sunk | while | flops 5245379 | bytes 17837040 | solution.py:113
  (489 shorter events, 1154.7 us)
Async XLA Ops:
  0.6 118.0 %copy-start = (bf16[256,512]{1,0:T(8,128)(2,1)S(1)}, bf16[256,512]{1,0:T(8,128)(2,1)}, u32[]{:S(2)}) copy-start(bf16[256,512]{1,0:T(8,128)(2,1)} %param.25) | copy-start | bytes 786436
  18.4 8.6 copy-start.22
  42.7 8.7 copy-start.6
  42.7 8.7 copy-start.10
  42.7 8.7 copy-start.14
  42.7 8.7 copy-start.18
  42.7 8.7 copy-start.22
  91.2 8.6 copy-start.6
  91.3 8.6 copy-start.10
  91.3 8.6 copy-start.14
  91.3 8.6 copy-start.18
  91.3 8.6 copy-start.22
  99.9 18.7 %copy-start.11 = (f32[8]{0:T(128)}, f32[8]{0:T(128)S(1)}, u32[]{:S(2)}) copy-start(f32[8]{0:T(128)S(1)} %get-tuple-element.926) | copy-start | bytes 100
  99.9 18.7 %copy-start.15 = (f32[8]{0:T(128)}, f32[8]{0:T(128)S(1)}, u32[]{:S(2)}) copy-start(f32[8]{0:T(128)S(1)} %get-tuple-element.927) | copy-start | bytes 100
  99.9 18.7 %copy-start.19 = (f32[8]{0:T(128)}, f32[8]{0:T(128)S(1)}, u32[]{:S(2)}) copy-start(f32[8]{0:T(128)S(1)} %get-tuple-element.928) | copy-start | bytes 100
  100.8 17.9 %copy-start.7 = (bf16[256,128]{1,0:T(8,128)(2,1)S(1)}, bf16[256,128]{1,0:T(8,128)(2,1)}, u32[]{:S(2)}) copy-start(bf16[256,128]{1,0:T(8,128)(2,1)} %param.24) | copy-start | bytes 196612
  170.2 39.9 %all-to-all-start = ((bf16[128,2,4096]{2,1,0:T(2,128)(2,1)}), bf16[128,2,4096]{2,1,0:T(2,128)(2,1)S(1)}, u32[]{:S(2)}, u32[]{:S(2)}) async-start(bf16[128,2,4096]{2,1,0:T(2,128)(2,1)} %reshape.544), calls=%async_computation | async-start | bytes 4194304 | tf_op jit(solution)/shard_map/all_to_all | solution.py:172
  181.3 19.0 %copy-start.12 = (f32[8]{0:T(128)S(1)}, f32[8]{0:T(128)}, u32[]{:S(2)}) copy-start(f32[8]{0:T(128)} %copy-done.11) | copy-start | bytes 100
  181.3 19.0 %copy-start.16 = (f32[8]{0:T(128)S(1)}, f32[8]{0:T(128)}, u32[]{:S(2)}) copy-start(f32[8]{0:T(128)} %copy-done.15) | copy-start | bytes 100
  181.3 19.0 %copy-start.20 = (f32[8]{0:T(128)S(1)}, f32[8]{0:T(128)}, u32[]{:S(2)}) copy-start(f32[8]{0:T(128)} %copy-done.19) | copy-start | bytes 100
  220.5 19.9 %collective-permute-start = (bf16[512,2,3,64]{0,2,3,1:T(4,128)(2,1)S(1)}, bf16[512,2,3,64]{0,2,3,1:T(4,128)(2,1)}, u32[]{:S(2)}, u32[]{:S(2)}) collective-permute-start(bf16[512,2,3,64]{0,2,3,1:T(4,128)(2,1)S(1)} %get-tuple-element.612), channel_id=1, source_target_pairs={{0,1},{1,2},{2,3},{3,4},{4,5},{5,6},{6,7},{7,8},{8,9},{9,10},{10,1... | collective-permute-start | bytes 1179656 | tf_op jit(solution)/shard_map/ppermute | solution.py:16
  225.0 15.3 collective-permute-start.1
  245.8 1106.9 %collective-permute-start.2 = (bf16[512,2,32,3]{0,2,3,1:T(8,128)(2,1)}, bf16[512,2,32,3]{0,2,3,1:T(8,128)(2,1)}, u32[]{:S(2)}, u32[]{:S(2)}) collective-permute-start(bf16[512,2,32,3]{0,2,3,1:T(8,128)(2,1)} %get-tuple-element.610), channel_id=1, source_target_pairs={{0,16},{16,32},{32,48},{48,64},{64,80},{80,96},{96,112},{112,0},{1... | collective-permute-start | bytes 589832 | tf_op jit(solution)/shard_map/ppermute | solution.py:16
  246.1 1106.6 %collective-permute-start.3 = (bf16[512,2,32,3]{0,2,3,1:T(8,128)(2,1)}, bf16[512,2,32,3]{0,2,3,1:T(8,128)(2,1)}, u32[]{:S(2)}, u32[]{:S(2)}) collective-permute-start(bf16[512,2,32,3]{0,2,3,1:T(8,128)(2,1)} %get-tuple-element.611), channel_id=1, source_target_pairs={{16,0},{32,16},{48,32},{64,48},{80,64},{96,80},{112,96},{0,112},{1... | collective-permute-start | bytes 589832 | tf_op jit(solution)/shard_map/ppermute | solution.py:19
  (37 other events, 214.3 us)
where the time goes:
time: 1730 us; the launch traced here: 1710 us
  local copies, waits for them, and re-layouts  1050 us (61%)
  other arithmetic  563 us (33%)
  matrix products  58.9 us (3%)
  starting transfers between devices  21.1 us (1%)
    gather x32, local copies, waits for them, and re-layouts, add_slot(): factor = jnp.take(flat_table, jnp.maximum(offset_col, 0), axis=0)  499 us
    gather x32, local copies, waits for them, and re-layouts, add_slot(): picked = jnp.take(flat_patterns, jnp.maximum(source_col, 0), axis=0)  484 us
    add x32, other arithmetic, add_slot(): imag_total + factor_real * picked_imag + factor_imag * picked_real  184 us
    slice x32, other arithmetic, add_slot(): factor_real = jnp.where(live_slot, factor[:, 0].astype(jnp.float32), 0.0)  118 us
    select_n x32, other arithmetic, add_slot(): factor = jnp.take(flat_table, jnp.maximum(offset_col, 0), axis=0)  65.2 us
    reduce_sum x6, other arithmetic, shift_sum(): jnp.sum(child_terms[:, :, 0] * cosine - child_terms[:, :, 1] * sine, axis=1)  52.4 us
    dot_general x5, matrix products, parent_block(): jnp.einsum('pkcus,sv->pkcuv', halfway, azimuth_matrix, preferred_element_...  51.8 us
    select_n x32, other arithmetic, add_slot(): picked = jnp.take(flat_patterns, jnp.maximum(source_col, 0), axis=0)  47.8 us
  transfers between devices with their start and end apart: 5, of which 1 were waited for; matrix products, arithmetic and copies ran while one was open for 66% of the time, Pallas kernels for 0%

commit v1 on v0

v1 whole, which is shorter than its diff:
```python
import math

import jax
import jax.numpy as jnp
import numpy as np
from jax import lax
from jax.experimental import pallas as pl
from jax.experimental.pallas import tpu as pltpu
from jax.sharding import PartitionSpec as P

F32 = jnp.float32
BF16 = jnp.bfloat16
VMEM_LIMIT = 60 * 1024 * 1024


PAIRS = ((3, 0), (1, 2))


def theta_phase(rows):
    return rows / 8.0 * np.cos(np.pi * (np.arange(rows) + 0.5) / rows)


def plane_phases(rows, cols, count):
    theta = np.pi * (np.arange(rows) + 0.5) / rows
    phi = 2.0 * np.pi * np.arange(count) / cols
    x = np.sin(theta)[:, None] * np.cos(phi)[None, :]
    y = np.sin(theta)[:, None] * np.sin(phi)[None, :]
    return rows / 8.0 * (x + y), rows / 8.0 * (x - y)


def fold_factors(rows, inner):
    phase = theta_phase(rows)[:, None]
    cosine = np.broadcast_to(np.cos(phase), (rows, inner))
    sine = np.broadcast_to(np.sin(phase), (rows, inner))
    top = np.concatenate([cosine, sine, cosine, -sine], axis=1)
    bottom = np.concatenate([-sine, cosine, sine, cosine], axis=1)
    return top.astype(np.float32), bottom.astype(np.float32)


def dot(a, b):
    return jnp.dot(a, b, preferred_element_type=F32)


def dot_t(a, b):
    return lax.dot_general(a, b, (((1,), (1,)), ((), ())), preferred_element_type=F32)


def aggregate_body(
    pat, a7, b7, a6, b6, top7, bottom7, cz, sz, tab6, tab5, out, m7, m6, level6, mixed, half6
):
    rows7, rows6, rows5 = a7.shape[1], a7.shape[0], a6.shape[0]
    cols6, cols5 = b7.shape[1], b6.shape[1]

    @pl.when(pl.program_id(0) == 0)
    def _():
        src = lax.broadcasted_iota(jnp.int32, (rows7, 4 * rows7), 0)
        dst = lax.broadcasted_iota(jnp.int32, (rows7, 4 * rows7), 1)
        spread = jnp.where((dst & (rows7 - 1)) == src, 1.0, 0.0).astype(BF16)
        wide = dot(a7[...], spread)
        m7[0:rows6, :] = (wide * top7[...]).astype(BF16)
        m7[rows6 : 2 * rows6, :] = (wide * bottom7[...]).astype(BF16)
        base = a6[...].astype(F32)
        c = base * cz[...]
        s = base * sz[...]
        m6[0, :, 0:rows6] = c.astype(BF16)
        m6[0, :, rows6 : 2 * rows6] = (-s).astype(BF16)
        m6[1, :, 0:rows6] = c.astype(BF16)
        m6[1, :, rows6 : 2 * rows6] = s.astype(BF16)

    step = 2 * rows7
    for o6 in range(8):
        base = o6 * 8 * step
        parts = []
        for k in range(4):
            low = pat[base + k * step : base + (k + 1) * step, :]
            high = pat[base + (k + 4) * step : base + (k + 5) * step, :]
            parts.append(jnp.concatenate([low, high], axis=0))
        lanes = parts[0].shape[1]
        h = dot(m7[...], jnp.concatenate(parts, axis=1))
        rows = []
        for a, b in PAIRS:
            ya = h[:, a * lanes : (a + 1) * lanes]
            yb = h[:, b * lanes : (b + 1) * lanes]
            rows.append((ya + yb).astype(BF16))
            rows.append((ya - yb).astype(BF16))
        y = dot(jnp.concatenate(rows, axis=0), b7[...])
        for half in range(2):
            cols = slice(half * (cols6 // 2), (half + 1) * (cols6 // 2))
            re = None
            for q in range(2):
                at = q * 4 * rows6
                pr = y[at : at + rows6, cols]
                pi = y[at + rows6 : at + 2 * rows6, cols]
                qr = y[at + 2 * rows6 : at + 3 * rows6, cols]
                qi = y[at + 3 * rows6 : at + 4 * rows6, cols]
                c = tab6[2 * q]
                s = tab6[2 * q + 1]
                if half == 1:
                    dr = c * pr + s * qi
                    di = c * pi - s * qr
                else:
                    dr = c * pr - s * qi
                    di = c * pi + s * qr
                re, im = (dr, di) if re is None else (re + dr, im + di)
            level6[o6, 0, :, cols] = re
            level6[o6, 1, :, cols] = im

    for part in range(2):
        for r in range(0, rows6, 16):
            x = [level6[o, part, r : r + 16, :] for o in range(8)]
            for t in range(2):
                z = [x[k + 4] + x[k] if t == 0 else x[k + 4] - x[k] for k in range(4)]
                for q, (a, b) in enumerate(PAIRS):
                    mixed[2 * q, t, part, r : r + 16, :] = (z[a] + z[b]).astype(BF16)
                    mixed[2 * q + 1, t, part, r : r + 16, :] = (z[a] - z[b]).astype(BF16)

    for x in range(4):
        for part in range(2):
            rhs = jnp.concatenate([mixed[x, 0, part], mixed[x, 1, 1 - part]], axis=0)
            half6[x, part] = dot(m6[part], rhs).astype(BF16)

    block = 64
    quarter = cols5 // 4
    low_lane = lax.broadcasted_iota(jnp.int32, (block, quarter), 1) < quarter // 2
    for u in range(0, rows5, block):
        lhs = jnp.concatenate(
            [half6[x, part, u : u + block, :] for x in range(4) for part in range(2)], axis=0
        )
        y = dot(lhs, b6[...])
        for tile in range(4):
            cols = slice(tile * quarter, (tile + 1) * quarter)
            re = None
            for q in range(2):
                at = q * 4 * block
                pr = y[at : at + block, cols]
                pi = y[at + block : at + 2 * block, cols]
                qr = y[at + 2 * block : at + 3 * block, cols]
                qi = y[at + 3 * block : at + 4 * block, cols]
                place = (tile + q) % 4
                c = tab5[place % 2, 0, u : u + block, :]
                s = tab5[place % 2, 1, u : u + block, :]
                if place >= 2:
                    dr = c * pr + s * qi
                    di = c * pi - s * qr
                else:
                    dr = c * pr - s * qi
                    di = c * pi + s * qr
                if q == 0:
                    re, im = dr, di
                else:
                    re, im = re + dr, im + di
            if_low = jnp.where(low_lane, re, pltpu.roll(im, quarter // 2, 1)).astype(BF16)
            if_high = jnp.where(low_lane, pltpu.roll(re, quarter // 2, 1), im).astype(BF16)
            for r in range(0, block, 16):
                band = (u + r) // 16
                out[2 * tile * 16 + band, 0] = if_low[r : r + 16, :]
                out[(2 * tile + 1) * 16 + band, 0] = if_high[r : r + 16, :]


def aggregate(patterns7, polar_up7, azimuth_up7, polar_up6, azimuth_up6):
    children, _, rows7, cols7 = patterns7.shape
    rows6, rows5 = polar_up7.shape[0], polar_up6.shape[0]
    cols6, cols5 = azimuth_up7.shape[1], azimuth_up6.shape[1]
    clusters = children // 64
    pat = patterns7.reshape(children * 2 * rows7, cols7)
    top7, bottom7 = fold_factors(rows6, rows7)
    z = theta_phase(rows5)[:, None]
    cz = np.broadcast_to(np.cos(z), (rows5, rows6)).astype(np.float32)
    sz = np.broadcast_to(np.sin(z), (rows5, rows6)).astype(np.float32)
    f0, f1 = plane_phases(rows6, cols6, cols6 // 2)
    tab6 = np.stack([np.cos(f0), np.sin(f0), np.cos(f1), np.sin(f1)]).astype(np.float32)
    g0, _ = plane_phases(rows5, cols5, cols5 // 2)
    g0 = g0.reshape(rows5, 2, cols5 // 4).transpose(1, 0, 2)
    tab5 = np.stack([np.cos(g0), np.sin(g0)], axis=1).astype(np.float32)
    full = lambda shape: pl.BlockSpec(shape, lambda g: (0,) * len(shape))
    consts = (top7, bottom7, cz, sz, tab6, tab5)
    weights = (polar_up7, azimuth_up7, polar_up6, azimuth_up6)
    lines = pat.shape[0] // clusters
    return pl.pallas_call(
        aggregate_body,
        grid=(clusters,),
        in_specs=[pl.BlockSpec((lines, cols7), lambda g: (g, 0))]
        + [full(a.shape) for a in weights]
        + [full(a.shape) for a in consts],
        out_specs=pl.BlockSpec((128, 1, 16, 128), lambda g: (0, g, 0, 0)),
        out_shape=jax.ShapeDtypeStruct((128, clusters, 16, 128), BF16),
        scratch_shapes=[
            pltpu.VMEM((2 * rows6, 4 * rows7), BF16),
            pltpu.VMEM((2, rows5, 2 * rows6), BF16),
            pltpu.VMEM((8, 2, rows6, cols6), F32),
            pltpu.VMEM((4, 2, 2, rows6, cols6), BF16),
            pltpu.VMEM((4, 2, rows5, cols6), BF16),
        ],
        compiler_params=pltpu.CompilerParams(vmem_limit_bytes=VMEM_LIMIT),
        name="aggregate",
    )(pat, *weights, *[jnp.asarray(a) for a in consts])


def table_body(tr, out, spread):
    theta = pl.program_id(0)
    entries = out.shape[0]
    count = tr.shape[3]
    re = tr[0, 0]
    im = tr[1, 0]
    stack = jnp.concatenate([re, re, im, -im], axis=0)
    row = lax.broadcasted_iota(jnp.int32, (entries, count), 0)
    col = lax.broadcasted_iota(jnp.int32, (entries, count), 1)
    unit = jnp.where(row == col, 1.0, 0.0).astype(BF16)
    turned = dot_t(unit, stack)
    for j in range(2):
        spread[j, pl.ds(theta, entries, 16), :] = turned[:, j * 128 : (j + 1) * 128]

    @pl.when(theta == 15)
    def _():
        for j in range(2):
            out[:, j] = spread[j].reshape(entries, 16, 128).astype(BF16)


def transfer_table(transfer):
    count, _, rows, cols = transfer.shape
    entries = (count + 1 + 7) // 8 * 8
    return pl.pallas_call(
        table_body,
        grid=(rows,),
        in_specs=[pl.BlockSpec((2, 1, cols, count), lambda i: (0, i, 0, 0))],
        out_specs=pl.BlockSpec((entries, 2, rows, 2 * cols), lambda i: (0, 0, 0, 0)),
        out_shape=jax.ShapeDtypeStruct((entries, 2, rows, 2 * cols), BF16),
        scratch_shapes=[pltpu.VMEM((2, entries * rows, 2 * cols), F32)],
        compiler_params=pltpu.CompilerParams(vmem_limit_bytes=VMEM_LIMIT),
        name="transfer_table",
    )(transfer.transpose(1, 2, 3, 0))


def tree(terms):
    while len(terms) > 1:
        terms = [terms[i] + terms[i + 1] for i in range(0, len(terms), 2)]
    return terms[0]


def translate5_body(src, off, level, table, out, total):
    targets, rows, lanes = level.shape
    slots = src.shape[0]

    def one(t, carry):
        acc1 = jnp.zeros((rows, lanes), F32)
        acc2 = jnp.zeros((rows, lanes), F32)
        for j in range(0, slots, 4):
            first, second = [], []
            for i in range(4):
                x = level[src[j + i, t]]
                w = table.at[off[j + i, t]]
                first.append(w[0] * x)
                second.append(w[1] * x)
            acc1 = acc1 + tree(first).astype(F32)
            acc2 = acc2 + tree(second).astype(F32)
        total[pl.ds(pl.multiple_of(t * rows, rows), rows), :] = acc1 + pltpu.roll(acc2, lanes // 2, 1)
        return carry

    lax.fori_loop(0, targets, one, 0, unroll=2)
    unit = jnp.where(
        lax.broadcasted_iota(jnp.int32, (lanes, lanes), 0)
        == lax.broadcasted_iota(jnp.int32, (lanes, lanes), 1),
        1.0,
        0.0,
    ).astype(BF16)
    for theta in range(rows):
        turned = dot_t(unit, total[pl.ds(theta, targets, rows), :].astype(BF16)).astype(BF16)
        out[0, theta] = turned[: lanes // 2]
        out[1, theta] = turned[lanes // 2 :]


def translate5(level, table, sources, offsets):
    targets, rows, lanes = level.shape
    smem = pl.BlockSpec(memory_space=pltpu.SMEM)
    vmem = pl.BlockSpec(memory_space=pltpu.VMEM)
    turned = pl.pallas_call(
        translate5_body,
        in_specs=[smem, smem, vmem, vmem],
        out_specs=vmem,
        out_shape=jax.ShapeDtypeStruct((2, rows, lanes // 2, targets), BF16),
        scratch_shapes=[pltpu.VMEM((targets * rows, lanes), F32)],
        compiler_params=pltpu.CompilerParams(vmem_limit_bytes=VMEM_LIMIT),
        name="translate5",
    )(sources, offsets, level, table)
    return turned.transpose(3, 0, 1, 2)


def edge_picks():
    pick = np.zeros((96, 256), np.float32)
    for side in range(2):
        for n in range(48):
            parent, child, j = n // 24, n % 24 // 3, n % 3
            pick[side * 48 + n, parent * 128 + child * 16 + (13 if side == 0 else 0) + j] = 1.0
    return pick


def edges_body(level, pick, right, left, last, first, last_r, first_r, last_l, first_l):
    lane = lax.broadcasted_iota(jnp.int32, (1024, 256), 0)
    col = lax.broadcasted_iota(jnp.int32, (1024, 256), 1)
    side = col >> 7
    place = lane >> 7
    part = (lane >> 6) & 1
    j = col & 3
    hit = (
        (((col & 127) >> 4) == place)
        & (((col >> 3) & 1) == side)
        & (((col >> 2) & 1) == part)
        & (j < 3)
        & ((lane & 63) == jnp.where(side == 0, 61 + j, j))
    )
    spread = jnp.where(hit, 1.0, 0.0).astype(BF16)
    for g in range(8):
        lhs = jnp.concatenate([level[8 * g + i] for i in range(8)], axis=1)
        both = dot(lhs, spread).astype(BF16)
        right[g] = both[:, :128]
        left[g] = both[:, 128:]

    def rows_of(source, count, low, high):
        for i in range(count):
            rhs = jnp.concatenate([source[2 * i], source[2 * i + 1]], axis=0)
            both = dot(pick[...], rhs).astype(BF16)
            low[i] = both[:48]
            high[i] = both[48:]

    rows_of(level, 32, last, first)
    rows_of(right, 4, last_r, first_r)
    rows_of(left, 4, last_l, first_l)


def edges(level):
    shape = lambda *s: jax.ShapeDtypeStruct(s, BF16)
    pick = jnp.asarray(edge_picks(), BF16)
    return pl.pallas_call(
        edges_body,
        out_shape=(shape(8, 128, 128),) * 2 + (shape(32, 48, 128),) * 2 + (shape(4, 48, 128),) * 4,
        compiler_params=pltpu.CompilerParams(vmem_limit_bytes=VMEM_LIMIT),
        name="edges",
    )(level, pick)


def stencil_maps():
    ext = np.zeros((1, 224), np.int32)
    factor = np.zeros((2, 8, 224), np.float32)
    sign = np.zeros((4, 8))
    for q, (a, b) in enumerate(PAIRS):
        for h in range(2):
            sign[2 * q, a + 4 * h] = sign[2 * q, b + 4 * h] = 1.0
            sign[2 * q + 1, a + 4 * h] = 1.0
            sign[2 * q + 1, b + 4 * h] = -1.0
    for col in range(224):
        if col < 128:
            owner, child, ext[0, col] = (0, 1), col // 16, col % 16 + 3
        else:
            n = (col - 128) % 48
            owner, child = (n // 24,), n % 24 // 3
            ext[0, col] = n % 3 + (0 if col < 176 else 19)
        for parity in owner:
            for x in range(4):
                factor[parity, 2 * x, col] = sign[x, child]
                factor[parity, 2 * x + 1, col] = sign[x, child] * (1.0 if child >= 4 else -1.0)
    return ext, factor


def stencils_body(tap_u, weight_u, trig, tap_v, weight_v, ext, factor, polar, azimuth):
    rows = tap_u.shape[0]
    base = jnp.zeros((rows, ext.shape[1]), F32)
    for k in range(4):
        base = base + jnp.where(tap_u[:, k : k + 1] == ext[...], weight_u[:, k : k + 1], 0.0)
    for parity in range(2):
        for kind in range(8):
            turned = base * trig[:, kind % 2 : kind % 2 + 1]
            polar[parity, kind * rows : (kind + 1) * rows, :] = (
                turned * factor[parity, kind : kind + 1, :]
            ).astype(BF16)
    i = lax.broadcasted_iota(jnp.int32, (128, 128), 0)

    def fill(at, matrix, part, index):
        first = part == 0
        azimuth[index, at : at + 128, :128] = jnp.where(first, matrix, 0.0).astype(BF16)
        azimuth[index, at : at + 128, 128:] = jnp.where(first, 0.0, matrix).astype(BF16)
        azimuth[index, at + 128 : at + 256, :128] = jnp.where(first, 0.0, -matrix).astype(BF16)
        azimuth[index, at + 128 : at + 256, 128:] = jnp.where(first, matrix, 0.0).astype(BF16)

    def matrix_at(q):
        total = jnp.zeros((128, 128), F32)
        for k in range(4):
            total = total + jnp.where(tap_v[k : k + 1, :] == q, weight_v[k : k + 1, :], 0.0)
        return total

    own = matrix_at((i & 63) + 3)
    j = i & 3
    halo = jnp.where(j < 3, matrix_at(j + 67 * ((i >> 3) & 1)), 0.0)
    for index in range(8):
        fill(0, own, i >> 6, index)
        fill(256, jnp.where((i >> 4) == index, halo, 0.0), (i >> 2) & 1, index)


def stencils(tap_u, weight_u, trig, tap_v, weight_v):
    ext, factor = stencil_maps()
    rows = tap_u.shape[0]
    return pl.pallas_call(
        stencils_body,
        out_shape=(
            jax.ShapeDtypeStruct((2, 8 * rows, 224), BF16),
            jax.ShapeDtypeStruct((8, 512, 256), BF16),
        ),
        compiler_params=pltpu.CompilerParams(vmem_limit_bytes=VMEM_LIMIT),
        name="stencils",
    )(tap_u, weight_u, trig, tap_v, weight_v, jnp.asarray(ext), jnp.asarray(factor))


def top_body(
    src, off, level, from_left, from_right, low, high, low_l, low_r, high_l, high_r, polar, azimuth,
    tab, transfer, out, table, half, level4, sem,
):
    count = transfer.shape[0]
    fetch = pltpu.make_async_copy(transfer, table.at[pl.ds(0, count)], sem)
    fetch.start()
    table[count] = jnp.zeros(table.shape[1:], BF16)

    def theta_stage(i, carry):
        for parity in range(2):
            rhs = jnp.concatenate([level[2 * i + parity], low[i], high[i]], axis=0)
            half[2 * i + parity] = dot(polar[parity], rhs).astype(BF16)
        return carry

    lax.fori_loop(0, 32, theta_stage, 0, unroll=4)
    for i in range(4):
        rows_low = low_l[i] + low_r[i]
        rows_high = high_l[i] + high_r[i]
        for parity in range(2):
            g = 2 * i + parity
            rhs = jnp.concatenate([from_left[g] + from_right[g], rows_low, rows_high], axis=0)
            half[64 + g] = dot(polar[parity], rhs).astype(BF16)

    def phi_stage(place, carry):
        rows = []
        for g in range(8):
            for x in range(4):
                a = slice(64 * x, 64 * x + 32)
                b = slice(64 * x + 32, 64 * x + 64)
                p = 8 * g + place
                rows.append(
                    jnp.concatenate([half[p, a], half[p, b], half[64 + g, a], half[64 + g, b]], axis=1)
                )
        y = dot(jnp.concatenate(rows, axis=0), azimuth[place])
        for g in range(8):
            re = im = None
            for q in range(2):
                at = 128 * g + 64 * q
                pr = y[at : at + 32, :128]
                pi = y[at : at + 32, 128:]
                qr = y[at + 32 : at + 64, :128]
                qi = y[at + 32 : at + 64, 128:]
                c = tab[2 * q]
                s = tab[2 * q + 1]
                dr = c * pr - s * qi
                di = c * pi + s * qr
                re, im = (dr, di) if q == 0 else (re + dr, im + di)
            level4[8 * g + place, 0] = re.astype(BF16)
            level4[8 * g + place, 1] = im.astype(BF16)
        return carry

    lax.fori_loop(0, 8, phi_stage, 0)
    fetch.wait()
    slots = src.shape[0]

    def one(t, carry):
        re = jnp.zeros((32, 128), F32)
        im = jnp.zeros((32, 128), F32)
        for j in range(0, slots, 2):
            terms_r, terms_i = [], []
            for i in range(2):
                x = level4.at[src[j + i, t]]
                w = table.at[off[j + i, t]]
                xr, xi = x[0], x[1]
                wr, wi = w[0], w[1]
                terms_r.append(wr * xr - wi * xi)
                terms_i.append(wr * xi + wi * xr)
            re = re + tree(terms_r).astype(F32)
            im = im + tree(terms_i).astype(F32)
        out[t, 0] = re.astype(BF16)
        out[t, 1] = im.astype(BF16)
        return carry

    lax.fori_loop(0, out.shape[0], one, 0)


def top_level(level, halos, polar, azimuth, tab, transfer, sources, offsets):
    count, _, rows, cols = transfer.shape
    smem = pl.BlockSpec(memory_space=pltpu.SMEM)
    vmem = pl.BlockSpec(memory_space=pltpu.VMEM)
    parents = level.shape[0]
    return pl.pallas_call(
        top_body,
        in_specs=[smem, smem] + [vmem] * 12 + [pl.BlockSpec(memory_space=pl.ANY)],
        out_specs=vmem,
        out_shape=jax.ShapeDtypeStruct((parents, 2, rows, cols), BF16),
        scratch_shapes=[
            pltpu.VMEM((count + 1, 2, rows, cols), BF16),
            pltpu.VMEM((72, 256, 128), BF16),
            pltpu.VMEM((parents, 2, rows, cols), BF16),
            pltpu.SemaphoreType.DMA,
        ],
        compiler_params=pltpu.CompilerParams(vmem_limit_bytes=VMEM_LIMIT),
        name="top_level",
    )(sources, offsets, level, *halos, polar, azimuth, tab, transfer)


def shards(
    patterns7,
    polar_up7,
    azimuth_up7,
    polar_up6,
    azimuth_up6,
    polar_first,
    polar_weights,
    azimuth_first,
    azimuth_weights,
    transfer5,
    sources5,
    offsets5,
    transfer4,
    sources4,
    offsets4,
):
    bands = lax.axis_size("ang")
    blocks = lax.axis_size("clu")
    band = lax.axis_index("ang")
    block = lax.axis_index("clu")

    send = aggregate(patterns7, polar_up7, azimuth_up7, polar_up6, azimuth_up6)
    arrived = lax.all_to_all(send, ("clu", "ang"), split_axis=0, concat_axis=0, tiled=True)

    count5 = transfer5.shape[0]
    count4 = transfer4.shape[0]
    table5 = transfer_table(transfer5)
    src5 = jnp.maximum(sources5.T, 0)
    off5 = jnp.where(offsets5.T < 0, count5, offsets5.T)
    src4 = jnp.maximum(sources4.T, 0)
    off4 = jnp.where(offsets4.T < 0, count4, offsets4.T)
    rows4 = polar_first.shape[0]
    cols4 = azimuth_first.shape[0]
    band_rows = rows4 // bands
    block_cols = cols4 // blocks
    taps = jnp.arange(4, dtype=jnp.int32)
    tap_u = lax.dynamic_slice_in_dim(polar_first, band * band_rows, band_rows, 0)
    tap_u = (tap_u - band * (band_rows // 2) + 3)[:, None] + taps[None, :]
    weight_u = lax.dynamic_slice_in_dim(polar_weights, band * band_rows, band_rows, 0).astype(F32)
    tap_v = lax.dynamic_slice_in_dim(azimuth_first, block * block_cols, block_cols, 0)
    tap_v = (tap_v[None, :] + taps[:, None] - block * (block_cols // 2) + 3) % (cols4 // 2)
    weight_v = lax.dynamic_slice_in_dim(azimuth_weights, block * block_cols, block_cols, 0)
    weight_v = weight_v.T.astype(F32)
    theta = (jnp.arange(band_rows, dtype=jnp.int32) + band * band_rows).astype(F32)
    theta = (theta + 0.5) * (math.pi / rows4)
    phi = (jnp.arange(block_cols, dtype=jnp.int32) + block * block_cols).astype(F32)
    phi = phi * (2.0 * math.pi / cols4)
    scale = rows4 / 8.0
    lift = scale * jnp.cos(theta)
    trig = jnp.stack([jnp.cos(lift), jnp.sin(lift)], axis=1)
    x = jnp.sin(theta)[:, None] * jnp.cos(phi)[None, :]
    y = jnp.sin(theta)[:, None] * jnp.sin(phi)[None, :]
    f0 = scale * (x + y)
    f1 = scale * (x - y)
    tab = jnp.stack([jnp.cos(f0), jnp.sin(f0), jnp.cos(f1), jnp.sin(f1)])
    polar, azimuth = stencils(tap_u, weight_u, trig, tap_v, weight_v)

    level = arrived.reshape(64, 128, 128)
    right, left, last, first, last_r, first_r, last_l, first_l = edges(level)

    def moved(value, step_block, step_band):
        pairs = []
        for c in range(blocks):
            for a in range(bands):
                to = a + step_band
                if 0 <= to < bands:
                    pairs.append((c * bands + a, (c + step_block) % blocks * bands + to))
        return lax.ppermute(value, ("clu", "ang"), pairs)

    halos = (
        moved(right, 1, 0),
        moved(left, -1, 0),
        moved(last, 0, 1),
        moved(first, 0, -1),
        moved(last_r, 1, 1),
        moved(last_l, -1, 1),
        moved(first_r, 1, -1),
        moved(first_l, -1, -1),
    )
    translated5 = translate5(arrived.reshape(512, 16, 128), table5, src5, off5)
    translated4 = top_level(level, halos, polar, azimuth, tab, transfer4, src4, off4)
    return (translated5, translated4)


def solution(mesh):
    in_specs = (
        P(("clu", "ang"), None, None, None),
        P(),
        P(),
        P(),
        P(),
        P(),
        P(),
        P(),
        P(),
        P(None, None, "ang", "clu"),
        P(),
        P(),
        P(None, None, "ang", "clu"),
        P(),
        P(),
    )
    out_specs = (P(None, None, "ang", "clu"), P(None, None, "ang", "clu"))
    return jax.shard_map(shards, mesh=mesh, in_specs=in_specs, out_specs=out_specs, check_vma=False)
```

time: 1730 us -> 180 us (0.10)
  local copies, waits for them, and re-layouts: 1050 us -> 5.51 us
  other arithmetic: 563 us -> 7.35 us
  Pallas kernels: 0 us -> 95.1 us
  matrix products: 58.9 us -> 0 us
  waiting for transfers between devices: 9.19 us -> 31.8 us
    gather x64 -> x0, local copies, waits for them, and re-layouts: 982 us -> none  [the longest x32 499 us: add_slot(): factor = jnp.take(flat_table, jnp.maximum(offset_col, 0), axis=0)]
    add x35 -> x2, other arithmetic: 185 us -> 1.43 us  [shards(): tap_u = (tap_u - band * (band_rows // 2) + 3)[:, None] + taps[None, :]]
    slice x32 -> x0, other arithmetic: 118 us -> none  [add_slot(): factor_real = jnp.where(live_slot, factor[:, 0].astype(jnp.float32), 0.0)]
    select_n x65 -> x3, other arithmetic: 114 us -> 1.8 us  [the longest x1 0.61 us: shards(): off5 = jnp.where(offsets5.T < 0, count5, offsets5.T)]
    pallas_call x0 -> x6, Pallas kernels: none -> 95.1 us  [the longest x1 42.4 us: translate5(): pl.pallas_call(translate5_body, in_specs=[smem, smem, vmem, vmem], out_sp...]
    dot_general x7 -> x0, matrix products: 58.9 us -> none  [the longest x5 51.8 us: parent_block(): jnp.einsum('pkcus,sv->pkcuv', halfway, azimuth_matrix, preferred_element_...]
    reduce_sum x8 -> x0, other arithmetic: 52.6 us -> none  [the longest x6 52.4 us: shift_sum(): jnp.sum(child_terms[:, :, 0] * cosine - child_terms[:, :, 1] * sine, axis=1)]
    cos x9 -> x1, other arithmetic: 38.5 us -> 0.2 us  [shards(): tab = jnp.stack([jnp.cos(f0), jnp.sin(f0), jnp.cos(f1), jnp.sin(f1)])]
  transfers between devices with their start and end apart: 5 -> 9, of which waited for: 1 -> 2; matrix products, arithmetic and copies ran while one was open for 66% -> 5% of each run, Pallas kernels for 0% -> 32%
where the time goes in v1:
time: 180 us; the launch traced here: 177 us
  Pallas kernels  95.1 us (53%)
  starting transfers between devices  36.2 us (20%)
  waiting for transfers between devices  31.8 us (18%)
  other arithmetic  7.35 us (4%)
  local copies, waits for them, and re-layouts  5.51 us (3%)
    pallas_call x1, Pallas kernels, translate5(): pl.pallas_call(translate5_body, in_specs=[smem, smem, vmem, vmem], out_sp...  42.4 us
    ppermute x8, starting transfers between devices, moved(): return lax.ppermute(value, ('clu', 'ang'), pairs)  25.4 us
    all_to_all x1, waiting for transfers between devices, shards(): lax.all_to_all(send, ('clu', 'ang'), split_axis=0, concat_axis=0, tiled=T...  22.7 us
    pallas_call x1, Pallas kernels, top_level(): pl.pallas_call(top_body, in_specs=[smem, smem] + [vmem] * 12 + [pl.BlockS...  17 us
    pallas_call x1, Pallas kernels, aggregate(): pl.pallas_call(aggregate_body, grid=(clusters,), in_specs=[pl.BlockSpec((...  16.7 us
    pallas_call x1, Pallas kernels, transfer_table(): pl.pallas_call(table_body, grid=(rows,), in_specs=[pl.BlockSpec((2, 1, co...  12.4 us
    all_to_all x1, starting transfers between devices, shards(): lax.all_to_all(send, ('clu', 'ang'), split_axis=0, concat_axis=0, tiled=T...  10.8 us
    ppermute x8, waiting for transfers between devices, moved(): return lax.ppermute(value, ('clu', 'ang'), pairs)  9.05 us
  transfers between devices with their start and end apart: 9, of which 2 were waited for; matrix products, arithmetic and copies ran while one was open for 5% of the time, Pallas kernels for 32%

profile of v1, /device:TPU:7, one launch (start us, length us, event | category | flops | bytes accessed | tf_op | source)
XLA Modules:
  0.0 177.0 jit_solution(17641482848095464938)
XLA Ops:
  0.6 1.4 copy.28.a7
  2.1 16.7 %aggregate.1 = bf16[128,4,16,128]{3,2,1,0:T(8,128)(2,1)} custom-call(bf16[32768,128]{1,0:T(8,128)(2,1)} %bitcast.18, bf16[128,64]{1,0:T(8,128)(2,1)} %copy.28.a7, bf16[128,256]{1,0:T(8,128)(2,1)} %b7.1, bf16[256,128]{1,0:T(8,128)(2,1)} %a6.1, bf16[256,512]{1,0:T(8,128)(2,1)} %b6.1, f32[128,256]{1,0:T(8,128)} %constant.68.clone.top7, ...), custom_call_target="tpu_custom_call" | custom-call | tf_op jit(solution)/shard_map/aggregate/pallas_call | solution.py:179
  18.8 10.8 %all-to-all-start = ((bf16[128,4,16,128]{3,2,1,0:T(8,128)(2,1)}), bf16[128,4,16,128]{3,2,1,0:T(8,128)(2,1)S(1)}, u32[]{:S(2)}, u32[]{:S(2)}) async-start(bf16[128,4,16,128]{3,2,1,0:T(8,128)(2,1)} %aggregate.1), calls=%async_computation | async-start | bytes 4194304 | tf_op jit(solution)/shard_map/all_to_all | solution.py:533
  29.6 0.8 dynamic_slice.14
  30.4 0.8 subtract_add_fusion
  31.4 0.6 pad_maximum_fusion.tab
  33.8 0.7 iota_add_fusion.tap_u
  35.7 22.7 %all-to-all-done = bf16[128,4,16,128]{3,2,1,0:T(8,128)(2,1)S(1)} async-done(((bf16[128,4,16,128]{3,2,1,0:T(8,128)(2,1)}), bf16[128,4,16,128]{3,2,1,0:T(8,128)(2,1)S(1)}, u32[]{:S(2)}, u32[]{:S(2)}) %all-to-all-start) | async-done | bytes 2097184 | tf_op jit(solution)/shard_map/all_to_all | solution.py:533
  58.5 1.4 copy-done.1
  59.9 3.9 %edges.1 = (bf16[8,128,128]{2,1,0:T(8,128)(2,1)}, bf16[8,128,128]{2,1,0:T(8,128)(2,1)}, bf16[32,48,128]{2,1,0:T(8,128)(2,1)}, bf16[32,48,128]{2,1,0:T(8,128)(2,1...) custom-call(bf16[64,128,128]{2,1,0:T(8,128)(2,1)} %bitcast.15, ...), custom_call_target="tpu_custom_call" | custom-call | tf_op jit(solution)/shard_map/edges/pallas_call | solution.py:333
  63.8 4.3 %collective-permute-start.4 = (bf16[4,48,128]{2,1,0:T(8,128)(2,1)}, bf16[4,48,128]{2,1,0:T(8,128)(2,1)S(1)}, u32[]{:S(2)}, u32[]{:S(2)}) collective-permute-start(bf16[4,48,128]{2,1,0:T(8,128)(2,1)} %get-tuple-element.16), channel_id=1, source_target_pairs={{0,17},{1,18},{2,19},{3,20},{4,21},{5,22},{6,23},{7,24},{8,25},{9,... | collective-permute-start | bytes 147464 | tf_op jit(solution)/shard_map/ppermute | solution.py:578
  68.1 2.9 %collective-permute-start.2 = (bf16[32,48,128]{2,1,0:T(8,128)(2,1)}, bf16[32,48,128]{2,1,0:T(8,128)(2,1)S(1)}, u32[]{:S(2)}, u32[]{:S(2)}) collective-permute-start(bf16[32,48,128]{2,1,0:T(8,128)(2,1)} %get-tuple-element.14), channel_id=1, source_target_pairs={{0,1},{1,2},{2,3},{3,4},{4,5},{5,6},{6,7},{7,8},{8,9},{9,10},{10,1... | collective-permute-start | bytes 1179656 | tf_op jit(solution)/shard_map/ppermute | solution.py:578
  71.0 1.9 %collective-permute-start.3 = (bf16[32,48,128]{2,1,0:T(8,128)(2,1)}, bf16[32,48,128]{2,1,0:T(8,128)(2,1)S(1)}, u32[]{:S(2)}, u32[]{:S(2)}) collective-permute-start(bf16[32,48,128]{2,1,0:T(8,128)(2,1)} %get-tuple-element.15), channel_id=1, source_target_pairs={{1,0},{2,1},{3,2},{4,3},{5,4},{6,5},{7,6},{8,7},{9,8},{10,9},{11,1... | collective-permute-start | bytes 1179656 | tf_op jit(solution)/shard_map/ppermute | solution.py:578
  72.9 1.3 convert_bitcast_fusion.weight_v
  74.2 8.7 %collective-permute-start.5 = (bf16[4,48,128]{2,1,0:T(8,128)(2,1)}, bf16[4,48,128]{2,1,0:T(8,128)(2,1)S(1)}, u32[]{:S(2)}, u32[]{:S(2)}) collective-permute-start(bf16[4,48,128]{2,1,0:T(8,128)(2,1)} %get-tuple-element.17), channel_id=1, source_target_pairs={{0,113},{1,114},{2,115},{3,116},{4,117},{5,118},{6,119},{7,120},{8... | collective-permute-start | bytes 147464 | tf_op jit(solution)/shard_map/ppermute | solution.py:578
  83.0 3.5 %collective-permute-start.1 = (bf16[8,128,128]{2,1,0:T(8,128)(2,1)}, bf16[8,128,128]{2,1,0:T(8,128)(2,1)S(1)}, u32[]{:S(2)}, u32[]{:S(2)}) collective-permute-start(bf16[8,128,128]{2,1,0:T(8,128)(2,1)} %get-tuple-element.13), channel_id=1, source_target_pairs={{0,112},{1,113},{2,114},{3,115},{4,116},{5,117},{6,118},{7,119},{8... | collective-permute-start | bytes 786440 | tf_op jit(solution)/shard_map/ppermute | solution.py:578
  86.6 1.9 %collective-permute-start.6 = (bf16[4,48,128]{2,1,0:T(8,128)(2,1)}, bf16[4,48,128]{2,1,0:T(8,128)(2,1)S(1)}, u32[]{:S(2)}, u32[]{:S(2)}) collective-permute-start(bf16[4,48,128]{2,1,0:T(8,128)(2,1)} %get-tuple-element.18), channel_id=1, source_target_pairs={{1,16},{2,17},{3,18},{4,19},{5,20},{6,21},{7,22},{8,23},{9,24},{10... | collective-permute-start | bytes 147464 | tf_op jit(solution)/shard_map/ppermute | solution.py:578
  88.6 9.0 %collective-permute-done.6.high_l = bf16[4,48,128]{2,1,0:T(8,128)(2,1)S(1)} collective-permute-done((bf16[4,48,128]{2,1,0:T(8,128)(2,1)}, bf16[4,48,128]{2,1,0:T(8,128)(2,1)S(1)}, u32[]{:S(2)}, u32[]{:S(2)}) %collective-permute-start.6) | collective-permute-done | bytes 49184 | tf_op jit(solution)/shard_map/ppermute | solution.py:578
  97.7 2.1 %collective-permute-start.7 = (bf16[4,48,128]{2,1,0:T(8,128)(2,1)}, bf16[4,48,128]{2,1,0:T(8,128)(2,1)S(1)}, u32[]{:S(2)}, u32[]{:S(2)}) collective-permute-start(bf16[4,48,128]{2,1,0:T(8,128)(2,1)} %get-tuple-element.19), channel_id=1, source_target_pairs={{1,112},{2,113},{3,114},{4,115},{5,116},{6,117},{7,118},{8,119},{9... | collective-permute-start | bytes 147464 | tf_op jit(solution)/shard_map/ppermute | solution.py:578
  100.5 0.7 copy.30.trig
  101.2 12.4 %transfer_table.1.table = bf16[320,2,16,128]{3,2,1,0:T(8,128)(2,1)} custom-call(bf16[2,16,64,316]{3,2,1,0:T(8,128)(2,1)} %bitcast.20), custom_call_target="tpu_custom_call" | custom-call | tf_op jit(solution)/shard_map/transfer_table/pallas_call | solution.py:222
  113.6 2.8 %stencils.1 = (bf16[2,256,224]{2,1,0:T(8,128)(2,1)}, bf16[8,512,256]{2,1,0:T(8,128)(2,1)}) custom-call(s32[32,4]{1,0:T(8,128)} %iota_add_fusion.tap_u, f32[32,4]{1,0:T(8,128)} %convert_element_type.37.weight_u, f32[32,2]{1,0:T(8,128)} %copy.30.trig, s32[4,128]{1,0:T(4,128)} %add_select_fusion.tap_v, f32[4,128]{1,0:T(4,128)} %convert_bitcast_fusion.weight_v, ...), custom_call_target="tpu_custom_call" | custom-call | tf_op jit(solution)/shard_map/stencils/pallas_call | solution.py:401
  116.3 42.4 %translate5.1 = bf16[2,16,64,512]{3,2,1,0:T(8,128)(2,1)} custom-call(s32[16,512]{1,0:T(8,128)} %maximum_bitcast_fusion.src, s32[16,512]{1,0:T(8,128)} %compare_select_fusion.off, bf16[512,16,128]{2,1,0:T(8,128)(2,1)} %bitcast.16, bf16[320,2,16,128]{3,2,1,0:T(8,128)(2,1)} %transfer_table.1.table), custom_call_target="tpu_custom_call" | custom-call | tf_op jit(solution)/shard_map/translate5/pallas_call | solution.py:276
  159.8 17.0 %top_level.1 = bf16[64,2,32,128]{3,2,1,0:T(8,128)(2,1)} custom-call(s32[16,64]{1,0:T(8,128)} %maximum_bitcast_fusion.1.src, s32[16,64]{1,0:T(8,128)} %compare_select_fusion.1.off, bf16[64,128,128]{2,1,0:T(8,128)(2,1)} %bitcast.17, bf16[8,128,128]{2,1,0:T(8,128)(2,1)} %copy-done.4, bf16[8,128,128]{2,1,0:T(8,128)(2,1)} %copy-done.5, ...), custom_call_target="tpu_custom_call" | custom-call | tf_op jit(solution)/shard_map/top_level/pallas_call | solution.py:494
  (48 shorter events, 5.4 us)
Async XLA Ops:
  0.6 87.9 %copy-start = (bf16[512,4]{0,1:T(4,128)(2,1)S(1)}, bf16[512,4]{0,1:T(4,128)(2,1)}, u32[]{:S(2)}) copy-start(bf16[512,4]{0,1:T(4,128)(2,1)} %param.30) | copy-start | bytes 12292
  18.7 13.9 %copy-start.12 = (s32[64,16]{0,1:T(8,128)S(1)}, s32[64,16]{0,1:T(8,128)}, u32[]{:S(2)}) copy-start(s32[64,16]{0,1:T(8,128)} %param.37) | copy-start | bytes 12292
  18.7 14.5 %copy-start.13 = (s32[64,16]{0,1:T(8,128)S(1)}, s32[64,16]{0,1:T(8,128)}, u32[]{:S(2)}) copy-start(s32[64,16]{0,1:T(8,128)} %param.38) | copy-start | bytes 12292
  18.7 15.8 %copy-start.10 = (s32[512,16]{0,1:T(8,128)S(1)}, s32[512,16]{0,1:T(8,128)}, u32[]{:S(2)}) copy-start(s32[512,16]{0,1:T(8,128)} %param.34) | copy-start | bytes 98308
  18.8 16.4 %copy-start.11 = (s32[512,16]{0,1:T(8,128)S(1)}, s32[512,16]{0,1:T(8,128)}, u32[]{:S(2)}) copy-start(s32[512,16]{0,1:T(8,128)} %param.35) | copy-start | bytes 98308
  18.8 39.7 %all-to-all-start = ((bf16[128,4,16,128]{3,2,1,0:T(8,128)(2,1)}), bf16[128,4,16,128]{3,2,1,0:T(8,128)(2,1)S(1)}, u32[]{:S(2)}, u32[]{:S(2)}) async-start(bf16[128,4,16,128]{3,2,1,0:T(8,128)(2,1)} %aggregate.1), calls=%async_computation | async-start | bytes 4194304 | tf_op jit(solution)/shard_map/all_to_all | solution.py:533
  58.5 1.4 copy-start.1
  63.8 19.1 %collective-permute-start.4 = (bf16[4,48,128]{2,1,0:T(8,128)(2,1)}, bf16[4,48,128]{2,1,0:T(8,128)(2,1)S(1)}, u32[]{:S(2)}, u32[]{:S(2)}) collective-permute-start(bf16[4,48,128]{2,1,0:T(8,128)(2,1)} %get-tuple-element.16), channel_id=1, source_target_pairs={{0,17},{1,18},{2,19},{3,20},{4,21},{5,22},{6,23},{7,24},{8,25},{9,... | collective-permute-start | bytes 147464 | tf_op jit(solution)/shard_map/ppermute | solution.py:578
  68.1 90.6 %collective-permute-start.2 = (bf16[32,48,128]{2,1,0:T(8,128)(2,1)}, bf16[32,48,128]{2,1,0:T(8,128)(2,1)S(1)}, u32[]{:S(2)}, u32[]{:S(2)}) collective-permute-start(bf16[32,48,128]{2,1,0:T(8,128)(2,1)} %get-tuple-element.14), channel_id=1, source_target_pairs={{0,1},{1,2},{2,3},{3,4},{4,5},{5,6},{6,7},{7,8},{8,9},{9,10},{10,1... | collective-permute-start | bytes 1179656 | tf_op jit(solution)/shard_map/ppermute | solution.py:578
  71.0 87.8 %collective-permute-start.3 = (bf16[32,48,128]{2,1,0:T(8,128)(2,1)}, bf16[32,48,128]{2,1,0:T(8,128)(2,1)S(1)}, u32[]{:S(2)}, u32[]{:S(2)}) collective-permute-start(bf16[32,48,128]{2,1,0:T(8,128)(2,1)} %get-tuple-element.15), channel_id=1, source_target_pairs={{1,0},{2,1},{3,2},{4,3},{5,4},{6,5},{7,6},{8,7},{9,8},{10,9},{11,1... | collective-permute-start | bytes 1179656 | tf_op jit(solution)/shard_map/ppermute | solution.py:578
  74.2 12.4 %collective-permute-start.5 = (bf16[4,48,128]{2,1,0:T(8,128)(2,1)}, bf16[4,48,128]{2,1,0:T(8,128)(2,1)S(1)}, u32[]{:S(2)}, u32[]{:S(2)}) collective-permute-start(bf16[4,48,128]{2,1,0:T(8,128)(2,1)} %get-tuple-element.17), channel_id=1, source_target_pairs={{0,113},{1,114},{2,115},{3,116},{4,117},{5,118},{6,119},{7,120},{8... | collective-permute-start | bytes 147464 | tf_op jit(solution)/shard_map/ppermute | solution.py:578
  82.8 75.8 %collective-permute-start = (bf16[8,128,128]{2,1,0:T(8,128)(2,1)}, bf16[8,128,128]{2,1,0:T(8,128)(2,1)S(1)}, u32[]{:S(2)}, u32[]{:S(2)}) collective-permute-start(bf16[8,128,128]{2,1,0:T(8,128)(2,1)} %get-tuple-element.12), channel_id=1, source_target_pairs={{0,16},{1,17},{2,18},{3,19},{4,20},{5,21},{6,22},{7,23},{8,24},{9,... | collective-permute-start | bytes 786440 | tf_op jit(solution)/shard_map/ppermute | solution.py:578
  82.9 30.6 %copy-start.6 = (bf16[4,48,128]{2,1,0:T(8,128)(2,1)}, bf16[4,48,128]{2,1,0:T(8,128)(2,1)S(1)}, u32[]{:S(2)}) copy-start(bf16[4,48,128]{2,1,0:T(8,128)(2,1)S(1)} %collective-permute-done.4.low_l) | copy-start | bytes 147460
  83.0 75.7 %collective-permute-start.1 = (bf16[8,128,128]{2,1,0:T(8,128)(2,1)}, bf16[8,128,128]{2,1,0:T(8,128)(2,1)S(1)}, u32[]{:S(2)}, u32[]{:S(2)}) collective-permute-start(bf16[8,128,128]{2,1,0:T(8,128)(2,1)} %get-tuple-element.13), channel_id=1, source_target_pairs={{0,112},{1,113},{2,114},{3,115},{4,116},{5,117},{6,118},{7,119},{8... | collective-permute-start | bytes 786440 | tf_op jit(solution)/shard_map/ppermute | solution.py:578
  86.6 26.9 %copy-start.7 = (bf16[4,48,128]{2,1,0:T(8,128)(2,1)}, bf16[4,48,128]{2,1,0:T(8,128)(2,1)S(1)}, u32[]{:S(2)}) copy-start(bf16[4,48,128]{2,1,0:T(8,128)(2,1)S(1)} %collective-permute-done.5.low_r) | copy-start | bytes 147460
  86.6 11.0 %collective-permute-start.6 = (bf16[4,48,128]{2,1,0:T(8,128)(2,1)}, bf16[4,48,128]{2,1,0:T(8,128)(2,1)S(1)}, u32[]{:S(2)}, u32[]{:S(2)}) collective-permute-start(bf16[4,48,128]{2,1,0:T(8,128)(2,1)} %get-tuple-element.18), channel_id=1, source_target_pairs={{1,16},{2,17},{3,18},{4,19},{5,20},{6,21},{7,22},{8,23},{9,24},{10... | collective-permute-start | bytes 147464 | tf_op jit(solution)/shard_map/ppermute | solution.py:578
  97.7 15.9 %copy-start.8 = (bf16[4,48,128]{2,1,0:T(8,128)(2,1)}, bf16[4,48,128]{2,1,0:T(8,128)(2,1)S(1)}, u32[]{:S(2)}) copy-start(bf16[4,48,128]{2,1,0:T(8,128)(2,1)S(1)} %collective-permute-done.6.high_l) | copy-start | bytes 147460
  97.7 61.0 %collective-permute-start.7 = (bf16[4,48,128]{2,1,0:T(8,128)(2,1)}, bf16[4,48,128]{2,1,0:T(8,128)(2,1)S(1)}, u32[]{:S(2)}, u32[]{:S(2)}) collective-permute-start(bf16[4,48,128]{2,1,0:T(8,128)(2,1)} %get-tuple-element.19), channel_id=1, source_target_pairs={{1,112},{2,113},{3,114},{4,115},{5,116},{6,117},{7,118},{8,119},{9... | collective-permute-start | bytes 147464 | tf_op jit(solution)/shard_map/ppermute | solution.py:578
  158.7 0.6 copy-start.9
  158.7 0.7 copy-start.4
  158.7 0.8 copy-start.5
  158.7 0.9 copy-start.2
  158.7 1.0 copy-start.3

commit v2 on v1

--- a/solution.py
+++ b/solution.py
@@ -10,7 +10,6 @@
 
 F32 = jnp.float32
 BF16 = jnp.bfloat16
-VMEM_LIMIT = 60 * 1024 * 1024
 
 
 PAIRS = ((3, 0), (1, 2))
@@ -191,44 +190,37 @@
             pltpu.VMEM((4, 2, 2, rows6, cols6), BF16),
             pltpu.VMEM((4, 2, rows5, cols6), BF16),
         ],
-        compiler_params=pltpu.CompilerParams(vmem_limit_bytes=VMEM_LIMIT),
+        compiler_params=pltpu.CompilerParams(vmem_limit_bytes=58 * 1024 * 1024),
         name="aggregate",
     )(pat, *weights, *[jnp.asarray(a) for a in consts])
 
 
-def table_body(tr, out, spread):
+def table_body(tr, out):
     theta = pl.program_id(0)
-    entries = out.shape[0]
-    count = tr.shape[3]
-    re = tr[0, 0]
-    im = tr[1, 0]
-    stack = jnp.concatenate([re, re, im, -im], axis=0)
+    entries = out.shape[0] // 16
+    count = tr.shape[4]
+    stack = jnp.concatenate([tr[0, 0, 0], tr[0, 1, 0], tr[1, 0, 0], tr[1, 1, 0]], axis=0)
     row = lax.broadcasted_iota(jnp.int32, (entries, count), 0)
     col = lax.broadcasted_iota(jnp.int32, (entries, count), 1)
     unit = jnp.where(row == col, 1.0, 0.0).astype(BF16)
     turned = dot_t(unit, stack)
-    for j in range(2):
-        spread[j, pl.ds(theta, entries, 16), :] = turned[:, j * 128 : (j + 1) * 128]
-
-    @pl.when(theta == 15)
-    def _():
-        for j in range(2):
-            out[:, j] = spread[j].reshape(entries, 16, 128).astype(BF16)
+    out[pl.ds(theta, entries, 16), :] = turned[:, :128]
+    out[pl.ds(theta + 8, entries, 16), :] = turned[:, 128:]
 
 
 def transfer_table(transfer):
     count, _, rows, cols = transfer.shape
     entries = (count + 1 + 7) // 8 * 8
+    turned = transfer.transpose(1, 2, 3, 0).reshape(2, 2, rows // 2, cols, count)
     return pl.pallas_call(
         table_body,
-        grid=(rows,),
-        in_specs=[pl.BlockSpec((2, 1, cols, count), lambda i: (0, i, 0, 0))],
-        out_specs=pl.BlockSpec((entries, 2, rows, 2 * cols), lambda i: (0, 0, 0, 0)),
-        out_shape=jax.ShapeDtypeStruct((entries, 2, rows, 2 * cols), BF16),
-        scratch_shapes=[pltpu.VMEM((2, entries * rows, 2 * cols), F32)],
-        compiler_params=pltpu.CompilerParams(vmem_limit_bytes=VMEM_LIMIT),
+        grid=(rows // 2,),
+        in_specs=[pl.BlockSpec((2, 2, 1, cols, count), lambda i: (0, 0, i, 0, 0))],
+        out_specs=pl.BlockSpec((entries * 16, 128), lambda i: (0, 0)),
+        out_shape=jax.ShapeDtypeStruct((entries * 16, 128), F32),
+        compiler_params=pltpu.CompilerParams(vmem_limit_bytes=12 * 1024 * 1024),
         name="transfer_table",
-    )(transfer.transpose(1, 2, 3, 0))
+    )(turned)
 
 
 def tree(terms):
@@ -237,23 +229,35 @@
     return terms[0]
 
 
-def translate5_body(src, off, level, table, out, total):
+def translate5_body(src, off, level, table, out, tiles, total):
     targets, rows, lanes = level.shape
-    slots = src.shape[0]
+    slots = src.shape[0] // targets
+    low = lax.broadcasted_iota(jnp.int32, (8, lanes), 1) < lanes // 2
+
+    def widen(t, carry):
+        x = level[t].astype(F32)
+        upper, lower = x[:8], x[8:]
+        at = pl.multiple_of(t * 16, 16)
+        tiles[pl.ds(at, 8), :] = jnp.where(low, upper, pltpu.roll(lower, lanes // 2, 1))
+        tiles[pl.ds(at + 8, 8), :] = jnp.where(low, pltpu.roll(upper, lanes // 2, 1), lower)
+        return carry
+
+    lax.fori_loop(0, targets, widen, 0, unroll=16)
 
     def one(t, carry):
-        acc1 = jnp.zeros((rows, lanes), F32)
-        acc2 = jnp.zeros((rows, lanes), F32)
-        for j in range(0, slots, 4):
-            first, second = [], []
-            for i in range(4):
-                x = level[src[j + i, t]]
-                w = table.at[off[j + i, t]]
-                first.append(w[0] * x)
-                second.append(w[1] * x)
-            acc1 = acc1 + tree(first).astype(F32)
-            acc2 = acc2 + tree(second).astype(F32)
-        total[pl.ds(pl.multiple_of(t * rows, rows), rows), :] = acc1 + pltpu.roll(acc2, lanes // 2, 1)
+        terms_r, terms_i = [], []
+        for j in range(slots):
+            s = pl.multiple_of(src[t * slots + j], 16)
+            o = pl.multiple_of(off[t * slots + j], 16)
+            xr = tiles[pl.ds(s, 8), :]
+            xi = tiles[pl.ds(s + 8, 8), :]
+            wr = table[pl.ds(o, 8), :]
+            wi = table[pl.ds(o + 8, 8), :]
+            terms_r.append(wr * xr - wi * xi)
+            terms_i.append(wr * xi + wi * xr)
+        at = pl.multiple_of(t * 16, 16)
+        total[pl.ds(at, 8), :] = tree(terms_r)
+        total[pl.ds(at + 8, 8), :] = tree(terms_i)
         return carry
 
     lax.fori_loop(0, targets, one, 0, unroll=2)
@@ -263,10 +267,10 @@
         1.0,
         0.0,
     ).astype(BF16)
-    for theta in range(rows):
-        turned = dot_t(unit, total[pl.ds(theta, targets, rows), :].astype(BF16)).astype(BF16)
-        out[0, theta] = turned[: lanes // 2]
-        out[1, theta] = turned[lanes // 2 :]
+    for row in range(16):
+        turned = dot_t(unit, total[pl.ds(row, targets, 16), :].astype(BF16)).astype(BF16)
+        out[row // 8, row % 8] = turned[: lanes // 2]
+        out[row // 8, row % 8 + 8] = turned[lanes // 2 :]
 
 
 def translate5(level, table, sources, offsets):
@@ -278,8 +282,11 @@
         in_specs=[smem, smem, vmem, vmem],
         out_specs=vmem,
         out_shape=jax.ShapeDtypeStruct((2, rows, lanes // 2, targets), BF16),
-        scratch_shapes=[pltpu.VMEM((targets * rows, lanes), F32)],
-        compiler_params=pltpu.CompilerParams(vmem_limit_bytes=VMEM_LIMIT),
+        scratch_shapes=[
+            pltpu.VMEM((targets * 16, lanes), F32),
+            pltpu.VMEM((targets * 16, lanes), F32),
+        ],
+        compiler_params=pltpu.CompilerParams(vmem_limit_bytes=24 * 1024 * 1024),
         name="translate5",
     )(sources, offsets, level, table)
     return turned.transpose(3, 0, 1, 2)
@@ -294,7 +301,7 @@
     return pick
 
 
-def edges_body(level, pick, right, left, last, first, last_r, first_r, last_l, first_l):
+def edges_body(level, pick, right, left, last, first):
     lane = lax.broadcasted_iota(jnp.int32, (1024, 256), 0)
     col = lax.broadcasted_iota(jnp.int32, (1024, 256), 1)
     side = col >> 7
@@ -315,16 +322,15 @@
         right[g] = both[:, :128]
         left[g] = both[:, 128:]
 
-    def rows_of(source, count, low, high):
-        for i in range(count):
-            rhs = jnp.concatenate([source[2 * i], source[2 * i + 1]], axis=0)
-            both = dot(pick[...], rhs).astype(BF16)
-            low[i] = both[:48]
-            high[i] = both[48:]
-
-    rows_of(level, 32, last, first)
-    rows_of(right, 4, last_r, first_r)
-    rows_of(left, 4, last_l, first_l)
+    edge_rows(level, pick, last, first)
+
+
+def edge_rows(source, pick, last, first):
+    for i in range(last.shape[0]):
+        rhs = jnp.concatenate([source[2 * i], source[2 * i + 1]], axis=0)
+        both = dot(pick[...], rhs).astype(BF16)
+        last[i] = both[:48]
+        first[i] = both[48:]
 
 
 def edges(level):
@@ -332,10 +338,27 @@
     pick = jnp.asarray(edge_picks(), BF16)
     return pl.pallas_call(
         edges_body,
-        out_shape=(shape(8, 128, 128),) * 2 + (shape(32, 48, 128),) * 2 + (shape(4, 48, 128),) * 4,
-        compiler_params=pltpu.CompilerParams(vmem_limit_bytes=VMEM_LIMIT),
+        out_shape=(shape(8, 128, 128),) * 2 + (shape(32, 48, 128),) * 2,
+        compiler_params=pltpu.CompilerParams(vmem_limit_bytes=10 * 1024 * 1024),
         name="edges",
     )(level, pick)
+
+
+def corners_body(from_left, from_right, pick, sides, last, first):
+    for g in range(sides.shape[0]):
+        sides[g] = from_left[g] + from_right[g]
+    edge_rows(sides, pick, last, first)
+
+
+def corners(from_left, from_right):
+    shape = lambda *s: jax.ShapeDtypeStruct(s, BF16)
+    pick = jnp.asarray(edge_picks(), BF16)
+    return pl.pallas_call(
+        corners_body,
+        out_shape=(shape(8, 128, 128),) + (shape(4, 48, 128),) * 2,
+        compiler_params=pltpu.CompilerParams(vmem_limit_bytes=4 * 1024 * 1024),
+        name="corners",
+    )(from_left, from_right, pick)
 
 
 def stencil_maps():
@@ -404,34 +427,36 @@
             jax.ShapeDtypeStruct((2, 8 * rows, 224), BF16),
             jax.ShapeDtypeStruct((8, 512, 256), BF16),
         ),
-        compiler_params=pltpu.CompilerParams(vmem_limit_bytes=VMEM_LIMIT),
+        compiler_params=pltpu.CompilerParams(vmem_limit_bytes=8 * 1024 * 1024),
         name="stencils",
     )(tap_u, weight_u, trig, tap_v, weight_v, jnp.asarray(ext), jnp.asarray(factor))
 
 
+def theta_stage(level, low, high, polar, half):
+    for i in range(low.shape[0]):
+        for parity in range(2):
+            rhs = jnp.concatenate([level[2 * i + parity], low[i], high[i]], axis=0)
+            half[2 * i + parity] = dot(polar[parity], rhs).astype(BF16)
+
+
+def theta_level(level, low, high, polar):
+    parents = level.shape[0]
+    return pl.pallas_call(
+        theta_stage,
+        out_shape=jax.ShapeDtypeStruct((parents, polar.shape[1], level.shape[2]), BF16),
+        compiler_params=pltpu.CompilerParams(vmem_limit_bytes=14 * 1024 * 1024),
+        name="theta_level",
+    )(level, low, high, polar)
+
+
 def top_body(
-    src, off, level, from_left, from_right, low, high, low_l, low_r, high_l, high_r, polar, azimuth,
-    tab, transfer, out, table, half, level4, sem,
+    src, off, half, sides, low, high, polar, azimuth, tab, transfer, out, table, side_half, level4, sem
 ):
     count = transfer.shape[0]
     fetch = pltpu.make_async_copy(transfer, table.at[pl.ds(0, count)], sem)
     fetch.start()
     table[count] = jnp.zeros(table.shape[1:], BF16)
-
-    def theta_stage(i, carry):
-        for parity in range(2):
-            rhs = jnp.concatenate([level[2 * i + parity], low[i], high[i]], axis=0)
-            half[2 * i + parity] = dot(polar[parity], rhs).astype(BF16)
-        return carry
-
-    lax.fori_loop(0, 32, theta_stage, 0, unroll=4)
-    for i in range(4):
-        rows_low = low_l[i] + low_r[i]
-        rows_high = high_l[i] + high_r[i]
-        for parity in range(2):
-            g = 2 * i + parity
-            rhs = jnp.concatenate([from_left[g] + from_right[g], rows_low, rows_high], axis=0)
-            half[64 + g] = dot(polar[parity], rhs).astype(BF16)
+    theta_stage(sides, low, high, polar, side_half)
 
     def phi_stage(place, carry):
         rows = []
@@ -441,7 +466,7 @@
                 b = slice(64 * x + 32, 64 * x + 64)
                 p = 8 * g + place
                 rows.append(
-                    jnp.concatenate([half[p, a], half[p, b], half[64 + g, a], half[64 + g, b]], axis=1)
+                    jnp.concatenate([half[p, a], half[p, b], side_half[g, a], side_half[g, b]], axis=1)
                 )
         y = dot(jnp.concatenate(rows, axis=0), azimuth[place])
         for g in range(8):
@@ -457,54 +482,62 @@
                 dr = c * pr - s * qi
                 di = c * pi + s * qr
                 re, im = (dr, di) if q == 0 else (re + dr, im + di)
-            level4[8 * g + place, 0] = re.astype(BF16)
-            level4[8 * g + place, 1] = im.astype(BF16)
+            at = pl.multiple_of((8 * g + place) * 64, 64)
+            level4[pl.ds(at, 32), :] = re
+            level4[pl.ds(at + 32, 32), :] = im
         return carry
 
     lax.fori_loop(0, 8, phi_stage, 0)
     fetch.wait()
-    slots = src.shape[0]
+    targets = out.shape[0]
+    slots = src.shape[0] // targets
 
     def one(t, carry):
-        re = jnp.zeros((32, 128), F32)
-        im = jnp.zeros((32, 128), F32)
-        for j in range(0, slots, 2):
-            terms_r, terms_i = [], []
-            for i in range(2):
-                x = level4.at[src[j + i, t]]
-                w = table.at[off[j + i, t]]
-                xr, xi = x[0], x[1]
-                wr, wi = w[0], w[1]
-                terms_r.append(wr * xr - wi * xi)
-                terms_i.append(wr * xi + wi * xr)
-            re = re + tree(terms_r).astype(F32)
-            im = im + tree(terms_i).astype(F32)
-        out[t, 0] = re.astype(BF16)
-        out[t, 1] = im.astype(BF16)
+        re = [jnp.zeros((8, 128), F32)] * 4
+        im = [jnp.zeros((8, 128), F32)] * 4
+        for j in range(slots):
+            at = pl.multiple_of(src[t * slots + j], 64)
+            w = table.at[off[t * slots + j]]
+            for r in range(4):
+                xr = level4[pl.ds(at + 8 * r, 8), :]
+                xi = level4[pl.ds(at + 32 + 8 * r, 8), :]
+                wr = w[0, 8 * r : 8 * r + 8].astype(F32)
+                wi = w[1, 8 * r : 8 * r + 8].astype(F32)
+                re[r] = re[r] + (wr * xr - wi * xi)
+                im[r] = im[r] + (wr * xi + wi * xr)
+        for r in range(4):
+            out[t, 0, 8 * r : 8 * r + 8] = re[r].astype(BF16)
+            out[t, 1, 8 * r : 8 * r + 8] = im[r].astype(BF16)
         return carry
 
-    lax.fori_loop(0, out.shape[0], one, 0)
-
-
-def top_level(level, halos, polar, azimuth, tab, transfer, sources, offsets):
+    lax.fori_loop(0, targets, one, 0)
+
+
+def top_level(half, sides, low, high, polar, azimuth, tab, transfer, sources, offsets):
     count, _, rows, cols = transfer.shape
     smem = pl.BlockSpec(memory_space=pltpu.SMEM)
     vmem = pl.BlockSpec(memory_space=pltpu.VMEM)
-    parents = level.shape[0]
+    parents = half.shape[0]
     return pl.pallas_call(
         top_body,
-        in_specs=[smem, smem] + [vmem] * 12 + [pl.BlockSpec(memory_space=pl.ANY)],
+        in_specs=[smem, smem] + [vmem] * 7 + [pl.BlockSpec(memory_space=pl.ANY)],
         out_specs=vmem,
         out_shape=jax.ShapeDtypeStruct((parents, 2, rows, cols), BF16),
         scratch_shapes=[
             pltpu.VMEM((count + 1, 2, rows, cols), BF16),
-            pltpu.VMEM((72, 256, 128), BF16),
-            pltpu.VMEM((parents, 2, rows, cols), BF16),
+            pltpu.VMEM((sides.shape[0],) + half.shape[1:], BF16),
+            pltpu.VMEM((parents * 2 * rows, cols), F32),
             pltpu.SemaphoreType.DMA,
         ],
-        compiler_params=pltpu.CompilerParams(vmem_limit_bytes=VMEM_LIMIT),
+        compiler_params=pltpu.CompilerParams(vmem_limit_bytes=24 * 1024 * 1024),
         name="top_level",
-    )(sources, offsets, level, *halos, polar, azimuth, tab, transfer)
+    )(sources, offsets, half, sides, low, high, polar, azimuth, tab, transfer)
+
+
+def flat_lists(sources, offsets, dead, source_rows, factor_rows):
+    src = jnp.maximum(sources, 0) * source_rows
+    off = jnp.where(offsets < 0, dead, offsets) * factor_rows
+    return src.reshape(-1), off.reshape(-1)
 
 
 def shards(
@@ -535,10 +568,8 @@
     count5 = transfer5.shape[0]
     count4 = transfer4.shape[0]
     table5 = transfer_table(transfer5)
-    src5 = jnp.maximum(sources5.T, 0)
-    off5 = jnp.where(offsets5.T < 0, count5, offsets5.T)
-    src4 = jnp.maximum(sources4.T, 0)
-    off4 = jnp.where(offsets4.T < 0, count4, offsets4.T)
+    src5, off5 = flat_lists(sources5, offsets5, count5, 16, 16)
+    src4, off4 = flat_lists(sources4, offsets4, count4, 64, 1)
     rows4 = polar_first.shape[0]
     cols4 = azimuth_first.shape[0]
     band_rows = rows4 // bands
@@ -564,31 +595,29 @@
     f1 = scale * (x - y)
     tab = jnp.stack([jnp.cos(f0), jnp.sin(f0), jnp.cos(f1), jnp.sin(f1)])
     polar, azimuth = stencils(tap_u, weight_u, trig, tap_v, weight_v)
+    arrived, table5, src5, off5, src4, off4, polar, azimuth, tab = lax.optimization_barrier(
+        (arrived, table5, src5, off5, src4, off4, polar, azimuth, tab)
+    )
 
     level = arrived.reshape(64, 128, 128)
-    right, left, last, first, last_r, first_r, last_l, first_l = edges(level)
-
-    def moved(value, step_block, step_band):
-        pairs = []
-        for c in range(blocks):
-            for a in range(bands):
-                to = a + step_band
-                if 0 <= to < bands:
-                    pairs.append((c * bands + a, (c + step_block) % blocks * bands + to))
-        return lax.ppermute(value, ("clu", "ang"), pairs)
-
-    halos = (
-        moved(right, 1, 0),
-        moved(left, -1, 0),
-        moved(last, 0, 1),
-        moved(first, 0, -1),
-        moved(last_r, 1, 1),
-        moved(last_l, -1, 1),
-        moved(first_r, 1, -1),
-        moved(first_l, -1, -1),
+    right, left, last, first = edges(level)
+    around = lambda step: [(i, (i + step) % blocks) for i in range(blocks)]
+    across = lambda step: [(i, i + step) for i in range(bands) if 0 <= i + step < bands]
+    from_left = lax.ppermute(right, "clu", around(1))
+    from_right = lax.ppermute(left, "clu", around(-1))
+    low = lax.ppermute(last, "ang", across(1))
+    high = lax.ppermute(first, "ang", across(-1))
+    translated5 = translate5(arrived.reshape(512, 16, 128), table5, src5, off5)
+    from_left, from_right, translated5 = lax.optimization_barrier(
+        (from_left, from_right, translated5)
     )
-    translated5 = translate5(arrived.reshape(512, 16, 128), table5, src5, off5)
-    translated4 = top_level(level, halos, polar, azimuth, tab, transfer4, src4, off4)
+    sides, side_last, side_first = corners(from_left, from_right)
+    side_low = lax.ppermute(side_last, "ang", across(1))
+    side_high = lax.ppermute(side_first, "ang", across(-1))
+    half = theta_level(level, low, high, polar)
+    translated4 = top_level(
+        half, sides, side_low, side_high, polar, azimuth, tab, transfer4, src4, off4
+    )
     return (translated5, translated4)
 
 

time: 180 us -> 125 us (0.69); the launches traced: 177 us -> 124 us
  Pallas kernels: 95.1 us -> 58.8 us
  waiting for transfers between devices: 31.8 us -> 21.7 us
  other arithmetic: 7.35 us -> 1.94 us
  starting transfers between devices: 36.2 us -> 31.1 us
  local copies, waits for them, and re-layouts: 5.51 us -> 9.37 us
    pallas_call x1, Pallas kernels: 42.4 us -> 21.2 us  [translate5(): pl.pallas_call(translate5_body, in_specs=[smem, smem, vmem, vmem], out_sp...]
    pallas_call x2 -> x4, Pallas kernels: 29.4 us -> 18.9 us  [the longest x1 13.4 us: top_level(): pl.pallas_call(top_body, in_specs=[smem, smem] + [vmem] * 7 + [pl.BlockSp...]
    all_to_all x1, waiting for transfers between devices: 22.7 us -> 17.2 us  [shards(): lax.all_to_all(send, ('clu', 'ang'), split_axis=0, concat_axis=0, tiled=T...]
    ppermute x8 -> x6, starting transfers between devices: 25.4 us -> 20.3 us  [the longest x1 7.95 us: shards(): side_low = lax.ppermute(side_last, 'ang', across(1))]
    ppermute x8 -> x6, waiting for transfers between devices: 9.05 us -> 4.49 us  [the longest x1 4.47 us: shards(): side_high = lax.ppermute(side_first, 'ang', across(-1))]
    unnamed x30 -> x32, local copies, waits for them, and re-layouts: 3.98 us -> 7.61 us
    pallas_call x1, Pallas kernels: 3.94 us -> 1.45 us  [edges(): pl.pallas_call(edges_body, out_shape=(shape(8, 128, 128),) * 2 + (shape(3...]
    pallas_call x1, Pallas kernels: 2.76 us -> 0.59 us  [stencils(): pl.pallas_call(stencils_body, out_shape=(jax.ShapeDtypeStruct((2, 8 * row...]
  transfers between devices with their start and end apart: 9 -> 7, of which waited for: 2 -> 2; matrix products, arithmetic and copies ran while one was open for 5% -> 3% of each run, Pallas kernels for 32% -> 22%
where the time goes in v2:
time: 125 us; the launch traced here: 124 us
  Pallas kernels  58.8 us (47%)
  starting transfers between devices  31.1 us (25%)
  waiting for transfers between devices  21.7 us (17%)
  local copies, waits for them, and re-layouts  9.37 us (7%)
  other arithmetic  1.94 us (2%)
    pallas_call x1, Pallas kernels, translate5(): pl.pallas_call(translate5_body, in_specs=[smem, smem, vmem, vmem], out_sp...  21.2 us
    all_to_all x1, waiting for transfers between devices, shards(): lax.all_to_all(send, ('clu', 'ang'), split_axis=0, concat_axis=0, tiled=T...  17.2 us
    pallas_call x1, Pallas kernels, aggregate(): pl.pallas_call(aggregate_body, grid=(clusters,), in_specs=[pl.BlockSpec((...  16.7 us
    pallas_call x1, Pallas kernels, top_level(): pl.pallas_call(top_body, in_specs=[smem, smem] + [vmem] * 7 + [pl.BlockSp...  13.4 us
    all_to_all x1, starting transfers between devices, shards(): lax.all_to_all(send, ('clu', 'ang'), split_axis=0, concat_axis=0, tiled=T...  10.8 us
    ppermute x1, starting transfers between devices, shards(): side_low = lax.ppermute(side_last, 'ang', across(1))  7.95 us
    unnamed x32, local copies, waits for them, and re-layouts  7.61 us
    ppermute x1, starting transfers between devices, shards(): low = lax.ppermute(last, 'ang', across(1))  4.55 us
  transfers between devices with their start and end apart: 7, of which 2 were waited for; matrix products, arithmetic and copies ran while one was open for 3% of the time, Pallas kernels for 22%

profile of v2, /device:TPU:7, one launch (start us, length us, event | category | flops | bytes accessed | tf_op | source)
XLA Modules:
  0.0 124.0 jit_solution(15554170893430305019)
XLA Ops:
  0.6 1.4 %copy.35.a7 = bf16[128,64]{1,0:T(8,128)(2,1)} copy(bf16[128,64]{0,1:T(8,128)(2,1)} %param.26) | data formatting | bytes 32768 | tf_op args[1]
  2.1 16.7 %aggregate.1 = bf16[128,4,16,128]{3,2,1,0:T(8,128)(2,1)} custom-call(bf16[32768,128]{1,0:T(8,128)(2,1)} %bitcast.15, bf16[128,64]{1,0:T(8,128)(2,1)} %copy.35.a7, bf16[128,256]{1,0:T(8,128)(2,1)} %b7.1, bf16[256,128]{1,0:T(8,128)(2,1)} %a6.1, bf16[256,512]{1,0:T(8,128)(2,1)} %b6.1, f32[128,256]{1,0:T(8,128)} %constant.70.clone.top7, ...), custom_call_target="tpu_custom_call" | custom-call | tf_op jit(solution)/shard_map/aggregate/pallas_call | solution.py:178
  18.8 10.8 %all-to-all-start = ((bf16[128,4,16,128]{3,2,1,0:T(8,128)(2,1)}), bf16[128,4,16,128]{3,2,1,0:T(8,128)(2,1)S(1)}, u32[]{:S(2)}, u32[]{:S(2)}) async-start(bf16[128,4,16,128]{3,2,1,0:T(8,128)(2,1)} %aggregate.1), calls=%async_computation | async-start | bytes 4194304 | tf_op jit(solution)/shard_map/all_to_all | solution.py:566
  30.9 1.4 %copy-done.5 = bf16[316,2,16,64]{0,3,2,1:T(8,128)(2,1)S(1)} copy-done((bf16[316,2,16,64]{0,3,2,1:T(8,128)(2,1)S(1)}, bf16[316,2,16,64]{0,3,2,1:T(8,128)(2,1)}, u32[]{:S(2)}) %copy-start.5) | copy-done | bytes 1294360
  32.3 2.8 %transfer_table.1.table = f32[5120,128]{1,0:T(8,128)S(1)} custom-call(bf16[2,2,8,64,316]{4,3,2,1,0:T(8,128)(2,1)S(1)} %bitcast.14), custom_call_target="tpu_custom_call" | custom-call | tf_op jit(solution)/shard_map/transfer_table/pallas_call | solution.py:215
  35.2 1.5 %copy-done.1 = f32[5120,128]{1,0:T(8,128)} copy-done((f32[5120,128]{1,0:T(8,128)}, f32[5120,128]{1,0:T(8,128)S(1)}, u32[]{:S(2)}) %copy-start.1) | copy-done | bytes 2621464
  36.7 0.8 dynamic_slice.14
  37.4 0.8 subtract_add_fusion
  38.2 0.7 convert_bitcast_fusion.weight_v
  38.9 0.6 stencils.1
  39.6 1.4 %copy-done.3 = bf16[8,512,256]{2,1,0:T(8,128)(2,1)} copy-done((bf16[8,512,256]{2,1,0:T(8,128)(2,1)}, bf16[8,512,256]{2,1,0:T(8,128)(2,1)S(1)}, u32[]{:S(2)}) %copy-start.3) | copy-done | bytes 2097176
  41.2 17.2 %all-to-all-done = bf16[128,4,16,128]{3,2,1,0:T(8,128)(2,1)S(1)} async-done(((bf16[128,4,16,128]{3,2,1,0:T(8,128)(2,1)}), bf16[128,4,16,128]{3,2,1,0:T(8,128)(2,1)S(1)}, u32[]{:S(2)}, u32[]{:S(2)}) %all-to-all-start) | async-done | bytes 2097184 | tf_op jit(solution)/shard_map/all_to_all | solution.py:566
  58.5 1.4 %edges.1 = (bf16[8,128,128]{2,1,0:T(8,128)(2,1)S(1)}, bf16[8,128,128]{2,1,0:T(8,128)(2,1)S(1)}, bf16[32,48,128]{2,1,0:T(8,128)(2,1)S(1)}, bf16[32,48,128]{2,1,0:T(8,128)(2,1)S(1)}) custom-call(bf16[64,128,128]{2,1,0:T(8,128)(2,1)S(1)} %bitcast.9, bf16[96,256]{1,0:T(8,128)(2,1)S(1)} %copy-done.6), custom_call_target="tpu_custom_call" | custom-call | tf_op jit(solution)/shard_map/edges/pallas_call | solution.py:339
  59.9 4.5 %collective-permute-start.2 = (bf16[32,48,128]{2,1,0:T(8,128)(2,1)S(1)}, bf16[32,48,128]{2,1,0:T(8,128)(2,1)S(1)}, u32[]{:S(2)}, u32[]{:S(2)}) collective-permute-start(bf16[32,48,128]{2,1,0:T(8,128)(2,1)S(1)} %get-tuple-element.34), channel_id=1, source_target_pairs={{0,1},{1,2},{2,3},{3,4},{4,5},{5,6},{6,7},{7,8},{8,9},{9,10},{10,1... | collective-permute-start | bytes 1179656 | tf_op jit(solution)/shard_map/ppermute | solution.py:608
  64.5 1.9 %collective-permute-start.3 = (bf16[32,48,128]{2,1,0:T(8,128)(2,1)S(1)}, bf16[32,48,128]{2,1,0:T(8,128)(2,1)S(1)}, u32[]{:S(2)}, u32[]{:S(2)}) collective-permute-start(bf16[32,48,128]{2,1,0:T(8,128)(2,1)S(1)} %get-tuple-element.35), channel_id=1, source_target_pairs={{1,0},{2,1},{3,2},{4,3},{5,4},{6,5},{7,6},{8,7},{9,8},{10,9},{11,1... | collective-permute-start | bytes 1179656 | tf_op jit(solution)/shard_map/ppermute | solution.py:609
  66.4 0.4 collective-permute-start
  66.8 3.3 %collective-permute-start.1 = (bf16[8,128,128]{2,1,0:T(8,128)(2,1)S(1)}, bf16[8,128,128]{2,1,0:T(8,128)(2,1)S(1)}, u32[]{:S(2)}, u32[]{:S(2)}) collective-permute-start(bf16[8,128,128]{2,1,0:T(8,128)(2,1)S(1)} %get-tuple-element.27), channel_id=1, source_target_pairs={{0,112},{16,0},{32,16},{48,32},{64,48},{80,64},{96,80},{112,96},{1... | collective-permute-start | bytes 786440 | tf_op jit(solution)/shard_map/ppermute | solution.py:607
  70.1 1.7 %copy-done.2 = f32[5120,128]{1,0:T(8,128)S(1)} copy-done((f32[5120,128]{1,0:T(8,128)S(1)}, f32[5120,128]{1,0:T(8,128)}, u32[]{:S(2)}) %copy-start.2) | copy-done | bytes 2621464
  71.8 21.2 %translate5.1 = bf16[2,16,64,512]{3,2,1,0:T(8,128)(2,1)} custom-call(s32[8192]{0:T(1024)S(1)} %reshape.424.src, s32[8192]{0:T(1024)S(1)} %reshape.425.off, bf16[512,16,128]{2,1,0:T(8,128)(2,1)S(1)} %bitcast.10, f32[5120,128]{1,0:T(8,128)S(1)} %copy-done.2), custom_call_target="tpu_custom_call" | custom-call | tf_op jit(solution)/shard_map/translate5/pallas_call | solution.py:280
  93.3 7.9 %collective-permute-start.4 = (bf16[4,48,128]{2,1,0:T(8,128)(2,1)S(1)}, bf16[4,48,128]{2,1,0:T(8,128)(2,1)S(1)}, u32[]{:S(2)}, u32[]{:S(2)}) collective-permute-start(bf16[4,48,128]{2,1,0:T(8,128)(2,1)S(1)} %get-tuple-element.40), channel_id=1, source_target_pairs={{0,1},{1,2},{2,3},{3,4},{4,5},{5,6},{6,7},{7,8},{8,9},{9,10},{10,1... | collective-permute-start | bytes 147464 | tf_op jit(solution)/shard_map/ppermute | solution.py:615
  101.3 2.2 %collective-permute-start.5 = (bf16[4,48,128]{2,1,0:T(8,128)(2,1)S(1)}, bf16[4,48,128]{2,1,0:T(8,128)(2,1)S(1)}, u32[]{:S(2)}, u32[]{:S(2)}) collective-permute-start(bf16[4,48,128]{2,1,0:T(8,128)(2,1)S(1)} %get-tuple-element.41), channel_id=1, source_target_pairs={{1,0},{2,1},{3,2},{4,3},{5,4},{6,5},{7,6},{8,7},{9,8},{10,9},{11,1... | collective-permute-start | bytes 147464 | tf_op jit(solution)/shard_map/ppermute | solution.py:616
  103.5 2.4 %theta_level.1.half = bf16[64,256,128]{2,1,0:T(8,128)(2,1)S(1)} custom-call(bf16[64,128,128]{2,1,0:T(8,128)(2,1)S(1)} %bitcast.11, bf16[32,48,128]{2,1,0:T(8,128)(2,1)S(1)} %collective-permute-done.2.low, bf16[32,48,128]{2,1,0:T(8,128)(2,1)S(1)} %collective-permute-done.3.high, bf16[2,256,224]{2,1,0:T(8,128)(2,1)S(1)} %get-tuple-element.36.polar), custom_call_target="tpu_custom_call" | custom-call | tf_op jit(solution)/shard_map/theta_level/pallas_call | solution.py:444
  106.0 4.5 %collective-permute-done.5.high = bf16[4,48,128]{2,1,0:T(8,128)(2,1)S(1)} collective-permute-done((bf16[4,48,128]{2,1,0:T(8,128)(2,1)S(1)}, bf16[4,48,128]{2,1,0:T(8,128)(2,1)S(1)}, u32[]{:S(2)}, u32[]{:S(2)}) %collective-permute-start.5) | collective-permute-done | bytes 49184 | tf_op jit(solution)/shard_map/ppermute | solution.py:616
  110.4 13.4 %top_level.1 = bf16[64,2,32,128]{3,2,1,0:T(8,128)(2,1)} custom-call(s32[1024]{0:T(1024)S(1)} %reshape.426.src, s32[1024]{0:T(1024)S(1)} %reshape.427.off, bf16[64,256,128]{2,1,0:T(8,128)(2,1)S(1)} %theta_level.1.half, bf16[8,128,128]{2,1,0:T(8,128)(2,1)S(1)} %get-tuple-element.39.sides, bf16[4,48,128]{2,1,0:T(8,128)(2,1)S(1)} %collective-permute-done.4.low, ...), custom_call_target="tpu_custom_call" | custom-call | tf_op jit(solution)/shard_map/top_level/pallas_call | solution.py:521
  (57 shorter events, 1.9 us)
Async XLA Ops:
  0.6 29.0 %copy-start = (bf16[512,4]{0,1:T(4,128)(2,1)S(1)}, bf16[512,4]{0,1:T(4,128)(2,1)}, u32[]{:S(2)}) copy-start(bf16[512,4]{0,1:T(4,128)(2,1)} %param.31) | copy-start | bytes 12292
  18.7 11.2 %copy-start.11 = (s32[64,16]{0,1:T(8,128)S(1)}, s32[64,16]{0,1:T(8,128)}, u32[]{:S(2)}) copy-start(s32[64,16]{0,1:T(8,128)} %param.39) | copy-start | bytes 12292
  18.7 11.4 %copy-start.12 = (s32[64,16]{0,1:T(8,128)S(1)}, s32[64,16]{0,1:T(8,128)}, u32[]{:S(2)}) copy-start(s32[64,16]{0,1:T(8,128)} %param.38) | copy-start | bytes 12292
  18.7 11.6 %copy-start.9 = (s32[512,16]{0,1:T(8,128)S(1)}, s32[512,16]{0,1:T(8,128)}, u32[]{:S(2)}) copy-start(s32[512,16]{0,1:T(8,128)} %param.36) | copy-start | bytes 98308
  18.8 11.9 %copy-start.10 = (s32[512,16]{0,1:T(8,128)S(1)}, s32[512,16]{0,1:T(8,128)}, u32[]{:S(2)}) copy-start(s32[512,16]{0,1:T(8,128)} %param.35) | copy-start | bytes 98308
  18.8 39.7 %all-to-all-start = ((bf16[128,4,16,128]{3,2,1,0:T(8,128)(2,1)}), bf16[128,4,16,128]{3,2,1,0:T(8,128)(2,1)S(1)}, u32[]{:S(2)}, u32[]{:S(2)}) async-start(bf16[128,4,16,128]{3,2,1,0:T(8,128)(2,1)} %aggregate.1), calls=%async_computation | async-start | bytes 4194304 | tf_op jit(solution)/shard_map/all_to_all | solution.py:566
  30.9 1.4 %copy-start.5 = (bf16[316,2,16,64]{0,3,2,1:T(8,128)(2,1)S(1)}, bf16[316,2,16,64]{0,3,2,1:T(8,128)(2,1)}, u32[]{:S(2)}) copy-start(bf16[316,2,16,64]{0,3,2,1:T(8,128)(2,1)} %param.34) | copy-start | bytes 3883012
  32.3 6.6 %copy-start.7 = (f32[2,8,224]{2,1,0:T(8,128)S(1)}, f32[2,8,224]{2,1,0:T(8,128)}, u32[]{:S(2)}) copy-start(f32[2,8,224]{2,1,0:T(8,128)} %constant.77.clone.factor) | copy-start | bytes 43012
  32.3 6.6 %copy-start.8 = (s32[1,224]{1,0:T(1,128)S(1)}, s32[1,224]{1,0:T(1,128)}, u32[]{:S(2)}) copy-start(s32[1,224]{1,0:T(1,128)} %constant.76.clone.ext) | copy-start | bytes 2692
  32.3 26.2 %copy-start.6 = (bf16[96,256]{1,0:T(8,128)(2,1)S(1)}, bf16[96,256]{1,0:T(8,128)(2,1)}, u32[]{:S(2)}) copy-start(bf16[96,256]{1,0:T(8,128)(2,1)} %constant.78.clone.pick) | copy-start | bytes 147460
  35.1 1.5 %copy-start.1 = (f32[5120,128]{1,0:T(8,128)}, f32[5120,128]{1,0:T(8,128)S(1)}, u32[]{:S(2)}) copy-start(f32[5120,128]{1,0:T(8,128)S(1)} %transfer_table.1.table) | copy-start | bytes 7864324
  39.5 1.4 %copy-start.3 = (bf16[8,512,256]{2,1,0:T(8,128)(2,1)}, bf16[8,512,256]{2,1,0:T(8,128)(2,1)S(1)}, u32[]{:S(2)}) copy-start(bf16[8,512,256]{2,1,0:T(8,128)(2,1)S(1)} %get-tuple-element.42.azimuth) | copy-start | bytes 6291460
  59.9 43.6 %collective-permute-start.2 = (bf16[32,48,128]{2,1,0:T(8,128)(2,1)S(1)}, bf16[32,48,128]{2,1,0:T(8,128)(2,1)S(1)}, u32[]{:S(2)}, u32[]{:S(2)}) collective-permute-start(bf16[32,48,128]{2,1,0:T(8,128)(2,1)S(1)} %get-tuple-element.34), channel_id=1, source_target_pairs={{0,1},{1,2},{2,3},{3,4},{4,5},{5,6},{6,7},{7,8},{8,9},{9,10},{10,1... | collective-permute-start | bytes 1179656 | tf_op jit(solution)/shard_map/ppermute | solution.py:608
  64.5 39.0 %collective-permute-start.3 = (bf16[32,48,128]{2,1,0:T(8,128)(2,1)S(1)}, bf16[32,48,128]{2,1,0:T(8,128)(2,1)S(1)}, u32[]{:S(2)}, u32[]{:S(2)}) collective-permute-start(bf16[32,48,128]{2,1,0:T(8,128)(2,1)S(1)} %get-tuple-element.35), channel_id=1, source_target_pairs={{1,0},{2,1},{3,2},{4,3},{5,4},{6,5},{7,6},{8,7},{9,8},{10,9},{11,1... | collective-permute-start | bytes 1179656 | tf_op jit(solution)/shard_map/ppermute | solution.py:609
  66.4 26.6 %collective-permute-start = (bf16[8,128,128]{2,1,0:T(8,128)(2,1)S(1)}, bf16[8,128,128]{2,1,0:T(8,128)(2,1)S(1)}, u32[]{:S(2)}, u32[]{:S(2)}) collective-permute-start(bf16[8,128,128]{2,1,0:T(8,128)(2,1)S(1)} %get-tuple-element.26), channel_id=1, source_target_pairs={{0,16},{16,32},{32,48},{48,64},{64,80},{80,96},{96,112},{112,0},{1... | collective-permute-start | bytes 786440 | tf_op jit(solution)/shard_map/ppermute | solution.py:606
  66.8 26.2 %collective-permute-start.1 = (bf16[8,128,128]{2,1,0:T(8,128)(2,1)S(1)}, bf16[8,128,128]{2,1,0:T(8,128)(2,1)S(1)}, u32[]{:S(2)}, u32[]{:S(2)}) collective-permute-start(bf16[8,128,128]{2,1,0:T(8,128)(2,1)S(1)} %get-tuple-element.27), channel_id=1, source_target_pairs={{0,112},{16,0},{32,16},{48,32},{64,48},{80,64},{96,80},{112,96},{1... | collective-permute-start | bytes 786440 | tf_op jit(solution)/shard_map/ppermute | solution.py:607
  70.1 1.7 %copy-start.2 = (f32[5120,128]{1,0:T(8,128)S(1)}, f32[5120,128]{1,0:T(8,128)}, u32[]{:S(2)}) copy-start(f32[5120,128]{1,0:T(8,128)} %copy-done.1) | copy-start | bytes 7864324
  71.8 38.6 %slice-start = ((s8[5177344]{0:T(1024)(128)(4,1)}), s8[4194304]{0:T(1024)(128)(4,1)S(1)}, s32[]{:S(2)}) async-start(s8[5177344]{0:T(1024)(128)(4,1)} %bitcast.12), calls=%async_computation.1 | async-start | bytes 8388608
  93.0 17.4 %slice-start.1 = ((s8[5177344]{0:T(1024)(128)(4,1)}), s8[983040]{0:T(1024)(128)(4,1)S(1)}, s32[]{:S(2)}) async-start(s8[5177344]{0:T(1024)(128)(4,1)} %bitcast.12), calls=%async_computation.2 | async-start | bytes 1966080
  93.3 12.6 %collective-permute-start.4 = (bf16[4,48,128]{2,1,0:T(8,128)(2,1)S(1)}, bf16[4,48,128]{2,1,0:T(8,128)(2,1)S(1)}, u32[]{:S(2)}, u32[]{:S(2)}) collective-permute-start(bf16[4,48,128]{2,1,0:T(8,128)(2,1)S(1)} %get-tuple-element.40), channel_id=1, source_target_pairs={{0,1},{1,2},{2,3},{3,4},{4,5},{5,6},{6,7},{7,8},{8,9},{9,10},{10,1... | collective-permute-start | bytes 147464 | tf_op jit(solution)/shard_map/ppermute | solution.py:615
  101.3 9.2 %copy-start.4 = (bf16[8,512,256]{2,1,0:T(8,128)(2,1)S(1)}, bf16[8,512,256]{2,1,0:T(8,128)(2,1)}, u32[]{:S(2)}) copy-start(bf16[8,512,256]{2,1,0:T(8,128)(2,1)} %copy-done.3) | copy-start | bytes 6291460
  101.3 9.2 %collective-permute-start.5 = (bf16[4,48,128]{2,1,0:T(8,128)(2,1)S(1)}, bf16[4,48,128]{2,1,0:T(8,128)(2,1)S(1)}, u32[]{:S(2)}, u32[]{:S(2)}) collective-permute-start(bf16[4,48,128]{2,1,0:T(8,128)(2,1)S(1)} %get-tuple-element.41), channel_id=1, source_target_pairs={{1,0},{2,1},{3,2},{4,3},{5,4},{6,5},{7,6},{8,7},{9,8},{10,9},{11,1... | collective-permute-start | bytes 147464 | tf_op jit(solution)/shard_map/ppermute | solution.py:616

commit v3 on v2

--- a/solution.py
+++ b/solution.py
@@ -47,7 +47,7 @@
 def aggregate_body(
     pat, a7, b7, a6, b6, top7, bottom7, cz, sz, tab6, tab5, out, m7, m6, level6, mixed, half6
 ):
-    rows7, rows6, rows5 = a7.shape[1], a7.shape[0], a6.shape[0]
+    rows7, rows6, rows5 = a7.shape[0], a7.shape[1], a6.shape[0]
     cols6, cols5 = b7.shape[1], b6.shape[1]
 
     @pl.when(pl.program_id(0) == 0)
@@ -55,7 +55,9 @@
         src = lax.broadcasted_iota(jnp.int32, (rows7, 4 * rows7), 0)
         dst = lax.broadcasted_iota(jnp.int32, (rows7, 4 * rows7), 1)
         spread = jnp.where((dst & (rows7 - 1)) == src, 1.0, 0.0).astype(BF16)
-        wide = dot(a7[...], spread)
+        wide = lax.dot_general(
+            a7[...], spread, (((0,), (0,)), ((), ())), preferred_element_type=F32
+        )
         m7[0:rows6, :] = (wide * top7[...]).astype(BF16)
         m7[rows6 : 2 * rows6, :] = (wide * bottom7[...]).astype(BF16)
         base = a6[...].astype(F32)
@@ -173,7 +175,7 @@
     tab5 = np.stack([np.cos(g0), np.sin(g0)], axis=1).astype(np.float32)
     full = lambda shape: pl.BlockSpec(shape, lambda g: (0,) * len(shape))
     consts = (top7, bottom7, cz, sz, tab6, tab5)
-    weights = (polar_up7, azimuth_up7, polar_up6, azimuth_up6)
+    weights = (polar_up7.T, azimuth_up7, polar_up6, azimuth_up6)
     lines = pat.shape[0] // clusters
     return pl.pallas_call(
         aggregate_body,
@@ -225,28 +227,47 @@
 
 def tree(terms):
     while len(terms) > 1:
-        terms = [terms[i] + terms[i + 1] for i in range(0, len(terms), 2)]
+        rest = terms[len(terms) // 2 * 2 :]
+        terms = [terms[i] + terms[i + 1] for i in range(0, len(terms) - 1, 2)] + rest
     return terms[0]
 
 
-def translate5_body(src, off, level, table, out, tiles, total):
-    targets, rows, lanes = level.shape
+def by_class(order, starts, slots, group, one):
+    for index, count in enumerate(slot_classes(slots)):
+        begin, end = starts[index], starts[index + 1]
+
+        def some(i, carry, begin=begin, end=end, count=count):
+            for k in range(group):
+                one(order[jnp.minimum(begin + i * group + k, end - 1)], count)
+            return carry
+
+        lax.fori_loop(0, (end - begin + group - 1) // group, some, 0)
+
+
+def slot_classes(slots):
+    return tuple(range(slots // 2, slots + 1, 2))
+
+
+def target_classes(sources):
+    targets, slots = sources.shape
+    live = jnp.sum((sources >= 0).astype(jnp.int32), axis=1)
+    kind = sum((live > count).astype(jnp.int32) for count in slot_classes(slots)[:-1])
+    index = jnp.arange(targets, dtype=jnp.int32)
+    key = kind * targets + index
+    place = jnp.sum((key[None, :] < key[:, None]).astype(jnp.int32), axis=1)
+    order = jnp.sum(jnp.where(place[None, :] == index[:, None], index[None, :], 0), axis=1)
+    kinds = jnp.arange(len(slot_classes(slots)) + 1, dtype=jnp.int32)
+    starts = jnp.sum((kind[None, :] < kinds[:, None]).astype(jnp.int32), axis=1)
+    return order, starts
+
+
+def translate_targets(src, off, order, starts, tiles, table, total, out):
+    targets, lanes = order.shape[0], tiles.shape[1]
     slots = src.shape[0] // targets
-    low = lax.broadcasted_iota(jnp.int32, (8, lanes), 1) < lanes // 2
-
-    def widen(t, carry):
-        x = level[t].astype(F32)
-        upper, lower = x[:8], x[8:]
-        at = pl.multiple_of(t * 16, 16)
-        tiles[pl.ds(at, 8), :] = jnp.where(low, upper, pltpu.roll(lower, lanes // 2, 1))
-        tiles[pl.ds(at + 8, 8), :] = jnp.where(low, pltpu.roll(upper, lanes // 2, 1), lower)
-        return carry
-
-    lax.fori_loop(0, targets, widen, 0, unroll=16)
-
-    def one(t, carry):
+
+    def one(t, count):
         terms_r, terms_i = [], []
-        for j in range(slots):
+        for j in range(count):
             s = pl.multiple_of(src[t * slots + j], 16)
             o = pl.multiple_of(off[t * slots + j], 16)
             xr = tiles[pl.ds(s, 8), :]
@@ -258,9 +279,8 @@
         at = pl.multiple_of(t * 16, 16)
         total[pl.ds(at, 8), :] = tree(terms_r)
         total[pl.ds(at + 8, 8), :] = tree(terms_i)
-        return carry
-
-    lax.fori_loop(0, targets, one, 0, unroll=2)
+
+    by_class(order, starts, slots, 4, one)
     unit = jnp.where(
         lax.broadcasted_iota(jnp.int32, (lanes, lanes), 0)
         == lax.broadcasted_iota(jnp.int32, (lanes, lanes), 1),
@@ -273,22 +293,77 @@
         out[row // 8, row % 8 + 8] = turned[lanes // 2 :]
 
 
-def translate5(level, table, sources, offsets):
-    targets, rows, lanes = level.shape
-    smem = pl.BlockSpec(memory_space=pltpu.SMEM)
-    vmem = pl.BlockSpec(memory_space=pltpu.VMEM)
+def first_targets_body(src, off, order, starts, level, table_from, out, tiles, table, total, sem):
+    clusters, rows, lanes = level.shape
+    low = lax.broadcasted_iota(jnp.int32, (8, lanes), 1) < lanes // 2
+    fetch = pltpu.make_async_copy(table_from, table, sem)
+    fetch.start()
+
+    def widen(t, carry):
+        x = level[t].astype(F32)
+        upper, lower = x[:8], x[8:]
+        at = pl.multiple_of(t * 16, 16)
+        tiles[pl.ds(at, 8), :] = jnp.where(low, upper, pltpu.roll(lower, lanes // 2, 1))
+        tiles[pl.ds(at + 8, 8), :] = jnp.where(low, pltpu.roll(upper, lanes // 2, 1), lower)
+        return carry
+
+    lax.fori_loop(0, clusters, widen, 0, unroll=16)
+    fetch.wait()
+    translate_targets(src, off, order, starts, tiles, table, total, out)
+
+
+def last_targets_body(
+    src, off, order, starts, tiles, table, before, out, total, turned, sem_before, sem_after
+):
+    targets = order.shape[0]
+    pass_on = pltpu.make_async_copy(before, out.at[:, :, :, pl.ds(0, targets)], sem_before)
+    pass_on.start()
+    translate_targets(src, off, order, starts, tiles, table, total, turned)
+    finish = pltpu.make_async_copy(turned, out.at[:, :, :, pl.ds(targets, targets)], sem_after)
+    finish.start()
+    finish.wait()
+    pass_on.wait()
+
+
+SMEM_SPEC = pl.BlockSpec(memory_space=pltpu.SMEM)
+VMEM_SPEC = pl.BlockSpec(memory_space=pltpu.VMEM)
+ANY_SPEC = pl.BlockSpec(memory_space=pl.ANY)
+
+
+def translate_first(level, table, lists):
+    clusters, rows, lanes = level.shape
+    targets = lists[2].shape[0]
+    return pl.pallas_call(
+        first_targets_body,
+        in_specs=[SMEM_SPEC] * 4 + [VMEM_SPEC, pl.BlockSpec(memory_space=pltpu.HBM)],
+        out_specs=(VMEM_SPEC,) * 3,
+        out_shape=(
+            jax.ShapeDtypeStruct((2, rows, lanes // 2, targets), BF16),
+            jax.ShapeDtypeStruct((clusters * 16, lanes), F32),
+            jax.ShapeDtypeStruct(table.shape, F32),
+        ),
+        scratch_shapes=[pltpu.VMEM((targets * 16, lanes), F32), pltpu.SemaphoreType.DMA],
+        compiler_params=pltpu.CompilerParams(vmem_limit_bytes=20 * 1024 * 1024),
+        name="translate_first",
+    )(*lists, level, table)
+
+
+def translate_last(tiles, table, before, lists):
+    parts, rows, half, targets = before.shape
     turned = pl.pallas_call(
-        translate5_body,
-        in_specs=[smem, smem, vmem, vmem],
-        out_specs=vmem,
-        out_shape=jax.ShapeDtypeStruct((2, rows, lanes // 2, targets), BF16),
+        last_targets_body,
+        in_specs=[SMEM_SPEC] * 4 + [VMEM_SPEC] * 3,
+        out_specs=ANY_SPEC,
+        out_shape=jax.ShapeDtypeStruct((parts, rows, half, 2 * targets), BF16),
         scratch_shapes=[
-            pltpu.VMEM((targets * 16, lanes), F32),
-            pltpu.VMEM((targets * 16, lanes), F32),
+            pltpu.VMEM((targets * 16, tiles.shape[1]), F32),
+            pltpu.VMEM(before.shape, BF16),
+            pltpu.SemaphoreType.DMA,
+            pltpu.SemaphoreType.DMA,
         ],
-        compiler_params=pltpu.CompilerParams(vmem_limit_bytes=24 * 1024 * 1024),
-        name="translate5",
-    )(sources, offsets, level, table)
+        compiler_params=pltpu.CompilerParams(vmem_limit_bytes=20 * 1024 * 1024),
+        name="translate_last",
+    )(*lists, tiles, table, before)
     return turned.transpose(3, 0, 1, 2)
 
 
@@ -301,7 +376,7 @@
     return pick
 
 
-def edges_body(level, pick, right, left, last, first):
+def edge_columns_body(level, right, left):
     lane = lax.broadcasted_iota(jnp.int32, (1024, 256), 0)
     col = lax.broadcasted_iota(jnp.int32, (1024, 256), 1)
     side = col >> 7
@@ -322,43 +397,36 @@
         right[g] = both[:, :128]
         left[g] = both[:, 128:]
 
-    edge_rows(level, pick, last, first)
-
-
-def edge_rows(source, pick, last, first):
+
+def edge_columns(level):
+    return pl.pallas_call(
+        edge_columns_body,
+        out_shape=(jax.ShapeDtypeStruct((8, 128, 128), BF16),) * 2,
+        compiler_params=pltpu.CompilerParams(vmem_limit_bytes=10 * 1024 * 1024),
+        name="edge_columns",
+    )(level)
+
+
+def edge_rows_body(level, from_left, from_right, pick, sides, last, first):
+    for g in range(sides.shape[0]):
+        sides[g] = from_left[g] + from_right[g]
+    own = level.shape[0] // 2
     for i in range(last.shape[0]):
-        rhs = jnp.concatenate([source[2 * i], source[2 * i + 1]], axis=0)
-        both = dot(pick[...], rhs).astype(BF16)
+        source, at = (level, 2 * i) if i < own else (sides, 2 * (i - own))
+        both = dot(pick[...], jnp.concatenate([source[at], source[at + 1]], axis=0)).astype(BF16)
         last[i] = both[:48]
         first[i] = both[48:]
 
 
-def edges(level):
-    shape = lambda *s: jax.ShapeDtypeStruct(s, BF16)
-    pick = jnp.asarray(edge_picks(), BF16)
+def edge_rows(level, from_left, from_right):
+    pairs = (level.shape[0] + from_left.shape[0]) // 2
     return pl.pallas_call(
-        edges_body,
-        out_shape=(shape(8, 128, 128),) * 2 + (shape(32, 48, 128),) * 2,
-        compiler_params=pltpu.CompilerParams(vmem_limit_bytes=10 * 1024 * 1024),
-        name="edges",
-    )(level, pick)
-
-
-def corners_body(from_left, from_right, pick, sides, last, first):
-    for g in range(sides.shape[0]):
-        sides[g] = from_left[g] + from_right[g]
-    edge_rows(sides, pick, last, first)
-
-
-def corners(from_left, from_right):
-    shape = lambda *s: jax.ShapeDtypeStruct(s, BF16)
-    pick = jnp.asarray(edge_picks(), BF16)
-    return pl.pallas_call(
-        corners_body,
-        out_shape=(shape(8, 128, 128),) + (shape(4, 48, 128),) * 2,
-        compiler_params=pltpu.CompilerParams(vmem_limit_bytes=4 * 1024 * 1024),
-        name="corners",
-    )(from_left, from_right, pick)
+        edge_rows_body,
+        out_shape=(jax.ShapeDtypeStruct(from_left.shape, BF16),)
+        + (jax.ShapeDtypeStruct((pairs, 48, 128), BF16),) * 2,
+        compiler_params=pltpu.CompilerParams(vmem_limit_bytes=8 * 1024 * 1024),
+        name="edge_rows",
+    )(level, from_left, from_right, jnp.asarray(edge_picks(), BF16))
 
 
 def stencil_maps():
@@ -432,31 +500,23 @@
     )(tap_u, weight_u, trig, tap_v, weight_v, jnp.asarray(ext), jnp.asarray(factor))
 
 
-def theta_stage(level, low, high, polar, half):
-    for i in range(low.shape[0]):
+def theta_stage(level, low, high, at, polar, half):
+    for i in range(level.shape[0] // 2):
         for parity in range(2):
-            rhs = jnp.concatenate([level[2 * i + parity], low[i], high[i]], axis=0)
+            rhs = jnp.concatenate([level[2 * i + parity], low[at + i], high[at + i]], axis=0)
             half[2 * i + parity] = dot(polar[parity], rhs).astype(BF16)
 
 
-def theta_level(level, low, high, polar):
-    parents = level.shape[0]
-    return pl.pallas_call(
-        theta_stage,
-        out_shape=jax.ShapeDtypeStruct((parents, polar.shape[1], level.shape[2]), BF16),
-        compiler_params=pltpu.CompilerParams(vmem_limit_bytes=14 * 1024 * 1024),
-        name="theta_level",
-    )(level, low, high, polar)
-
-
 def top_body(
-    src, off, half, sides, low, high, polar, azimuth, tab, transfer, out, table, side_half, level4, sem
+    src, off, order, starts, level, sides, low, high, polar, azimuth, tab, transfer, out,
+    table, half, side_half, level4, sem,
 ):
     count = transfer.shape[0]
     fetch = pltpu.make_async_copy(transfer, table.at[pl.ds(0, count)], sem)
     fetch.start()
     table[count] = jnp.zeros(table.shape[1:], BF16)
-    theta_stage(sides, low, high, polar, side_half)
+    theta_stage(level, low, high, 0, polar, half)
+    theta_stage(sides, low, high, level.shape[0] // 2, polar, side_half)
 
     def phi_stage(place, carry):
         rows = []
@@ -492,10 +552,10 @@
     targets = out.shape[0]
     slots = src.shape[0] // targets
 
-    def one(t, carry):
+    def one(t, count):
         re = [jnp.zeros((8, 128), F32)] * 4
         im = [jnp.zeros((8, 128), F32)] * 4
-        for j in range(slots):
+        for j in range(count):
             at = pl.multiple_of(src[t * slots + j], 64)
             w = table.at[off[t * slots + j]]
             for r in range(4):
@@ -508,36 +568,35 @@
         for r in range(4):
             out[t, 0, 8 * r : 8 * r + 8] = re[r].astype(BF16)
             out[t, 1, 8 * r : 8 * r + 8] = im[r].astype(BF16)
-        return carry
-
-    lax.fori_loop(0, targets, one, 0)
-
-
-def top_level(half, sides, low, high, polar, azimuth, tab, transfer, sources, offsets):
+
+    by_class(order, starts, slots, 1, one)
+
+
+def top_level(level, sides, low, high, polar, azimuth, tab, transfer, sources, offsets, order, starts):
     count, _, rows, cols = transfer.shape
-    smem = pl.BlockSpec(memory_space=pltpu.SMEM)
-    vmem = pl.BlockSpec(memory_space=pltpu.VMEM)
-    parents = half.shape[0]
+    parents = level.shape[0]
+    lines = polar.shape[1:2] + level.shape[2:]
     return pl.pallas_call(
         top_body,
-        in_specs=[smem, smem] + [vmem] * 7 + [pl.BlockSpec(memory_space=pl.ANY)],
-        out_specs=vmem,
+        in_specs=[SMEM_SPEC] * 4 + [VMEM_SPEC] * 7 + [ANY_SPEC],
+        out_specs=VMEM_SPEC,
         out_shape=jax.ShapeDtypeStruct((parents, 2, rows, cols), BF16),
         scratch_shapes=[
             pltpu.VMEM((count + 1, 2, rows, cols), BF16),
-            pltpu.VMEM((sides.shape[0],) + half.shape[1:], BF16),
+            pltpu.VMEM((parents,) + lines, BF16),
+            pltpu.VMEM((sides.shape[0],) + lines, BF16),
             pltpu.VMEM((parents * 2 * rows, cols), F32),
             pltpu.SemaphoreType.DMA,
         ],
         compiler_params=pltpu.CompilerParams(vmem_limit_bytes=24 * 1024 * 1024),
         name="top_level",
-    )(sources, offsets, half, sides, low, high, polar, azimuth, tab, transfer)
+    )(sources, offsets, order, starts, level, sides, low, high, polar, azimuth, tab, transfer)
 
 
 def flat_lists(sources, offsets, dead, source_rows, factor_rows):
     src = jnp.maximum(sources, 0) * source_rows
     off = jnp.where(offsets < 0, dead, offsets) * factor_rows
-    return src.reshape(-1), off.reshape(-1)
+    return (src.reshape(-1), off.reshape(-1)) + target_classes(sources)
 
 
 def shards(
@@ -568,8 +627,12 @@
     count5 = transfer5.shape[0]
     count4 = transfer4.shape[0]
     table5 = transfer_table(transfer5)
-    src5, off5 = flat_lists(sources5, offsets5, count5, 16, 16)
-    src4, off4 = flat_lists(sources4, offsets4, count4, 64, 1)
+    half5 = sources5.shape[0] // 2
+    lists5 = (
+        flat_lists(sources5[:half5], offsets5[:half5], count5, 16, 16),
+        flat_lists(sources5[half5:], offsets5[half5:], count5, 16, 16),
+    )
+    lists4 = flat_lists(sources4, offsets4, count4, 64, 1)
     rows4 = polar_first.shape[0]
     cols4 = azimuth_first.shape[0]
     band_rows = rows4 // bands
@@ -595,28 +658,25 @@
     f1 = scale * (x - y)
     tab = jnp.stack([jnp.cos(f0), jnp.sin(f0), jnp.cos(f1), jnp.sin(f1)])
     polar, azimuth = stencils(tap_u, weight_u, trig, tap_v, weight_v)
-    arrived, table5, src5, off5, src4, off4, polar, azimuth, tab = lax.optimization_barrier(
-        (arrived, table5, src5, off5, src4, off4, polar, azimuth, tab)
+    arrived, table5, lists5, lists4, polar, azimuth, tab = lax.optimization_barrier(
+        (arrived, table5, lists5, lists4, polar, azimuth, tab)
     )
 
     level = arrived.reshape(64, 128, 128)
-    right, left, last, first = edges(level)
+    right, left = edge_columns(level)
     around = lambda step: [(i, (i + step) % blocks) for i in range(blocks)]
     across = lambda step: [(i, i + step) for i in range(bands) if 0 <= i + step < bands]
     from_left = lax.ppermute(right, "clu", around(1))
     from_right = lax.ppermute(left, "clu", around(-1))
+    before, tiles, table5 = translate_first(arrived.reshape(512, 16, 128), table5, lists5[0])
+    from_left, from_right, tiles = lax.optimization_barrier((from_left, from_right, tiles))
+    sides, last, first = edge_rows(level, from_left, from_right)
+    last, first, tiles = lax.optimization_barrier((last, first, tiles))
     low = lax.ppermute(last, "ang", across(1))
     high = lax.ppermute(first, "ang", across(-1))
-    translated5 = translate5(arrived.reshape(512, 16, 128), table5, src5, off5)
-    from_left, from_right, translated5 = lax.optimization_barrier(
-        (from_left, from_right, translated5)
-    )
-    sides, side_last, side_first = corners(from_left, from_right)
-    side_low = lax.ppermute(side_last, "ang", across(1))
-    side_high = lax.ppermute(side_first, "ang", across(-1))
-    half = theta_level(level, low, high, polar)
+    translated5 = translate_last(tiles, table5, before, lists5[1])
     translated4 = top_level(
-        half, sides, side_low, side_high, polar, azimuth, tab, transfer4, src4, off4
+        level, sides, low, high, polar, azimuth, tab, transfer4, *lists4
     )
     return (translated5, translated4)
 

time: 125 us -> 108 us (0.86)
  starting transfers between devices: 31.1 us -> 21.5 us
  Pallas kernels: 58.8 us -> 55.3 us
  waiting for transfers between devices: 21.7 us -> 18.3 us
  other arithmetic: 1.94 us -> 3.25 us
    ppermute x2 -> x0, starting transfers between devices: 10.2 us -> none  [the longest x1 7.95 us: shards(): side_low = lax.ppermute(side_last, 'ang', across(1))]
    ppermute x2 -> x0, waiting for transfers between devices: 4.48 us -> none  [the longest x1 4.47 us: shards(): side_high = lax.ppermute(side_first, 'ang', across(-1))]
    pallas_call x5, Pallas kernels: 38.7 us -> 35.1 us  [the longest x1 14.2 us: top_level(): pl.pallas_call(top_body, in_specs=[SMEM_SPEC] * 4 + [VMEM_SPEC] * 7 + [AN...]
    ppermute x1, waiting for transfers between devices: 0.01 us -> 2.56 us  [shards(): high = lax.ppermute(first, 'ang', across(-1))]
    all_to_all x1, waiting for transfers between devices: 17.2 us -> 15.7 us  [shards(): lax.all_to_all(send, ('clu', 'ang'), split_axis=0, concat_axis=0, tiled=T...]
    unnamed x32 -> x31, local copies, waits for them, and re-layouts: 7.61 us -> 6.12 us
    reduce_sum x0 -> x11, other arithmetic: none -> 1.28 us  [the longest x3 0.54 us: target_classes(): place = jnp.sum((key[None, :] < key[:, None]).astype(jnp.int32), axis=1)]
  transfers between devices with their start and end apart: 7 -> 5, of which waited for: 2 -> 2; matrix products, arithmetic and copies ran while one was open for 3% -> 5% of each run, Pallas kernels for 22% -> 21%
where the time goes in v3:
time: 108 us
  Pallas kernels  55.3 us (51%)
  starting transfers between devices  21.5 us (20%)
  waiting for transfers between devices  18.3 us (17%)
  local copies, waits for them, and re-layouts  8.16 us (8%)
  other arithmetic  3.25 us (3%)
  between operations  1.15 us (1%)
    pallas_call x1, Pallas kernels, aggregate(): pl.pallas_call(aggregate_body, grid=(clusters,), in_specs=[pl.BlockSpec((...  16.7 us
    all_to_all x1, waiting for transfers between devices, shards(): lax.all_to_all(send, ('clu', 'ang'), split_axis=0, concat_axis=0, tiled=T...  15.7 us
    pallas_call x1, Pallas kernels, top_level(): pl.pallas_call(top_body, in_specs=[SMEM_SPEC] * 4 + [VMEM_SPEC] * 7 + [AN...  14.2 us
    all_to_all x1, starting transfers between devices, shards(): lax.all_to_all(send, ('clu', 'ang'), split_axis=0, concat_axis=0, tiled=T...  10.8 us
    pallas_call x1, Pallas kernels, translate_first(): pl.pallas_call(first_targets_body, in_specs=[SMEM_SPEC] * 4 + [VMEM_SPEC,...  10.5 us
    pallas_call x1, Pallas kernels, translate_last(): pl.pallas_call(last_targets_body, in_specs=[SMEM_SPEC] * 4 + [VMEM_SPEC]...  8.69 us
    unnamed x31, local copies, waits for them, and re-layouts  6.12 us
    ppermute x1, starting transfers between devices, shards(): low = lax.ppermute(last, 'ang', across(1))  5.11 us
  transfers between devices with their start and end apart: 5, of which 2 were waited for; matrix products, arithmetic and copies ran while one was open for 5% of the time, Pallas kernels for 21%

profile of v3, /device:TPU:7, one launch (start us, length us, event | category | flops | bytes accessed | tf_op | source)
XLA Modules:
  0.0 107.5 jit_solution(10696479250440660954)
XLA Ops:
  0.6 16.7 %aggregate.1 = bf16[128,4,16,128]{3,2,1,0:T(8,128)(2,1)} custom-call(bf16[32768,128]{1,0:T(8,128)(2,1)} %bitcast.17, bf16[64,128]{1,0:T(8,128)(2,1)} %bitcast.19, bf16[128,256]{1,0:T(8,128)(2,1)} %b7.1, bf16[256,128]{1,0:T(8,128)(2,1)} %a6.1, bf16[256,512]{1,0:T(8,128)(2,1)} %b6.1, f32[128,256]{1,0:T(8,128)} %constant.27.clone.top7, ...), custom_call_target="tpu_custom_call" | custom-call | tf_op jit(solution)/shard_map/aggregate/pallas_call | solution.py:180
  17.4 10.8 %all-to-all-start = ((bf16[128,4,16,128]{3,2,1,0:T(8,128)(2,1)}), bf16[128,4,16,128]{3,2,1,0:T(8,128)(2,1)S(1)}, u32[]{:S(2)}, u32[]{:S(2)}) async-start(bf16[128,4,16,128]{3,2,1,0:T(8,128)(2,1)} %aggregate.1), calls=%async_computation | async-start | bytes 4194304 | tf_op jit(solution)/shard_map/all_to_all | solution.py:625
  28.3 0.8 subtract_add_fusion
  29.2 0.8 dynamic_slice.14
  30.0 0.7 convert_bitcast_fusion.weight_v
  32.0 1.4 %copy-done.5 = bf16[316,2,16,64]{0,3,2,1:T(8,128)(2,1)S(1)} copy-done((bf16[316,2,16,64]{0,3,2,1:T(8,128)(2,1)S(1)}, bf16[316,2,16,64]{0,3,2,1:T(8,128)(2,1)}, u32[]{:S(2)}) %copy-start.5) | copy-done | bytes 1294360
  33.4 2.8 %transfer_table.1.table_from = f32[5120,128]{1,0:T(8,128)S(1)} custom-call(bf16[2,2,8,64,316]{4,3,2,1,0:T(8,128)(2,1)S(1)} %bitcast.16), custom_call_target="tpu_custom_call" | custom-call | tf_op jit(solution)/shard_map/transfer_table/pallas_call | solution.py:217
  36.3 1.5 %copy-done.1 = f32[5120,128]{1,0:T(8,128)} copy-done((f32[5120,128]{1,0:T(8,128)}, f32[5120,128]{1,0:T(8,128)S(1)}, u32[]{:S(2)}) %copy-start.1) | copy-done | bytes 2621464
  37.9 0.6 stencils.1
  38.5 1.3 %copy-done.3 = bf16[8,512,256]{2,1,0:T(8,128)(2,1)} copy-done((bf16[8,512,256]{2,1,0:T(8,128)(2,1)}, bf16[8,512,256]{2,1,0:T(8,128)(2,1)S(1)}, u32[]{:S(2)}) %copy-start.3) | copy-done | bytes 2097176
  40.6 0.2 fusion.2
  41.0 0.2 convert_reduce_fusion.1
  41.4 15.7 %all-to-all-done = bf16[128,4,16,128]{3,2,1,0:T(8,128)(2,1)S(1)} async-done(((bf16[128,4,16,128]{3,2,1,0:T(8,128)(2,1)}), bf16[128,4,16,128]{3,2,1,0:T(8,128)(2,1)S(1)}, u32[]{:S(2)}, u32[]{:S(2)}) %all-to-all-start) | async-done | bytes 2097184 | tf_op jit(solution)/shard_map/all_to_all | solution.py:625
  57.1 1.0 edge_columns.1
  58.2 0.4 collective-permute-start
  58.6 3.2 %collective-permute-start.1 = (bf16[8,128,128]{2,1,0:T(8,128)(2,1)S(1)}, bf16[8,128,128]{2,1,0:T(8,128)(2,1)S(1)}, u32[]{:S(2)}, u32[]{:S(2)}) collective-permute-start(bf16[8,128,128]{2,1,0:T(8,128)(2,1)S(1)} %get-tuple-element.43), channel_id=1, source_target_pairs={{0,112},{16,0},{32,16},{48,32},{64,48},{80,64},{96,80},{112,96},{1... | collective-permute-start | bytes 786440 | tf_op jit(solution)/shard_map/ppermute | solution.py:670
  61.8 1.7 %copy-done.2 = f32[5120,128]{1,0:T(8,128)S(1)} copy-done((f32[5120,128]{1,0:T(8,128)S(1)}, f32[5120,128]{1,0:T(8,128)}, u32[]{:S(2)}) %copy-start.2) | copy-done | bytes 2621464
  63.5 10.5 %translate_first.1 = (bf16[2,16,64,256]{3,2,1,0:T(8,128)(2,1)S(1)}, f32[8192,128]{1,0:T(8,128)S(1)}, f32[5120,128]{1,0:T(8,128)S(1)}) custom-call(s32[4096]{0:T(1024)S(1)} %reshape.547.src, s32[4096]{0:T(1024)S(1)} %reshape.548.off, s32[256]{0:T(256)S(1)} %select_reduce_fusion.1.order, s32[6]{0:T(128)S(1)} %convert_reduce_fusion.7.starts, ...), custom_call_target="tpu_custom_call" | custom-call | tf_op jit(solution)/shard_map/translate_first/pallas_call | solution.py:336
  74.1 0.6 edge_rows.1
  74.7 5.1 %collective-permute-start.2 = (bf16[36,48,128]{2,1,0:T(8,128)(2,1)S(1)}, bf16[36,48,128]{2,1,0:T(8,128)(2,1)S(1)}, u32[]{:S(2)}, u32[]{:S(2)}) collective-permute-start(bf16[36,48,128]{2,1,0:T(8,128)(2,1)S(1)} %get-tuple-element.63), channel_id=1, source_target_pairs={{0,1},{1,2},{2,3},{3,4},{4,5},{5,6},{6,7},{7,8},{8,9},{9,10},{10,1... | collective-permute-start | bytes 1327112 | tf_op jit(solution)/shard_map/ppermute | solution.py:675
  79.9 1.9 %collective-permute-start.3 = (bf16[36,48,128]{2,1,0:T(8,128)(2,1)S(1)}, bf16[36,48,128]{2,1,0:T(8,128)(2,1)S(1)}, u32[]{:S(2)}, u32[]{:S(2)}) collective-permute-start(bf16[36,48,128]{2,1,0:T(8,128)(2,1)S(1)} %get-tuple-element.64), channel_id=1, source_target_pairs={{1,0},{2,1},{3,2},{4,3},{5,4},{6,5},{7,6},{8,7},{9,8},{10,9},{11,1... | collective-permute-start | bytes 1327112 | tf_op jit(solution)/shard_map/ppermute | solution.py:676
  81.8 8.7 %translate_last.1 = bf16[2,16,64,512]{3,2,1,0:T(8,128)(2,1)} custom-call(s32[4096]{0:T(1024)S(1)} %reshape.549.src, s32[4096]{0:T(1024)S(1)} %reshape.550.off, s32[256]{0:T(256)S(1)} %select_reduce_fusion.order, s32[6]{0:T(128)S(1)} %convert_reduce_fusion.6.starts, f32[8192,128]{1,0:T(8,128)S(1)} %get-tuple-element.55.tiles, ...), custom_call_target="tpu_custom_call" | custom-call | tf_op jit(solution)/shard_map/translate_last/pallas_call | solution.py:353
  90.5 2.6 %collective-permute-done.3.high = bf16[36,48,128]{2,1,0:T(8,128)(2,1)S(1)} collective-permute-done((bf16[36,48,128]{2,1,0:T(8,128)(2,1)S(1)}, bf16[36,48,128]{2,1,0:T(8,128)(2,1)S(1)}, u32[]{:S(2)}, u32[]{:S(2)}) %collective-permute-start.3) | collective-permute-done | bytes 442400 | tf_op jit(solution)/shard_map/ppermute | solution.py:676
  93.1 14.2 %top_level.1 = bf16[64,2,32,128]{3,2,1,0:T(8,128)(2,1)} custom-call(s32[1024]{0:T(1024)S(1)} %reshape.551.src, s32[1024]{0:T(1024)S(1)} %reshape.552.off, s32[64]{0:T(128)S(1)} %select_reduce_fusion.2.order, s32[6]{0:T(128)S(1)} %convert_reduce_fusion.8.starts, bf16[64,128,128]{2,1,0:T(8,128)(2,1)S(1)} %bitcast.13, ...), custom_call_target="tpu_custom_call" | custom-call | tf_op jit(solution)/shard_map/top_level/pallas_call | solution.py:579
  (67 shorter events, 2.9 us)
Async XLA Ops:
  0.6 28.5 %copy-start = (bf16[512,4]{0,1:T(4,128)(2,1)S(1)}, bf16[512,4]{0,1:T(4,128)(2,1)}, u32[]{:S(2)}) copy-start(bf16[512,4]{0,1:T(4,128)(2,1)} %param.30) | copy-start | bytes 12292
  17.4 13.3 %copy-start.9 = (s32[512,16]{0,1:T(8,128)S(1)}, s32[512,16]{0,1:T(8,128)}, u32[]{:S(2)}) copy-start(s32[512,16]{0,1:T(8,128)} %param.34) | copy-start | bytes 98308
  17.4 13.3 %copy-start.11 = (s32[64,16]{0,1:T(8,128)S(1)}, s32[64,16]{0,1:T(8,128)}, u32[]{:S(2)}) copy-start(s32[64,16]{0,1:T(8,128)} %param.37) | copy-start | bytes 12292
  17.4 13.3 %copy-start.10 = (s32[512,16]{0,1:T(8,128)S(1)}, s32[512,16]{0,1:T(8,128)}, u32[]{:S(2)}) copy-start(s32[512,16]{0,1:T(8,128)} %param.35) | copy-start | bytes 98308
  17.4 13.3 %copy-start.12 = (s32[64,16]{0,1:T(8,128)S(1)}, s32[64,16]{0,1:T(8,128)}, u32[]{:S(2)}) copy-start(s32[64,16]{0,1:T(8,128)} %param.38) | copy-start | bytes 12292
  17.4 39.7 %all-to-all-start = ((bf16[128,4,16,128]{3,2,1,0:T(8,128)(2,1)}), bf16[128,4,16,128]{3,2,1,0:T(8,128)(2,1)S(1)}, u32[]{:S(2)}, u32[]{:S(2)}) async-start(bf16[128,4,16,128]{3,2,1,0:T(8,128)(2,1)} %aggregate.1), calls=%async_computation | async-start | bytes 4194304 | tf_op jit(solution)/shard_map/all_to_all | solution.py:625
  31.2 6.7 %copy-start.7 = (f32[2,8,224]{2,1,0:T(8,128)S(1)}, f32[2,8,224]{2,1,0:T(8,128)}, u32[]{:S(2)}) copy-start(f32[2,8,224]{2,1,0:T(8,128)} %constant.92.clone.factor) | copy-start | bytes 43012
  31.2 6.7 %copy-start.8 = (s32[1,224]{1,0:T(1,128)S(1)}, s32[1,224]{1,0:T(1,128)}, u32[]{:S(2)}) copy-start(s32[1,224]{1,0:T(1,128)} %constant.91.clone.ext) | copy-start | bytes 2692
  32.0 1.4 %copy-start.5 = (bf16[316,2,16,64]{0,3,2,1:T(8,128)(2,1)S(1)}, bf16[316,2,16,64]{0,3,2,1:T(8,128)(2,1)}, u32[]{:S(2)}) copy-start(bf16[316,2,16,64]{0,3,2,1:T(8,128)(2,1)} %param.33) | copy-start | bytes 3883012
  36.2 1.5 %copy-start.1 = (f32[5120,128]{1,0:T(8,128)}, f32[5120,128]{1,0:T(8,128)S(1)}, u32[]{:S(2)}) copy-start(f32[5120,128]{1,0:T(8,128)S(1)} %transfer_table.1.table_from) | copy-start | bytes 7864324
  38.5 1.3 %copy-start.3 = (bf16[8,512,256]{2,1,0:T(8,128)(2,1)}, bf16[8,512,256]{2,1,0:T(8,128)(2,1)S(1)}, u32[]{:S(2)}) copy-start(bf16[8,512,256]{2,1,0:T(8,128)(2,1)S(1)} %get-tuple-element.66.azimuth) | copy-start | bytes 6291460
  57.1 17.0 %copy-start.6 = (bf16[96,256]{1,0:T(8,128)(2,1)S(1)}, bf16[96,256]{1,0:T(8,128)(2,1)}, u32[]{:S(2)}) copy-start(bf16[96,256]{1,0:T(8,128)(2,1)} %constant.93.clone.pick) | copy-start | bytes 147460
  58.2 15.9 %collective-permute-start = (bf16[8,128,128]{2,1,0:T(8,128)(2,1)S(1)}, bf16[8,128,128]{2,1,0:T(8,128)(2,1)S(1)}, u32[]{:S(2)}, u32[]{:S(2)}) collective-permute-start(bf16[8,128,128]{2,1,0:T(8,128)(2,1)S(1)} %get-tuple-element.42), channel_id=1, source_target_pairs={{0,16},{16,32},{32,48},{48,64},{64,80},{80,96},{96,112},{112,0},{1... | collective-permute-start | bytes 786440 | tf_op jit(solution)/shard_map/ppermute | solution.py:669
  58.6 15.5 %collective-permute-start.1 = (bf16[8,128,128]{2,1,0:T(8,128)(2,1)S(1)}, bf16[8,128,128]{2,1,0:T(8,128)(2,1)S(1)}, u32[]{:S(2)}, u32[]{:S(2)}) collective-permute-start(bf16[8,128,128]{2,1,0:T(8,128)(2,1)S(1)} %get-tuple-element.43), channel_id=1, source_target_pairs={{0,112},{16,0},{32,16},{48,32},{64,48},{80,64},{96,80},{112,96},{1... | collective-permute-start | bytes 786440 | tf_op jit(solution)/shard_map/ppermute | solution.py:670
  61.8 1.7 %copy-start.2 = (f32[5120,128]{1,0:T(8,128)S(1)}, f32[5120,128]{1,0:T(8,128)}, u32[]{:S(2)}) copy-start(f32[5120,128]{1,0:T(8,128)} %copy-done.1) | copy-start | bytes 7864324
  74.7 15.8 %collective-permute-start.2 = (bf16[36,48,128]{2,1,0:T(8,128)(2,1)S(1)}, bf16[36,48,128]{2,1,0:T(8,128)(2,1)S(1)}, u32[]{:S(2)}, u32[]{:S(2)}) collective-permute-start(bf16[36,48,128]{2,1,0:T(8,128)(2,1)S(1)} %get-tuple-element.63), channel_id=1, source_target_pairs={{0,1},{1,2},{2,3},{3,4},{4,5},{5,6},{6,7},{7,8},{8,9},{9,10},{10,1... | collective-permute-start | bytes 1327112 | tf_op jit(solution)/shard_map/ppermute | solution.py:675
  79.9 13.2 %collective-permute-start.3 = (bf16[36,48,128]{2,1,0:T(8,128)(2,1)S(1)}, bf16[36,48,128]{2,1,0:T(8,128)(2,1)S(1)}, u32[]{:S(2)}, u32[]{:S(2)}) collective-permute-start(bf16[36,48,128]{2,1,0:T(8,128)(2,1)S(1)} %get-tuple-element.64), channel_id=1, source_target_pairs={{1,0},{2,1},{3,2},{4,3},{5,4},{6,5},{7,6},{8,7},{9,8},{10,9},{11,1... | collective-permute-start | bytes 1327112 | tf_op jit(solution)/shard_map/ppermute | solution.py:676
  81.8 11.3 %slice-start = ((s8[5177344]{0:T(1024)(128)(4,1)}), s8[4194304]{0:T(1024)(128)(4,1)S(1)}, s32[]{:S(2)}) async-start(s8[5177344]{0:T(1024)(128)(4,1)} %bitcast.14), calls=%async_computation.1 | async-start | bytes 8388608
  81.8 11.3 %slice-start.1 = ((s8[5177344]{0:T(1024)(128)(4,1)}), s8[983040]{0:T(1024)(128)(4,1)S(1)}, s32[]{:S(2)}) async-start(s8[5177344]{0:T(1024)(128)(4,1)} %bitcast.14), calls=%async_computation.2 | async-start | bytes 1966080
  81.8 11.3 %copy-start.4 = (bf16[8,512,256]{2,1,0:T(8,128)(2,1)S(1)}, bf16[8,512,256]{2,1,0:T(8,128)(2,1)}, u32[]{:S(2)}) copy-start(bf16[8,512,256]{2,1,0:T(8,128)(2,1)} %copy-done.3) | copy-start | bytes 6291460

commit v4 on v3

--- a/solution.py
+++ b/solution.py
@@ -10,6 +10,8 @@
 
 F32 = jnp.float32
 BF16 = jnp.bfloat16
+TOGETHER = 2
+BLOCK5 = 128
 
 
 PAIRS = ((3, 0), (1, 2))
@@ -69,42 +71,46 @@
         m6[1, :, rows6 : 2 * rows6] = s.astype(BF16)
 
     step = 2 * rows7
-    for o6 in range(8):
-        base = o6 * 8 * step
-        parts = []
-        for k in range(4):
-            low = pat[base + k * step : base + (k + 1) * step, :]
-            high = pat[base + (k + 4) * step : base + (k + 5) * step, :]
-            parts.append(jnp.concatenate([low, high], axis=0))
-        lanes = parts[0].shape[1]
-        h = dot(m7[...], jnp.concatenate(parts, axis=1))
+    for first in range(0, 8, TOGETHER):
+        stacks = []
+        for o6 in range(first, first + TOGETHER):
+            base = o6 * 8 * step
+            for k in range(4):
+                low = pat[base + k * step : base + (k + 1) * step, :]
+                high = pat[base + (k + 4) * step : base + (k + 5) * step, :]
+                stacks.append(jnp.concatenate([low, high], axis=0))
+        lanes = stacks[0].shape[1]
+        h = dot(m7[...], jnp.concatenate(stacks, axis=1))
         rows = []
-        for a, b in PAIRS:
-            ya = h[:, a * lanes : (a + 1) * lanes]
-            yb = h[:, b * lanes : (b + 1) * lanes]
-            rows.append((ya + yb).astype(BF16))
-            rows.append((ya - yb).astype(BF16))
-        y = dot(jnp.concatenate(rows, axis=0), b7[...])
-        for half in range(2):
-            cols = slice(half * (cols6 // 2), (half + 1) * (cols6 // 2))
-            re = None
-            for q in range(2):
-                at = q * 4 * rows6
-                pr = y[at : at + rows6, cols]
-                pi = y[at + rows6 : at + 2 * rows6, cols]
-                qr = y[at + 2 * rows6 : at + 3 * rows6, cols]
-                qi = y[at + 3 * rows6 : at + 4 * rows6, cols]
-                c = tab6[2 * q]
-                s = tab6[2 * q + 1]
-                if half == 1:
-                    dr = c * pr + s * qi
-                    di = c * pi - s * qr
-                else:
-                    dr = c * pr - s * qi
-                    di = c * pi + s * qr
-                re, im = (dr, di) if re is None else (re + dr, im + di)
-            level6[o6, 0, :, cols] = re
-            level6[o6, 1, :, cols] = im
+        for n in range(TOGETHER):
+            for a, b in PAIRS:
+                ya = h[:, (4 * n + a) * lanes : (4 * n + a + 1) * lanes]
+                yb = h[:, (4 * n + b) * lanes : (4 * n + b + 1) * lanes]
+                rows.append((ya + yb).astype(BF16))
+                rows.append((ya - yb).astype(BF16))
+        everything = dot(jnp.concatenate(rows, axis=0), b7[...])
+        for n in range(TOGETHER):
+            y = everything[n * 8 * rows6 : (n + 1) * 8 * rows6]
+            for half in range(2):
+                cols = slice(half * (cols6 // 2), (half + 1) * (cols6 // 2))
+                re = None
+                for q in range(2):
+                    at = q * 4 * rows6
+                    pr = y[at : at + rows6, cols]
+                    pi = y[at + rows6 : at + 2 * rows6, cols]
+                    qr = y[at + 2 * rows6 : at + 3 * rows6, cols]
+                    qi = y[at + 3 * rows6 : at + 4 * rows6, cols]
+                    c = tab6[2 * q]
+                    s = tab6[2 * q + 1]
+                    if half == 1:
+                        dr = c * pr + s * qi
+                        di = c * pi - s * qr
+                    else:
+                        dr = c * pr - s * qi
+                        di = c * pi + s * qr
+                    re, im = (dr, di) if re is None else (re + dr, im + di)
+                level6[first + n, 0, :, cols] = re
+                level6[first + n, 1, :, cols] = im
 
     for part in range(2):
         for r in range(0, rows6, 16):
@@ -120,7 +126,7 @@
             rhs = jnp.concatenate([mixed[x, 0, part], mixed[x, 1, 1 - part]], axis=0)
             half6[x, part] = dot(m6[part], rhs).astype(BF16)
 
-    block = 64
+    block = BLOCK5
     quarter = cols5 // 4
     low_lane = lax.broadcasted_iota(jnp.int32, (block, quarter), 1) < quarter // 2
     for u in range(0, rows5, block):
@@ -333,6 +339,7 @@
 def translate_first(level, table, lists):
     clusters, rows, lanes = level.shape
     targets = lists[2].shape[0]
+    table = pltpu.with_memory_space_constraint(table, pltpu.HBM)
     return pl.pallas_call(
         first_targets_body,
         in_specs=[SMEM_SPEC] * 4 + [VMEM_SPEC, pl.BlockSpec(memory_space=pltpu.HBM)],
@@ -469,8 +476,6 @@
         first = part == 0
         azimuth[index, at : at + 128, :128] = jnp.where(first, matrix, 0.0).astype(BF16)
         azimuth[index, at : at + 128, 128:] = jnp.where(first, 0.0, matrix).astype(BF16)
-        azimuth[index, at + 128 : at + 256, :128] = jnp.where(first, 0.0, -matrix).astype(BF16)
-        azimuth[index, at + 128 : at + 256, 128:] = jnp.where(first, matrix, 0.0).astype(BF16)
 
     def matrix_at(q):
         total = jnp.zeros((128, 128), F32)
@@ -483,7 +488,7 @@
     halo = jnp.where(j < 3, matrix_at(j + 67 * ((i >> 3) & 1)), 0.0)
     for index in range(8):
         fill(0, own, i >> 6, index)
-        fill(256, jnp.where((i >> 4) == index, halo, 0.0), (i >> 2) & 1, index)
+        fill(128, jnp.where((i >> 4) == index, halo, 0.0), (i >> 2) & 1, index)
 
 
 def stencils(tap_u, weight_u, trig, tap_v, weight_v):
@@ -493,18 +498,21 @@
         stencils_body,
         out_shape=(
             jax.ShapeDtypeStruct((2, 8 * rows, 224), BF16),
-            jax.ShapeDtypeStruct((8, 512, 256), BF16),
+            jax.ShapeDtypeStruct((8, 256, 256), BF16),
         ),
         compiler_params=pltpu.CompilerParams(vmem_limit_bytes=8 * 1024 * 1024),
         name="stencils",
     )(tap_u, weight_u, trig, tap_v, weight_v, jnp.asarray(ext), jnp.asarray(factor))
 
 
-def theta_stage(level, low, high, at, polar, half):
+def theta_stage(level, low, high, at, polar, half, swap):
     for i in range(level.shape[0] // 2):
         for parity in range(2):
             rhs = jnp.concatenate([level[2 * i + parity], low[at + i], high[at + i]], axis=0)
-            half[2 * i + parity] = dot(polar[parity], rhs).astype(BF16)
+            y = dot(polar[parity], rhs)
+            for x in range(4):
+                c, s = y[64 * x : 64 * x + 32], y[64 * x + 32 : 64 * x + 64]
+                half[2 * i + parity, 32 * x : 32 * x + 32] = (c + swap(s)).astype(BF16)
 
 
 def top_body(
@@ -515,19 +523,25 @@
     fetch = pltpu.make_async_copy(transfer, table.at[pl.ds(0, count)], sem)
     fetch.start()
     table[count] = jnp.zeros(table.shape[1:], BF16)
-    theta_stage(level, low, high, 0, polar, half)
-    theta_stage(sides, low, high, level.shape[0] // 2, polar, side_half)
+    lane = lax.broadcasted_iota(jnp.int32, (32, 128), 1)
+    wide = jnp.where(lane < 64, -1.0, 1.0)
+    real = (lane & 4) == 0
+
+    def swap_wide(s):
+        return pltpu.roll(s, 64, 1) * wide
+
+    def swap_near(s):
+        return jnp.where(real, -pltpu.roll(s, 124, 1), pltpu.roll(s, 4, 1))
+
+    theta_stage(level, low, high, 0, polar, half, swap_wide)
+    theta_stage(sides, low, high, level.shape[0] // 2, polar, side_half, swap_near)
 
     def phi_stage(place, carry):
         rows = []
         for g in range(8):
             for x in range(4):
-                a = slice(64 * x, 64 * x + 32)
-                b = slice(64 * x + 32, 64 * x + 64)
-                p = 8 * g + place
-                rows.append(
-                    jnp.concatenate([half[p, a], half[p, b], side_half[g, a], side_half[g, b]], axis=1)
-                )
+                a = slice(32 * x, 32 * x + 32)
+                rows.append(jnp.concatenate([half[8 * g + place, a], side_half[g, a]], axis=1))
         y = dot(jnp.concatenate(rows, axis=0), azimuth[place])
         for g in range(8):
             re = im = None
@@ -572,10 +586,10 @@
     by_class(order, starts, slots, 1, one)
 
 
-def top_level(level, sides, low, high, polar, azimuth, tab, transfer, sources, offsets, order, starts):
+def top_level(level, sides, low, high, polar, azimuth, tab, transfer, lists):
     count, _, rows, cols = transfer.shape
     parents = level.shape[0]
-    lines = polar.shape[1:2] + level.shape[2:]
+    lines = (polar.shape[1] // 2, level.shape[2])
     return pl.pallas_call(
         top_body,
         in_specs=[SMEM_SPEC] * 4 + [VMEM_SPEC] * 7 + [ANY_SPEC],
@@ -588,9 +602,9 @@
             pltpu.VMEM((parents * 2 * rows, cols), F32),
             pltpu.SemaphoreType.DMA,
         ],
-        compiler_params=pltpu.CompilerParams(vmem_limit_bytes=24 * 1024 * 1024),
+        compiler_params=pltpu.CompilerParams(vmem_limit_bytes=30 * 1024 * 1024),
         name="top_level",
-    )(sources, offsets, order, starts, level, sides, low, high, polar, azimuth, tab, transfer)
+    )(*lists, level, sides, low, high, polar, azimuth, tab, transfer)
 
 
 def flat_lists(sources, offsets, dead, source_rows, factor_rows):
@@ -676,7 +690,7 @@
     high = lax.ppermute(first, "ang", across(-1))
     translated5 = translate_last(tiles, table5, before, lists5[1])
     translated4 = top_level(
-        level, sides, low, high, polar, azimuth, tab, transfer4, *lists4
+        level, sides, low, high, polar, azimuth, tab, transfer4, lists4
     )
     return (translated5, translated4)
 

time: 108 us -> 106 us (0.981)
  waiting for transfers between devices: 18.3 us -> 12.2 us
  other arithmetic: 3.25 us -> 9.27 us
  Pallas kernels: 55.3 us -> 53.8 us
    all_to_all x1, waiting for transfers between devices: 15.7 us -> 9.8 us  [shards(): lax.all_to_all(send, ('clu', 'ang'), split_axis=0, concat_axis=0, tiled=T...]
    reduce_sum x3, other arithmetic: 0.35 us -> 2.08 us  [target_classes(): starts = jnp.sum((kind[None, :] < kinds[:, None]).astype(jnp.int32), axis=1)]
    add x2, other arithmetic: 0.02 us -> 1.4 us  [target_classes(): key = kind * targets + index]
    reduce_sum x2, other arithmetic: 0.04 us -> 1.22 us  [target_classes(): live = jnp.sum((sources >= 0).astype(jnp.int32), axis=1)]
    reduce_sum x3, other arithmetic: 0.35 us -> 1.52 us  [target_classes(): jnp.sum(jnp.where(place[None, :] == index[:, None], index[None, :], 0), a...]
    unnamed x31 -> x37, local copies, waits for them, and re-layouts: 6.12 us -> 5.11 us
  transfers between devices with their start and end apart: 5 -> 5, of which waited for: 2 -> 2; matrix products, arithmetic and copies ran while one was open for 5% -> 11% of each run, Pallas kernels for 21% -> 21%
where the time goes in v4:
time: 106 us; the launch traced here: 105 us
  Pallas kernels  53.8 us (51%)
  starting transfers between devices  21.5 us (20%)
  waiting for transfers between devices  12.2 us (12%)
  other arithmetic  9.27 us (9%)
  local copies, waits for them, and re-layouts  7.15 us (7%)
  between operations  1.13 us (1%)
    pallas_call x1, Pallas kernels, aggregate(): pl.pallas_call(aggregate_body, grid=(clusters,), in_specs=[pl.BlockSpec((...  16.5 us
    pallas_call x1, Pallas kernels, top_level(): pl.pallas_call(top_body, in_specs=[SMEM_SPEC] * 4 + [VMEM_SPEC] * 7 + [AN...  13.3 us
    all_to_all x1, starting transfers between devices, shards(): lax.all_to_all(send, ('clu', 'ang'), split_axis=0, concat_axis=0, tiled=T...  10.8 us
    pallas_call x1, Pallas kernels, translate_first(): pl.pallas_call(first_targets_body, in_specs=[SMEM_SPEC] * 4 + [VMEM_SPEC,...  10.3 us
    all_to_all x1, waiting for transfers between devices, shards(): lax.all_to_all(send, ('clu', 'ang'), split_axis=0, concat_axis=0, tiled=T...  9.8 us
    pallas_call x1, Pallas kernels, translate_last(): pl.pallas_call(last_targets_body, in_specs=[SMEM_SPEC] * 4 + [VMEM_SPEC]...  8.79 us
    ppermute x1, starting transfers between devices, shards(): low = lax.ppermute(last, 'ang', across(1))  5.11 us
    unnamed x37, local copies, waits for them, and re-layouts  5.11 us
  transfers between devices with their start and end apart: 5, of which 2 were waited for; matrix products, arithmetic and copies ran while one was open for 11% of the time, Pallas kernels for 21%

profile of v4, /device:TPU:7, one launch (start us, length us, event | category | flops | bytes accessed | tf_op | source)
XLA Modules:
  0.0 105.1 jit_solution(9254736838638226646)
XLA Ops:
  0.6 16.5 %aggregate.1 = bf16[128,4,16,128]{3,2,1,0:T(8,128)(2,1)} custom-call(bf16[32768,128]{1,0:T(8,128)(2,1)} %bitcast.17, bf16[64,128]{1,0:T(8,128)(2,1)} %bitcast.19, bf16[128,256]{1,0:T(8,128)(2,1)} %b7.1, bf16[256,128]{1,0:T(8,128)(2,1)} %a6.1, bf16[256,512]{1,0:T(8,128)(2,1)} %b6.1, f32[128,256]{1,0:T(8,128)} %constant.27.clone.top7, ...), custom_call_target="tpu_custom_call" | custom-call | tf_op jit(solution)/shard_map/aggregate/pallas_call | solution.py:186
  17.1 10.8 %all-to-all-start = ((bf16[128,4,16,128]{3,2,1,0:T(8,128)(2,1)}), bf16[128,4,16,128]{3,2,1,0:T(8,128)(2,1)S(1)}, u32[]{:S(2)}, u32[]{:S(2)}) async-start(bf16[128,4,16,128]{3,2,1,0:T(8,128)(2,1)} %aggregate.1), calls=%async_computation | async-start | bytes 4194304 | tf_op jit(solution)/shard_map/all_to_all | solution.py:639
  28.0 0.8 subtract_add_fusion
  29.0 0.8 dynamic_slice.14
  29.7 0.7 convert_bitcast_fusion.weight_v
  33.5 1.4 %copy-done.2 = bf16[316,2,16,64]{0,3,2,1:T(8,128)(2,1)S(1)} copy-done((bf16[316,2,16,64]{0,3,2,1:T(8,128)(2,1)S(1)}, bf16[316,2,16,64]{0,3,2,1:T(8,128)(2,1)}, u32[]{:S(2)}) %copy-start.2) | copy-done | bytes 1294360
  34.9 2.8 %transfer_table.1.table_from = f32[5120,128]{1,0:T(8,128)S(1)} custom-call(bf16[2,2,8,64,316]{4,3,2,1,0:T(8,128)(2,1)S(1)} %bitcast.16), custom_call_target="tpu_custom_call" | custom-call | tf_op jit(solution)/shard_map/transfer_table/pallas_call | solution.py:223
  37.7 1.5 %copy-done.1 = f32[5120,128]{1,0:T(8,128)} copy-done((f32[5120,128]{1,0:T(8,128)}, f32[5120,128]{1,0:T(8,128)S(1)}, u32[]{:S(2)}) %copy-start.1) | copy-done | bytes 2621464
  41.3 0.7 iota_add_fusion.3
  42.0 0.7 convert_reduce_fusion.8.starts
  42.7 0.7 iota_add_fusion.1
  43.4 0.7 convert_reduce_fusion.6.starts
  44.1 0.7 convert_reduce_fusion.7.starts
  44.9 0.7 select_reduce_fusion.2.order
  46.2 0.7 select_reduce_fusion.order
  47.1 9.8 %all-to-all-done = bf16[128,4,16,128]{3,2,1,0:T(8,128)(2,1)S(1)} async-done(((bf16[128,4,16,128]{3,2,1,0:T(8,128)(2,1)}), bf16[128,4,16,128]{3,2,1,0:T(8,128)(2,1)S(1)}, u32[]{:S(2)}, u32[]{:S(2)}) %all-to-all-start) | async-done | bytes 2097184 | tf_op jit(solution)/shard_map/all_to_all | solution.py:639
  56.9 1.0 edge_columns.1
  58.3 3.2 %collective-permute-start.1 = (bf16[8,128,128]{2,1,0:T(8,128)(2,1)S(1)}, bf16[8,128,128]{2,1,0:T(8,128)(2,1)S(1)}, u32[]{:S(2)}, u32[]{:S(2)}) collective-permute-start(bf16[8,128,128]{2,1,0:T(8,128)(2,1)S(1)} %get-tuple-element.43), channel_id=1, source_target_pairs={{0,112},{16,0},{32,16},{48,32},{64,48},{80,64},{96,80},{112,96},{1... | collective-permute-start | bytes 786440 | tf_op jit(solution)/shard_map/ppermute | solution.py:684
  62.2 10.3 %translate_first.1 = (bf16[2,16,64,256]{3,2,1,0:T(8,128)(2,1)S(1)}, f32[8192,128]{1,0:T(8,128)S(1)}, f32[5120,128]{1,0:T(8,128)S(1)}) custom-call(s32[4096]{0:T(1024)S(1)} %reshape.547.src, s32[4096]{0:T(1024)S(1)} %reshape.548.off, s32[256]{0:T(256)S(1)} %select_reduce_fusion.1.order, s32[6]{0:T(128)S(1)} %copy-done.10, bf16[512,16,128]{2,1,0:T(8,128)(2,1)S(1)} %bitcast.11, ...), custom_call_target="tpu_custom_call" | custom-call | tf_op jit(solution)/shard_map/translate_first/pallas_call | solution.py:343
  73.2 5.1 %collective-permute-start.2 = (bf16[36,48,128]{2,1,0:T(8,128)(2,1)S(1)}, bf16[36,48,128]{2,1,0:T(8,128)(2,1)S(1)}, u32[]{:S(2)}, u32[]{:S(2)}) collective-permute-start(bf16[36,48,128]{2,1,0:T(8,128)(2,1)S(1)} %get-tuple-element.63), channel_id=1, source_target_pairs={{0,1},{1,2},{2,3},{3,4},{4,5},{5,6},{6,7},{7,8},{8,9},{9,10},{10,1... | collective-permute-start | bytes 1327112 | tf_op jit(solution)/shard_map/ppermute | solution.py:689
  78.3 1.9 %collective-permute-start.3 = (bf16[36,48,128]{2,1,0:T(8,128)(2,1)S(1)}, bf16[36,48,128]{2,1,0:T(8,128)(2,1)S(1)}, u32[]{:S(2)}, u32[]{:S(2)}) collective-permute-start(bf16[36,48,128]{2,1,0:T(8,128)(2,1)S(1)} %get-tuple-element.64), channel_id=1, source_target_pairs={{1,0},{2,1},{3,2},{4,3},{5,4},{6,5},{7,6},{8,7},{9,8},{10,9},{11,1... | collective-permute-start | bytes 1327112 | tf_op jit(solution)/shard_map/ppermute | solution.py:690
  80.3 8.8 %translate_last.1 = bf16[2,16,64,512]{3,2,1,0:T(8,128)(2,1)} custom-call(s32[4096]{0:T(1024)S(1)} %reshape.549.src, s32[4096]{0:T(1024)S(1)} %reshape.550.off, s32[256]{0:T(256)S(1)} %copy-done.6, s32[6]{0:T(128)S(1)} %copy-done.11, f32[8192,128]{1,0:T(8,128)S(1)} %get-tuple-element.55.tiles, f32[5120,128]{1,0:T(8,128)S(1)} %get-tuple-element.56.table, ...), custom_call_target="tpu_custom_call" | custom-call | tf_op jit(solution)/shard_map/translate_last/pallas_call | solution.py:360
  89.1 2.4 %collective-permute-done.3.high = bf16[36,48,128]{2,1,0:T(8,128)(2,1)S(1)} collective-permute-done((bf16[36,48,128]{2,1,0:T(8,128)(2,1)S(1)}, bf16[36,48,128]{2,1,0:T(8,128)(2,1)S(1)}, u32[]{:S(2)}, u32[]{:S(2)}) %collective-permute-start.3) | collective-permute-done | bytes 442400 | tf_op jit(solution)/shard_map/ppermute | solution.py:690
  91.6 13.3 %top_level.1 = bf16[64,2,32,128]{3,2,1,0:T(8,128)(2,1)} custom-call(s32[1024]{0:T(1024)S(1)} %reshape.551.src, s32[1024]{0:T(1024)S(1)} %reshape.552.off, s32[64]{0:T(128)S(1)} %copy-done.9, s32[6]{0:T(128)S(1)} %copy-done.8, bf16[64,128,128]{2,1,0:T(8,128)(2,1)S(1)} %bitcast.13, bf16[8,128,128]{2,1,0:T(8,128)(2,1)S(1)} %get-tuple-element.62.sides, ...), custom_call_target="tpu_custom_call" | custom-call | tf_op jit(solution)/shard_map/top_level/pallas_call | solution.py:593
  (73 shorter events, 8.0 us)
Async XLA Ops:
  0.6 28.2 %copy-start = (bf16[512,4]{0,1:T(4,128)(2,1)S(1)}, bf16[512,4]{0,1:T(4,128)(2,1)}, u32[]{:S(2)}) copy-start(bf16[512,4]{0,1:T(4,128)(2,1)} %param.30) | copy-start | bytes 12292
  17.1 13.3 %copy-start.12 = (s32[512,16]{0,1:T(8,128)S(1)}, s32[512,16]{0,1:T(8,128)}, u32[]{:S(2)}) copy-start(s32[512,16]{0,1:T(8,128)} %param.34) | copy-start | bytes 98308
  17.1 13.9 %copy-start.14 = (s32[64,16]{0,1:T(8,128)S(1)}, s32[64,16]{0,1:T(8,128)}, u32[]{:S(2)}) copy-start(s32[64,16]{0,1:T(8,128)} %param.37) | copy-start | bytes 12292
  17.1 14.5 %copy-start.13 = (s32[512,16]{0,1:T(8,128)S(1)}, s32[512,16]{0,1:T(8,128)}, u32[]{:S(2)}) copy-start(s32[512,16]{0,1:T(8,128)} %param.35) | copy-start | bytes 98308
  17.1 14.5 %copy-start.15 = (s32[64,16]{0,1:T(8,128)S(1)}, s32[64,16]{0,1:T(8,128)}, u32[]{:S(2)}) copy-start(s32[64,16]{0,1:T(8,128)} %param.38) | copy-start | bytes 12292
  17.1 39.7 %all-to-all-start = ((bf16[128,4,16,128]{3,2,1,0:T(8,128)(2,1)}), bf16[128,4,16,128]{3,2,1,0:T(8,128)(2,1)S(1)}, u32[]{:S(2)}, u32[]{:S(2)}) async-start(bf16[128,4,16,128]{3,2,1,0:T(8,128)(2,1)} %aggregate.1), calls=%async_computation | async-start | bytes 4194304 | tf_op jit(solution)/shard_map/all_to_all | solution.py:639
  32.7 6.7 %copy-start.4 = (f32[2,8,224]{2,1,0:T(8,128)S(1)}, f32[2,8,224]{2,1,0:T(8,128)}, u32[]{:S(2)}) copy-start(f32[2,8,224]{2,1,0:T(8,128)} %constant.92.clone.factor) | copy-start | bytes 43012
  33.5 1.4 %copy-start.2 = (bf16[316,2,16,64]{0,3,2,1:T(8,128)(2,1)S(1)}, bf16[316,2,16,64]{0,3,2,1:T(8,128)(2,1)}, u32[]{:S(2)}) copy-start(bf16[316,2,16,64]{0,3,2,1:T(8,128)(2,1)} %param.33) | copy-start | bytes 3883012
  37.7 1.5 %copy-start.1 = (f32[5120,128]{1,0:T(8,128)}, f32[5120,128]{1,0:T(8,128)S(1)}, u32[]{:S(2)}) copy-start(f32[5120,128]{1,0:T(8,128)S(1)} %transfer_table.1.table_from) | copy-start | bytes 7864324
  39.4 0.7 copy-start.5
  40.1 0.7 copy-start.7
  57.9 14.6 %copy-start.3 = (bf16[96,256]{1,0:T(8,128)(2,1)S(1)}, bf16[96,256]{1,0:T(8,128)(2,1)}, u32[]{:S(2)}) copy-start(bf16[96,256]{1,0:T(8,128)(2,1)} %constant.93.clone.pick) | copy-start | bytes 147460
  57.9 14.6 %collective-permute-start = (bf16[8,128,128]{2,1,0:T(8,128)(2,1)S(1)}, bf16[8,128,128]{2,1,0:T(8,128)(2,1)S(1)}, u32[]{:S(2)}, u32[]{:S(2)}) collective-permute-start(bf16[8,128,128]{2,1,0:T(8,128)(2,1)S(1)} %get-tuple-element.42), channel_id=1, source_target_pairs={{0,16},{16,32},{32,48},{48,64},{64,80},{80,96},{96,112},{112,0},{1... | collective-permute-start | bytes 786440 | tf_op jit(solution)/shard_map/ppermute | solution.py:683
  58.3 14.2 %collective-permute-start.1 = (bf16[8,128,128]{2,1,0:T(8,128)(2,1)S(1)}, bf16[8,128,128]{2,1,0:T(8,128)(2,1)S(1)}, u32[]{:S(2)}, u32[]{:S(2)}) collective-permute-start(bf16[8,128,128]{2,1,0:T(8,128)(2,1)S(1)} %get-tuple-element.43), channel_id=1, source_target_pairs={{0,112},{16,0},{32,16},{48,32},{64,48},{80,64},{96,80},{112,96},{1... | collective-permute-start | bytes 786440 | tf_op jit(solution)/shard_map/ppermute | solution.py:684
  61.5 0.7 copy-start.10
  62.2 18.0 %copy-start.6 = (s32[256]{0:T(256)S(1)}, s32[256]{0:T(256)}, u32[]{:S(2)}) copy-start(s32[256]{0:T(256)} %select_reduce_fusion.order) | copy-start | bytes 3076
  62.2 18.1 %copy-start.11 = (s32[6]{0:T(128)S(1)}, s32[6]{0:T(128)}, u32[]{:S(2)}) copy-start(s32[6]{0:T(128)} %convert_reduce_fusion.6.starts) | copy-start | bytes 76
  73.2 15.9 %collective-permute-start.2 = (bf16[36,48,128]{2,1,0:T(8,128)(2,1)S(1)}, bf16[36,48,128]{2,1,0:T(8,128)(2,1)S(1)}, u32[]{:S(2)}, u32[]{:S(2)}) collective-permute-start(bf16[36,48,128]{2,1,0:T(8,128)(2,1)S(1)} %get-tuple-element.63), channel_id=1, source_target_pairs={{0,1},{1,2},{2,3},{3,4},{4,5},{5,6},{6,7},{7,8},{8,9},{9,10},{10,1... | collective-permute-start | bytes 1327112 | tf_op jit(solution)/shard_map/ppermute | solution.py:689
  78.3 13.2 %collective-permute-start.3 = (bf16[36,48,128]{2,1,0:T(8,128)(2,1)S(1)}, bf16[36,48,128]{2,1,0:T(8,128)(2,1)S(1)}, u32[]{:S(2)}, u32[]{:S(2)}) collective-permute-start(bf16[36,48,128]{2,1,0:T(8,128)(2,1)S(1)} %get-tuple-element.64), channel_id=1, source_target_pairs={{1,0},{2,1},{3,2},{4,3},{5,4},{6,5},{7,6},{8,7},{9,8},{10,9},{11,1... | collective-permute-start | bytes 1327112 | tf_op jit(solution)/shard_map/ppermute | solution.py:690
  80.2 11.3 %slice-start = ((s8[5177344]{0:T(1024)(128)(4,1)}), s8[4194304]{0:T(1024)(128)(4,1)S(1)}, s32[]{:S(2)}) async-start(s8[5177344]{0:T(1024)(128)(4,1)} %bitcast.14), calls=%async_computation.1 | async-start | bytes 8388608
  80.3 11.3 %slice-start.1 = ((s8[5177344]{0:T(1024)(128)(4,1)}), s8[983040]{0:T(1024)(128)(4,1)S(1)}, s32[]{:S(2)}) async-start(s8[5177344]{0:T(1024)(128)(4,1)} %bitcast.14), calls=%async_computation.2 | async-start | bytes 1966080
  80.3 11.3 %copy-start.8 = (s32[6]{0:T(128)S(1)}, s32[6]{0:T(128)}, u32[]{:S(2)}) copy-start(s32[6]{0:T(128)} %convert_reduce_fusion.8.starts) | copy-start | bytes 76
  80.3 11.3 %copy-start.9 = (s32[64]{0:T(128)S(1)}, s32[64]{0:T(128)}, u32[]{:S(2)}) copy-start(s32[64]{0:T(128)} %select_reduce_fusion.2.order) | copy-start | bytes 772

commit v5 on v4

--- a/solution.py
+++ b/solution.py
@@ -340,6 +340,7 @@
     clusters, rows, lanes = level.shape
     targets = lists[2].shape[0]
     table = pltpu.with_memory_space_constraint(table, pltpu.HBM)
+    lists = tuple(pltpu.with_memory_space_constraint(a, pltpu.HBM) for a in lists)
     return pl.pallas_call(
         first_targets_body,
         in_specs=[SMEM_SPEC] * 4 + [VMEM_SPEC, pl.BlockSpec(memory_space=pltpu.HBM)],
@@ -583,7 +584,7 @@
             out[t, 0, 8 * r : 8 * r + 8] = re[r].astype(BF16)
             out[t, 1, 8 * r : 8 * r + 8] = im[r].astype(BF16)
 
-    by_class(order, starts, slots, 1, one)
+    by_class(order, starts, slots, 2, one)
 
 
 def top_level(level, sides, low, high, polar, azimuth, tab, transfer, lists):

time: 106 us -> 105 us (level)
  waiting for transfers between devices: 12.2 us -> 17.4 us
  other arithmetic: 9.27 us -> 4.33 us
    all_to_all x1, waiting for transfers between devices: 9.8 us -> 14.9 us  [shards(): lax.all_to_all(send, ('clu', 'ang'), split_axis=0, concat_axis=0, tiled=T...]
    unnamed x37 -> x25, local copies, waits for them, and re-layouts: 5.11 us -> 3.06 us
    add x2, other arithmetic: 1.4 us -> 0.02 us  [target_classes(): key = kind * targets + index]
    reduce_sum x3, other arithmetic: 2.08 us -> 0.86 us  [target_classes(): starts = jnp.sum((kind[None, :] < kinds[:, None]).astype(jnp.int32), axis=1)]
    reshape x6, local copies, waits for them, and re-layouts: 0.56 us -> 1.77 us  [flat_lists(): return (src.reshape(-1), off.reshape(-1)) + target_classes(sources)]
    reduce_sum x2, other arithmetic: 1.22 us -> 0.04 us  [target_classes(): live = jnp.sum((sources >= 0).astype(jnp.int32), axis=1)]
  transfers between devices with their start and end apart: 5 -> 5, of which waited for: 2 -> 2; matrix products, arithmetic and copies ran while one was open for 11% -> 7% of each run, Pallas kernels for 21% -> 22%
where the time goes in v5:
time: 105 us; the launch traced here: 104 us
  Pallas kernels  53.9 us (51%)
  starting transfers between devices  21.5 us (20%)
  waiting for transfers between devices  17.4 us (17%)
  local copies, waits for them, and re-layouts  6.32 us (6%)
  other arithmetic  4.33 us (4%)
  between operations  1.09 us (1%)
    pallas_call x1, Pallas kernels, aggregate(): pl.pallas_call(aggregate_body, grid=(clusters,), in_specs=[pl.BlockSpec((...  16.5 us
    all_to_all x1, waiting for transfers between devices, shards(): lax.all_to_all(send, ('clu', 'ang'), split_axis=0, concat_axis=0, tiled=T...  14.9 us
    pallas_call x1, Pallas kernels, top_level(): pl.pallas_call(top_body, in_specs=[SMEM_SPEC] * 4 + [VMEM_SPEC] * 7 + [AN...  13.1 us
    all_to_all x1, starting transfers between devices, shards(): lax.all_to_all(send, ('clu', 'ang'), split_axis=0, concat_axis=0, tiled=T...  10.8 us
    pallas_call x1, Pallas kernels, translate_first(): pl.pallas_call(first_targets_body, in_specs=[SMEM_SPEC] * 4 + [VMEM_SPEC,...  10.7 us
    pallas_call x1, Pallas kernels, translate_last(): pl.pallas_call(last_targets_body, in_specs=[SMEM_SPEC] * 4 + [VMEM_SPEC]...  8.8 us
    ppermute x1, starting transfers between devices, shards(): low = lax.ppermute(last, 'ang', across(1))  5.11 us
    ppermute x1, starting transfers between devices, shards(): from_right = lax.ppermute(left, 'clu', around(-1))  3.22 us
  transfers between devices with their start and end apart: 5, of which 2 were waited for; matrix products, arithmetic and copies ran while one was open for 7% of the time, Pallas kernels for 22%

profile of v5, /device:TPU:7, one launch (start us, length us, event | category | flops | bytes accessed | tf_op | source)
XLA Modules:
  0.0 104.5 jit_solution(18090326270099892472)
XLA Ops:
  0.6 16.5 %aggregate.1 = bf16[128,4,16,128]{3,2,1,0:T(8,128)(2,1)} custom-call(bf16[32768,128]{1,0:T(8,128)(2,1)} %bitcast.17, bf16[64,128]{1,0:T(8,128)(2,1)} %bitcast.19, bf16[128,256]{1,0:T(8,128)(2,1)} %b7.1, bf16[256,128]{1,0:T(8,128)(2,1)} %a6.1, bf16[256,512]{1,0:T(8,128)(2,1)} %b6.1, f32[128,256]{1,0:T(8,128)} %constant.27.clone.top7, ...), custom_call_target="tpu_custom_call" | custom-call | tf_op jit(solution)/shard_map/aggregate/pallas_call | solution.py:186
  17.1 10.8 %all-to-all-start = ((bf16[128,4,16,128]{3,2,1,0:T(8,128)(2,1)}), bf16[128,4,16,128]{3,2,1,0:T(8,128)(2,1)S(1)}, u32[]{:S(2)}, u32[]{:S(2)}) async-start(bf16[128,4,16,128]{3,2,1,0:T(8,128)(2,1)} %aggregate.1), calls=%async_computation | async-start | bytes 4194304 | tf_op jit(solution)/shard_map/all_to_all | solution.py:640
  28.0 0.8 subtract_add_fusion
  29.0 0.8 dynamic_slice.14
  29.7 0.7 convert_bitcast_fusion.weight_v
  30.8 0.7 reshape.547.src
  31.9 0.7 reshape.548.off
  32.9 1.4 %copy-done.2 = bf16[316,2,16,64]{0,3,2,1:T(8,128)(2,1)S(1)} copy-done((bf16[316,2,16,64]{0,3,2,1:T(8,128)(2,1)S(1)}, bf16[316,2,16,64]{0,3,2,1:T(8,128)(2,1)}, u32[]{:S(2)}) %copy-start.2) | copy-done | bytes 1294360
  34.3 2.8 %transfer_table.1.table_from = f32[5120,128]{1,0:T(8,128)S(1)} custom-call(bf16[2,2,8,64,316]{4,3,2,1,0:T(8,128)(2,1)S(1)} %bitcast.16), custom_call_target="tpu_custom_call" | custom-call | tf_op jit(solution)/shard_map/transfer_table/pallas_call | solution.py:223
  37.2 1.5 %copy-done.1 = f32[5120,128]{1,0:T(8,128)} copy-done((f32[5120,128]{1,0:T(8,128)}, f32[5120,128]{1,0:T(8,128)S(1)}, u32[]{:S(2)}) %copy-start.1) | copy-done | bytes 2621464
  38.8 0.5 stencils.1
  39.6 0.6 convert_reduce_fusion.7.starts
  41.3 0.7 select_reduce_fusion.1.order
  42.0 14.9 %all-to-all-done = bf16[128,4,16,128]{3,2,1,0:T(8,128)(2,1)S(1)} async-done(((bf16[128,4,16,128]{3,2,1,0:T(8,128)(2,1)}), bf16[128,4,16,128]{3,2,1,0:T(8,128)(2,1)S(1)}, u32[]{:S(2)}, u32[]{:S(2)}) %all-to-all-start) | async-done | bytes 2097184 | tf_op jit(solution)/shard_map/all_to_all | solution.py:640
  56.9 1.0 edge_columns.1
  57.9 0.4 collective-permute-start
  58.3 3.2 %collective-permute-start.1 = (bf16[8,128,128]{2,1,0:T(8,128)(2,1)S(1)}, bf16[8,128,128]{2,1,0:T(8,128)(2,1)S(1)}, u32[]{:S(2)}, u32[]{:S(2)}) collective-permute-start(bf16[8,128,128]{2,1,0:T(8,128)(2,1)S(1)} %get-tuple-element.43), channel_id=1, source_target_pairs={{0,112},{16,0},{32,16},{48,32},{64,48},{80,64},{96,80},{112,96},{1... | collective-permute-start | bytes 786440 | tf_op jit(solution)/shard_map/ppermute | solution.py:685
  61.5 10.7 %translate_first.1 = (bf16[2,16,64,256]{3,2,1,0:T(8,128)(2,1)S(1)}, f32[8192,128]{1,0:T(8,128)S(1)}, f32[5120,128]{1,0:T(8,128)S(1)}) custom-call(s32[4096]{0:T(1024)} %reshape.547.src, s32[4096]{0:T(1024)} %reshape.548.off, s32[256]{0:T(256)} %select_reduce_fusion.1.order, s32[6]{0:T(128)} %convert_reduce_fusion.7.starts, ...), custom_call_target="tpu_custom_call" | custom-call | tf_op jit(solution)/shard_map/translate_first/pallas_call | solution.py:344
  72.3 0.6 edge_rows.1
  72.9 5.1 %collective-permute-start.2 = (bf16[36,48,128]{2,1,0:T(8,128)(2,1)S(1)}, bf16[36,48,128]{2,1,0:T(8,128)(2,1)S(1)}, u32[]{:S(2)}, u32[]{:S(2)}) collective-permute-start(bf16[36,48,128]{2,1,0:T(8,128)(2,1)S(1)} %get-tuple-element.63), channel_id=1, source_target_pairs={{0,1},{1,2},{2,3},{3,4},{4,5},{5,6},{6,7},{7,8},{8,9},{9,10},{10,1... | collective-permute-start | bytes 1327112 | tf_op jit(solution)/shard_map/ppermute | solution.py:690
  78.0 1.9 %collective-permute-start.3 = (bf16[36,48,128]{2,1,0:T(8,128)(2,1)S(1)}, bf16[36,48,128]{2,1,0:T(8,128)(2,1)S(1)}, u32[]{:S(2)}, u32[]{:S(2)}) collective-permute-start(bf16[36,48,128]{2,1,0:T(8,128)(2,1)S(1)} %get-tuple-element.64), channel_id=1, source_target_pairs={{1,0},{2,1},{3,2},{4,3},{5,4},{6,5},{7,6},{8,7},{9,8},{10,9},{11,1... | collective-permute-start | bytes 1327112 | tf_op jit(solution)/shard_map/ppermute | solution.py:691
  80.0 8.8 %translate_last.1 = bf16[2,16,64,512]{3,2,1,0:T(8,128)(2,1)} custom-call(s32[4096]{0:T(1024)S(1)} %reshape.549.src, s32[4096]{0:T(1024)S(1)} %reshape.550.off, s32[256]{0:T(256)S(1)} %select_reduce_fusion.order, s32[6]{0:T(128)S(1)} %convert_reduce_fusion.6.starts, f32[8192,128]{1,0:T(8,128)S(1)} %get-tuple-element.55.tiles, ...), custom_call_target="tpu_custom_call" | custom-call | tf_op jit(solution)/shard_map/translate_last/pallas_call | solution.py:361
  88.8 2.5 %collective-permute-done.3.high = bf16[36,48,128]{2,1,0:T(8,128)(2,1)S(1)} collective-permute-done((bf16[36,48,128]{2,1,0:T(8,128)(2,1)S(1)}, bf16[36,48,128]{2,1,0:T(8,128)(2,1)S(1)}, u32[]{:S(2)}, u32[]{:S(2)}) %collective-permute-start.3) | collective-permute-done | bytes 442400 | tf_op jit(solution)/shard_map/ppermute | solution.py:691
  91.3 13.1 %top_level.1 = bf16[64,2,32,128]{3,2,1,0:T(8,128)(2,1)} custom-call(s32[1024]{0:T(1024)S(1)} %reshape.551.src, s32[1024]{0:T(1024)S(1)} %reshape.552.off, s32[64]{0:T(128)S(1)} %select_reduce_fusion.2.order, s32[6]{0:T(128)S(1)} %convert_reduce_fusion.8.starts, bf16[64,128,128]{2,1,0:T(8,128)(2,1)S(1)} %bitcast.13, ...), custom_call_target="tpu_custom_call" | custom-call | tf_op jit(solution)/shard_map/top_level/pallas_call | solution.py:594
  (61 shorter events, 2.8 us)
Async XLA Ops:
  0.6 28.2 %copy-start = (bf16[512,4]{0,1:T(4,128)(2,1)S(1)}, bf16[512,4]{0,1:T(4,128)(2,1)}, u32[]{:S(2)}) copy-start(bf16[512,4]{0,1:T(4,128)(2,1)} %param.30) | copy-start | bytes 12292
  17.1 13.3 %copy-start.6 = (s32[512,16]{0,1:T(8,128)S(1)}, s32[512,16]{0,1:T(8,128)}, u32[]{:S(2)}) copy-start(s32[512,16]{0,1:T(8,128)} %param.34) | copy-start | bytes 98308
  17.1 13.3 %copy-start.8 = (s32[64,16]{0,1:T(8,128)S(1)}, s32[64,16]{0,1:T(8,128)}, u32[]{:S(2)}) copy-start(s32[64,16]{0,1:T(8,128)} %param.37) | copy-start | bytes 12292
  17.1 13.3 %copy-start.7 = (s32[512,16]{0,1:T(8,128)S(1)}, s32[512,16]{0,1:T(8,128)}, u32[]{:S(2)}) copy-start(s32[512,16]{0,1:T(8,128)} %param.35) | copy-start | bytes 98308
  17.1 13.3 %copy-start.9 = (s32[64,16]{0,1:T(8,128)S(1)}, s32[64,16]{0,1:T(8,128)}, u32[]{:S(2)}) copy-start(s32[64,16]{0,1:T(8,128)} %param.38) | copy-start | bytes 12292
  17.1 39.7 %all-to-all-start = ((bf16[128,4,16,128]{3,2,1,0:T(8,128)(2,1)}), bf16[128,4,16,128]{3,2,1,0:T(8,128)(2,1)S(1)}, u32[]{:S(2)}, u32[]{:S(2)}) async-start(bf16[128,4,16,128]{3,2,1,0:T(8,128)(2,1)} %aggregate.1), calls=%async_computation | async-start | bytes 4194304 | tf_op jit(solution)/shard_map/all_to_all | solution.py:640
  31.5 7.3 %copy-start.4 = (f32[2,8,224]{2,1,0:T(8,128)S(1)}, f32[2,8,224]{2,1,0:T(8,128)}, u32[]{:S(2)}) copy-start(f32[2,8,224]{2,1,0:T(8,128)} %constant.92.clone.factor) | copy-start | bytes 43012
  31.5 7.3 %copy-start.5 = (s32[1,224]{1,0:T(1,128)S(1)}, s32[1,224]{1,0:T(1,128)}, u32[]{:S(2)}) copy-start(s32[1,224]{1,0:T(1,128)} %constant.91.clone.ext) | copy-start | bytes 2692
  32.9 1.4 %copy-start.2 = (bf16[316,2,16,64]{0,3,2,1:T(8,128)(2,1)S(1)}, bf16[316,2,16,64]{0,3,2,1:T(8,128)(2,1)}, u32[]{:S(2)}) copy-start(bf16[316,2,16,64]{0,3,2,1:T(8,128)(2,1)} %param.33) | copy-start | bytes 3883012
  37.2 1.5 %copy-start.1 = (f32[5120,128]{1,0:T(8,128)}, f32[5120,128]{1,0:T(8,128)S(1)}, u32[]{:S(2)}) copy-start(f32[5120,128]{1,0:T(8,128)S(1)} %transfer_table.1.table_from) | copy-start | bytes 7864324
  57.9 14.4 %copy-start.3 = (bf16[96,256]{1,0:T(8,128)(2,1)S(1)}, bf16[96,256]{1,0:T(8,128)(2,1)}, u32[]{:S(2)}) copy-start(bf16[96,256]{1,0:T(8,128)(2,1)} %constant.93.clone.pick) | copy-start | bytes 147460
  57.9 14.3 %collective-permute-start = (bf16[8,128,128]{2,1,0:T(8,128)(2,1)S(1)}, bf16[8,128,128]{2,1,0:T(8,128)(2,1)S(1)}, u32[]{:S(2)}, u32[]{:S(2)}) collective-permute-start(bf16[8,128,128]{2,1,0:T(8,128)(2,1)S(1)} %get-tuple-element.42), channel_id=1, source_target_pairs={{0,16},{16,32},{32,48},{48,64},{64,80},{80,96},{96,112},{112,0},{1... | collective-permute-start | bytes 786440 | tf_op jit(solution)/shard_map/ppermute | solution.py:684
  58.3 13.9 %collective-permute-start.1 = (bf16[8,128,128]{2,1,0:T(8,128)(2,1)S(1)}, bf16[8,128,128]{2,1,0:T(8,128)(2,1)S(1)}, u32[]{:S(2)}, u32[]{:S(2)}) collective-permute-start(bf16[8,128,128]{2,1,0:T(8,128)(2,1)S(1)} %get-tuple-element.43), channel_id=1, source_target_pairs={{0,112},{16,0},{32,16},{48,32},{64,48},{80,64},{96,80},{112,96},{1... | collective-permute-start | bytes 786440 | tf_op jit(solution)/shard_map/ppermute | solution.py:685
  72.9 15.9 %collective-permute-start.2 = (bf16[36,48,128]{2,1,0:T(8,128)(2,1)S(1)}, bf16[36,48,128]{2,1,0:T(8,128)(2,1)S(1)}, u32[]{:S(2)}, u32[]{:S(2)}) collective-permute-start(bf16[36,48,128]{2,1,0:T(8,128)(2,1)S(1)} %get-tuple-element.63), channel_id=1, source_target_pairs={{0,1},{1,2},{2,3},{3,4},{4,5},{5,6},{6,7},{7,8},{8,9},{9,10},{10,1... | collective-permute-start | bytes 1327112 | tf_op jit(solution)/shard_map/ppermute | solution.py:690
  78.0 13.2 %collective-permute-start.3 = (bf16[36,48,128]{2,1,0:T(8,128)(2,1)S(1)}, bf16[36,48,128]{2,1,0:T(8,128)(2,1)S(1)}, u32[]{:S(2)}, u32[]{:S(2)}) collective-permute-start(bf16[36,48,128]{2,1,0:T(8,128)(2,1)S(1)} %get-tuple-element.64), channel_id=1, source_target_pairs={{1,0},{2,1},{3,2},{4,3},{5,4},{6,5},{7,6},{8,7},{9,8},{10,9},{11,1... | collective-permute-start | bytes 1327112 | tf_op jit(solution)/shard_map/ppermute | solution.py:691
  79.9 11.3 %slice-start = ((s8[5177344]{0:T(1024)(128)(4,1)}), s8[4194304]{0:T(1024)(128)(4,1)S(1)}, s32[]{:S(2)}) async-start(s8[5177344]{0:T(1024)(128)(4,1)} %bitcast.14), calls=%async_computation.1 | async-start | bytes 8388608
  80.0 11.3 %slice-start.1 = ((s8[5177344]{0:T(1024)(128)(4,1)}), s8[983040]{0:T(1024)(128)(4,1)S(1)}, s32[]{:S(2)}) async-start(s8[5177344]{0:T(1024)(128)(4,1)} %bitcast.14), calls=%async_computation.2 | async-start | bytes 1966080
